TPU v7x, 256 devices: a whole 4x4x8 slice. The times are simulated.
256 devices in a mesh: win: 32 (over y, x, core), grp: 8 (over z).
Axes of the slice: x: 4, y: 4, z: 8, core: 2. Of those that a mesh axis runs over, the one named last changes fastest.
Arguments:
- traces: bfloat16 [256, 512, 2048], P(('win', 'grp'))
- pair_lists: int32 [32, 3], P('win'), may hold values from -1 to 3, as said below
- observed: float32 [32, 3, 16, 16, 2048], P('win'), may hold values from -4 to 4
Outputs:
- correl: float32 [32, 3, 16, 16, 2048], P('win', None, None, None, 'grp')
- trace_gradient: bfloat16 [256, 512, 2048], P(('win', 'grp'))
Inputs may be any that keep to these rules, and one draw needn't show every extreme that they name: `pair_lists`: each row lists distinct offsets in increasing order, followed by -1 in its empty slots; block a lists only offsets o with a + o < 32; every block lists at least one offset, and block 0 fills all 3 slots and lists offset 4 - 1.
All inputs are finite; a program needn't handle non-finite values.
Results may differ from a plain program's by a relative error of at most 0.014.
Values may be sent and summed in bfloat16 or wider, within the bound.
No kernel may reach another device: no remote copies, remote signals or barrier semaphores. Data moves between devices by JAX's collectives and lax.ppermute only.
A program may use at most 192 MiB of HBM per device.

v0:
```python
import math

import jax
import jax.numpy as jnp
from jax import lax
from jax.sharding import PartitionSpec as P

SEG = 2048
FREQ = 1024
BAND = 64
OFFSETS = 4


def passed_along(array, axis, by):
    peers = lax.axis_size(axis)
    pairs = [(i, i + by) for i in range(peers) if 0 <= i + by < peers]
    return lax.ppermute(array, axis, pairs)


def dft_table(first_column, column_count):
    samples = jnp.arange(SEG, dtype=jnp.int32)
    columns = first_column + jnp.arange(column_count, dtype=jnp.int32)
    harmonic = columns % FREQ
    phases = samples[:, None] * harmonic[None, :] % SEG
    angles = phases.astype(jnp.float32) * (2.0 * math.pi / SEG)
    values = jnp.where(columns[None, :] < FREQ, jnp.cos(angles), -jnp.sin(angles))
    return values.astype(jnp.bfloat16)


def whiten(spectrum):
    halfway = spectrum.shape[-1] // 2
    real_part = spectrum[..., :halfway]
    imag_part = spectrum[..., halfway:]
    power_bins = real_part * real_part + imag_part * imag_part
    banded = power_bins.reshape(power_bins.shape[:-1] + (halfway // BAND, BAND))
    inverse = lax.rsqrt(jnp.mean(banded, axis=-1) + 1e-05)
    spread = jnp.broadcast_to(inverse[..., None], banded.shape).reshape(power_bins.shape)
    return spectrum * jnp.concatenate([spread, spread], axis=-1)


def split_halves(operand):
    halfway = operand.shape[-1] // 2
    return (operand[..., :halfway], operand[..., halfway:])


def widen(operand):
    return operand.astype(jnp.float32)


def correlate(leading, trailing, windows_total):
    lead_real, lead_imag = split_halves(leading)
    trail_real, trail_imag = split_halves(trailing)
    left_real = widen(lead_real)[:, :, None, :]
    left_imag = widen(lead_imag)[:, :, None, :]
    right_real = widen(trail_real)[:, None, :, :]
    right_imag = widen(trail_imag)[:, None, :, :]
    real_sum = jnp.sum(left_real * right_real + left_imag * right_imag, axis=0)
    imag_sum = jnp.sum(left_real * right_imag - left_imag * right_real, axis=0)
    return jnp.concatenate([real_sum, imag_sum], axis=-1) / windows_total


def pull_first(residual, trailing):
    resid_real, resid_imag = split_halves(residual)
    trail_real, trail_imag = split_halves(trailing)
    left_real = widen(resid_real)[None]
    left_imag = widen(resid_imag)[None]
    right_real = widen(trail_real)[:, None, :, :]
    right_imag = widen(trail_imag)[:, None, :, :]
    real_part = jnp.sum(left_real * right_real + left_imag * right_imag, axis=2)
    imag_part = jnp.sum(left_real * right_imag - left_imag * right_real, axis=2)
    return jnp.concatenate([real_part, imag_part], axis=-1)


def pull_second(residual, leading):
    resid_real, resid_imag = split_halves(residual)
    lead_real, lead_imag = split_halves(leading)
    left_real = widen(resid_real)[None]
    left_imag = widen(resid_imag)[None]
    right_real = widen(lead_real)[:, :, None, :]
    right_imag = widen(lead_imag)[:, :, None, :]
    real_part = jnp.sum(left_real * right_real - left_imag * right_imag, axis=1)
    imag_part = jnp.sum(left_real * right_imag + left_imag * right_real, axis=1)
    return jnp.concatenate([real_part, imag_part], axis=-1)


def on_device(traces, pair_lists, observed):
    win_dev, channels, samples = traces.shape
    column_total = 2 * FREQ
    column_step = min(512, column_total)
    tables = [
        dft_table(start_col, column_step) for start_col in range(0, column_total, column_step)
    ]
    flat_traces = traces.reshape(win_dev * channels, samples)
    spectra = jnp.concatenate(
        [
            jnp.dot(flat_traces, table_part, preferred_element_type=jnp.float32)
            for table_part in tables
        ],
        axis=1,
    )
    spectra = spectra.reshape(win_dev, channels, column_total)
    whitened = whiten(spectra).astype(jnp.bfloat16)
    grp_count = lax.axis_size("grp")
    share_width = column_total // grp_count
    moved_blocks = lax.all_to_all(whitened, "win", split_axis=1, concat_axis=0, tiled=True)
    windows_total = moved_blocks.shape[0] * grp_count
    partner_list = [moved_blocks] + [
        passed_along(moved_blocks, "win", -offset) for offset in range(1, OFFSETS)
    ]
    stacked = jnp.stack(partner_list)
    offsets = pair_lists[0]
    slot_total = offsets.shape[0]
    live_slots = (offsets >= 0).astype(jnp.float32)[:, None, None, None]
    partners = [
        lax.dynamic_index_in_dim(stacked, jnp.maximum(offsets[slot_index], 0), 0, keepdims=False)
        for slot_index in range(slot_total)
    ]
    correl = (
        jnp.stack(
            [correlate(moved_blocks, partner_block, windows_total) for partner_block in partners]
        )
        * live_slots
    )
    share_start = lax.axis_index("grp") * share_width
    totals = lax.psum(correl, "grp")
    correl_share = lax.dynamic_slice_in_dim(totals, share_start, share_width, 3)
    residual = ((totals - observed[0]) * live_slots).astype(jnp.bfloat16)
    own_grad = pull_first(residual[0], partners[0])
    for slot_index in range(1, slot_total):
        own_grad = own_grad + pull_first(residual[slot_index], partners[slot_index])
    contrib = []
    for offset in range(OFFSETS):
        chosen = jnp.zeros_like(residual[0])
        for slot_index in range(slot_total):
            chosen = jnp.where(offsets[slot_index] == offset, residual[slot_index], chosen)
        contrib.append(pull_second(chosen, moved_blocks))
    white_grad = own_grad + contrib[0]
    for offset in range(1, OFFSETS):
        white_grad = white_grad + passed_along(
            contrib[offset].astype(jnp.bfloat16), "win", offset
        ).astype(jnp.float32)
    returned = lax.all_to_all(
        white_grad.astype(jnp.bfloat16), "win", split_axis=0, concat_axis=1, tiled=True
    )
    unused, pullback = jax.vjp(whiten, spectra)
    spectra_grad = pullback(returned.astype(jnp.float32))[0].astype(jnp.bfloat16)
    flat_grad = spectra_grad.reshape(win_dev * channels, column_total)
    trace_grad = jnp.zeros((win_dev * channels, samples), jnp.float32)
    for table_index in range(len(tables)):
        start_col = table_index * column_step
        trace_grad = trace_grad + jnp.dot(
            flat_grad[:, start_col : start_col + column_step],
            tables[table_index].T,
            preferred_element_type=jnp.float32,
        )
    return (correl_share[None], trace_grad.reshape(win_dev, channels, samples).astype(jnp.bfloat16))


def solution(mesh):
    return jax.shard_map(
        on_device,
        mesh=mesh,
        in_specs=(P(("win", "grp"), None, None), P("win", None), P("win", None, None, None, None)),
        out_specs=(P("win", None, None, None, "grp"), P(("win", "grp"), None, None)),
        check_vma=False,
    )
```

profile of v0, /device:TPU:64, one launch (start us, length us, event | category | flops | bytes accessed | tf_op | source)
XLA Modules:
  0.0 815.4 jit_solution(5095351248463171921)
XLA Ops:
  7.3 1.4 copy-done
  8.8 17.5 %fusion.41 = f32[512,512]{1,0:T(8,128)S(1)} fusion(bf16[1,512,2048]{2,1,0:T(8,128)(2,1)S(1)} %copy-done, s32[512]{0:T(512)S(1)} %add_select_fusion.4, pred[512]{0:T(512)(128)(4,1)S(1)} %fusion.60), kind=kOutput, calls=%fused_computation.95 | convolution fusion | flops 1091567616 | bytes 3148288 | tf_op jit(solution)/shard_map/dot_general | solution.py:96
  26.2 17.2 %fusion.43 = f32[512,512]{1,0:T(8,128)S(1)} fusion(bf16[1,512,2048]{2,1,0:T(8,128)(2,1)S(1)} %copy-done, s32[512]{0:T(512)S(1)} %add_select_fusion.5, pred[512]{0:T(512)(128)(4,1)S(1)} %fusion.61), kind=kOutput, calls=%fused_computation.97 | convolution fusion | flops 1091567616 | bytes 3148288 | tf_op jit(solution)/shard_map/dot_general | solution.py:96
  43.4 17.6 %fusion.45 = f32[512,512]{1,0:T(8,128)S(1)} fusion(bf16[1,512,2048]{2,1,0:T(8,128)(2,1)S(1)} %copy-done, s32[512]{0:T(512)S(1)} %add_select_fusion.6, pred[512]{0:T(512)(128)(4,1)S(1)} %fusion.62), kind=kOutput, calls=%fused_computation.99 | convolution fusion | flops 1091567616 | bytes 3148288 | tf_op jit(solution)/shard_map/dot_general | solution.py:96
  61.0 17.2 %fusion.47 = f32[512,512]{1,0:T(8,128)S(1)} fusion(bf16[1,512,2048]{2,1,0:T(8,128)(2,1)S(1)} %copy-done, s32[512]{0:T(512)S(1)} %add_select_fusion.7, pred[512]{0:T(512)(128)(4,1)S(1)} %iota_compare_fusion), kind=kOutput, calls=%fused_computation.101 | convolution fusion | flops 1091567616 | bytes 3148288 | tf_op jit(solution)/shard_map/dot_general | solution.py:96
  79.2 2.0 copy-done.3
  82.7 3.9 fusion.16
  86.6 10.8 %copy.14 = bf16[1,512,2048]{2,0,1:T(2,128)(2,1)} copy(bf16[1,512,2048]{1,2,0:T(8,128)(2,1)} %fusion.16) | data formatting | bytes 4194304 | tf_op jit(solution)/shard_map/convert_element_type | solution.py:102
  98.0 13.2 %reduce.2 = bf16[512,2048]{1,0:T(8,128)(2,1)S(1)} reduce(bf16[512,1,2048]{2,1,0:T(2,128)(2,1)} %bitcast.118, bf16[]{:T(256)} %broadcast.306), dimensions={1}, to_apply=%bitcast.108.reduce_sub_computation | reduce | bytes 4194306
  111.1 2.8 reshape.499
  113.9 35.9 %all_to_all.21 = bf16[32,2,16384]{2,1,0:T(2,128)(2,1)S(1)} all-to-all(bf16[32,2,16384]{2,1,0:T(2,128)(2,1)} %reshape.499), channel_id=1, replica_groups=mesh['win'=32,'grp'=8] {'win'}, dimensions={0} | all-to-all | bytes 4194304 | tf_op jit(solution)/shard_map/all_to_all | solution.py:105
  149.8 6.8 reshape.500
  156.5 3.5 copy.17
  166.4 2.5 slice_convert_fusion.7
  169.0 38.9 %collective-permute-done.2 = bf16[32,16,2048]{2,1,0:T(8,128)(2,1)S(1)} collective-permute-done((bf16[32,16,2048]{2,1,0:T(8,128)(2,1)S(1)}, bf16[32,16,2048]{2,1,0:T(8,128)(2,1)S(1)}, u32[]{:S(2)}, u32[]{:S(2)}) %collective-permute-start.2) | collective-permute-done | bytes 2097184 | tf_op jit(solution)/shard_map/ppermute | solution.py:17
  207.9 3.9 collective-permute-done.1
  214.0 1.8 slice_convert_fusion.6
  215.8 3.7 slice_convert_fusion
  219.5 35.8 %add_reduce_fusion.9 = (f32[16,16,1024]{2,1,0:T(8,128)}, f32[16,16,1024]{2,1,0:T(8,128)}, f32[16,16,1024]{2,1,0:T(8,128)}, f32[16,16,1024]{2,1,0:T(8,128)}, f32[16,16,1024]{2,1,0:T(8,128)}, /*index=5*/f32[16,16,1024]{2,1,0:T(8,128)}) fusion(f32[32,16,1024]{2,1,0:T(8,128)} %get-tuple-element.50, f32[32,16,1024]{2,1,0:T(8,128)} %get-tuple-element.48, ...), kind=kLoop, calls=%fused_computation.19 | loop fusion | flops 199753728 | bytes 23068672 | tf_op jit(solution)/shard_map/reduce_sum | solution.py:57
  255.3 1.8 maximum_multiply_fusion.1
  258.3 3.4 maximum_multiply_fusion
  269.2 204.8 %all-reduce.4.cloned.1.call-done = f32[3,16,16,2048]{3,2,1,0:T(8,128)} async-done(((f32[3,16,16,2048]{3,2,1,0:T(8,128)}), f32[3,16,16,2048]{3,2,1,0:T(8,128)}) %all-reduce.4.cloned.1.call-update) | async-done | bytes 6291472 | tf_op jit(solution)/shard_map/psum | solution.py:125
  474.0 6.4 fusion.1
  480.4 1.3 slice_bitcast_fusion
  485.0 70.5 %subtract_reduce_fusion.2 = (bf16[32,16,1024]{2,1,0:T(8,128)(2,1)S(1)}, bf16[32,16,1024]{2,1,0:T(8,128)(2,1)S(1)}, f32[32,16,1024]{2,1,0:T(8,128)S(1)}, f32[32,1...) fusion(f32[16,16,1024]{2,1,0:T(8,128)S(1)} %get-tuple-element.5, ...), kind=kLoop, calls=%fused_computation.5 | loop fusion | flops 264241152 | bytes 23068672 | tf_op jit(solution)/shard_map/reduce_sum | solution.py:81
  555.5 1.9 pad_maximum_fusion.5
  557.3 4.2 collective-permute-start.5
  561.7 5.0 collective-permute-start.4
  566.8 1.5 pad_maximum_fusion.3
  568.2 3.3 collective-permute-start.3
  571.6 20.6 %add_reduce_fusion.4 = (f32[32,16,1024]{2,1,0:T(8,128)S(1)}, f32[32,16,1024]{2,1,0:T(8,128)S(1)}) fusion(f32[16,16,1024]{2,1,0:T(8,128)S(1)} %get-tuple-element.60, f32[16,16,1024]{2,1,0:T(8,128)S(1)} %get-tuple-element.59, f32[32,16,1024]{2,1,0:T(8,128)S(1)} %copy-done.9, f32[32,16,1024]{2,1,0:T(8,128)S(1)} %copy-done.10), kind=kLoop, calls=%fused_computation.9 | loop fusion | flops 66060288 | bytes 10485760 | tf_op jit(solution)/shard_map/reduce_sum | solution.py:69
  592.2 20.6 %add_reduce_fusion.5 = (f32[32,16,1024]{2,1,0:T(8,128)S(1)}, f32[32,16,1024]{2,1,0:T(8,128)S(1)}) fusion(f32[16,16,1024]{2,1,0:T(8,128)S(1)} %get-tuple-element.62, f32[16,16,1024]{2,1,0:T(8,128)S(1)} %get-tuple-element.61, f32[32,16,1024]{2,1,0:T(8,128)S(1)} %copy-done.8, f32[32,16,1024]{2,1,0:T(8,128)S(1)} %copy-done.7), kind=kLoop, calls=%fused_computation.11 | loop fusion | flops 66060288 | bytes 10485760 | tf_op jit(solution)/shard_map/reduce_sum | solution.py:69
  613.0 1.3 copy-done.4
  614.4 20.5 %add_reduce_fusion.6 = (f32[32,16,1024]{2,1,0:T(8,128)S(1)}, f32[32,16,1024]{2,1,0:T(8,128)S(1)}) fusion(f32[16,16,1024]{2,1,0:T(8,128)S(1)} %get-tuple-element.64, f32[16,16,1024]{2,1,0:T(8,128)S(1)} %get-tuple-element.63, f32[32,16,1024]{2,1,0:T(8,128)S(1)} %copy-done.4, f32[32,16,1024]{2,1,0:T(8,128)S(1)} %get-tuple-element.49), kind=kLoop, calls=%fused_computation.13 | loop fusion | flops 66060288 | bytes 10485760 | tf_op jit(solution)/shard_map/reduce_sum | solution.py:69
  634.9 14.6 %collective-permute-done.4 = bf16[32,16,2048]{2,1,0:T(8,128)(2,1)} collective-permute-done((bf16[32,16,2048]{2,1,0:T(8,128)(2,1)S(1)}, bf16[32,16,2048]{2,1,0:T(8,128)(2,1)}, u32[]{:S(2)}, u32[]{:S(2)}) %collective-permute-start.4) | collective-permute-done | bytes 2097184 | tf_op jit(solution)/shard_map/ppermute | solution.py:17
  649.6 5.7 fusion.25
  655.3 32.6 %all-to-all-start.1 = ((bf16[32,16,2048]{2,1,0:T(8,128)(2,1)}), bf16[32,16,2048]{2,1,0:T(8,128)(2,1)S(1)}, u32[]{:S(2)}, u32[]{:S(2)}) async-start(bf16[32,16,2048]{2,1,0:T(8,128)(2,1)} %fusion.25), calls=%async_computation.1 | async-start | bytes 4194304 | tf_op jit(solution)/shard_map/all_to_all | solution.py:142
  687.9 2.1 dynamic-slice_bitcast_fusion.3
  690.0 27.9 %all-to-all-done.1 = bf16[32,16,2048]{2,1,0:T(8,128)(2,1)S(1)} async-done(((bf16[32,16,2048]{2,1,0:T(8,128)(2,1)}), bf16[32,16,2048]{2,1,0:T(8,128)(2,1)S(1)}, u32[]{:S(2)}, u32[]{:S(2)}) %all-to-all-start.1) | async-done | bytes 2097184 | tf_op jit(solution)/shard_map/all_to_all | solution.py:142
  717.9 2.5 bitcast_convert_fusion
  720.4 5.5 copy.15
  725.9 3.5 fusion.39
  730.2 2.9 bitcast_multiply_fusion.1
  734.3 1.4 fusion.40
  735.7 17.7 %fusion.49 = f32[512,2048]{1,0:T(8,128)S(1)} fusion(s32[512]{0:T(512)S(1)} %add_select_fusion.5, pred[512]{0:T(512)(128)(4,1)S(1)} %fusion.61, bf16[512,2048]{0,1:T(8,128)(2,1)S(1)} %fusion.40), kind=kOutput, calls=%fused_computation.107 | convolution fusion | flops 1091567616 | bytes 4721152 | tf_op jit(solution)/shard_map/dot_general | solution.py:151
  753.5 17.8 %fusion.50 = f32[512,2048]{1,0:T(8,128)S(1)} fusion(s32[512]{0:T(512)S(1)} %add_select_fusion.6, pred[512]{0:T(512)(128)(4,1)S(1)} %fusion.62, bf16[512,2048]{0,1:T(8,128)(2,1)S(1)} %fusion.40), kind=kOutput, calls=%fused_computation.108 | convolution fusion | flops 1091567616 | bytes 4721152 | tf_op jit(solution)/shard_map/dot_general | solution.py:151
  771.2 18.1 %fusion.51 = f32[512,2048]{1,0:T(8,128)S(1)} fusion(s32[512]{0:T(512)S(1)} %add_select_fusion.7, pred[512]{0:T(512)(128)(4,1)S(1)} %iota_compare_fusion, bf16[512,2048]{0,1:T(8,128)(2,1)S(1)} %fusion.40), kind=kOutput, calls=%fused_computation.109 | convolution fusion | flops 1091567616 | bytes 4721152 | tf_op jit(solution)/shard_map/dot_general | solution.py:151
  789.4 19.0 %fusion.38 = bf16[1,512,2048]{2,1,0:T(8,128)(2,1)} fusion(f32[512,2048]{1,0:T(8,128)S(1)} %fusion.49, f32[512,2048]{1,0:T(8,128)S(1)} %fusion.51, f32[512,2048]{1,0:T(8,128)S(1)} %fusion.50, s32[512]{0:T(512)S(1)} %add_select_fusion.4, pred[512]{0:T(512)(128)(4,1)S(1)} %fusion.60, bf16[512,2048]{0,1:T(8,128)(2,1)S(1)} %fusion.40), kind=kOutput, calls=%fused_computation.84 | convolution fusion | flops 1095761920 | bytes 15206912 | tf_op jit(solution)/shard_map/dot_general | solution.py:151
  (90 shorter events, 16.5 us)
Async XLA Ops:
  7.2 1.6 copy-start
  7.2 466.8 %all-reduce.4.cloned.1.call-start = ((), (), s32[]{:S(2)}) async-start(), calls=%async_computation.2 | async-start | bytes 12582912 | tf_op jit(solution)/shard_map/psum | solution.py:125
  43.4 34.8 %copy-start.13 = (f32[512,512]{1,0:T(8,128)}, f32[512,512]{1,0:T(8,128)S(1)}, u32[]{:S(2)}) copy-start(f32[512,512]{1,0:T(8,128)S(1)} %fusion.43) | copy-start | bytes 3145732
  61.0 17.2 %copy-start.15 = (f32[512,512]{1,0:T(8,128)}, f32[512,512]{1,0:T(8,128)S(1)}, u32[]{:S(2)}) copy-start(f32[512,512]{1,0:T(8,128)S(1)} %fusion.45) | copy-start | bytes 3145732
  78.2 1.0 copy-start.17
  79.2 2.0 copy-start.3
  82.6 3.9 copy-start.5
  156.5 7.4 copy-start.25
  160.0 47.9 %collective-permute-start.2 = (bf16[32,16,2048]{2,1,0:T(8,128)(2,1)S(1)}, bf16[32,16,2048]{2,1,0:T(8,128)(2,1)S(1)}, u32[]{:S(2)}, u32[]{:S(2)}) collective-permute-start(bf16[32,16,2048]{2,1,0:T(8,128)(2,1)S(1)} %bitcast.111), channel_id=1, source_target_pairs={{24,0},{32,8},{40,16},{48,24},{56,32},{64,40},{72,48},{80,56},{88,... | collective-permute-start | bytes 6291464 | tf_op jit(solution)/shard_map/ppermute | solution.py:17
  161.3 50.5 %collective-permute-start.1 = (bf16[32,16,2048]{2,1,0:T(8,128)(2,1)S(1)}, bf16[32,16,2048]{2,1,0:T(8,128)(2,1)S(1)}, u32[]{:S(2)}, u32[]{:S(2)}) collective-permute-start(bf16[32,16,2048]{2,1,0:T(8,128)(2,1)S(1)} %bitcast.112), channel_id=1, source_target_pairs={{16,0},{24,8},{32,16},{40,24},{48,32},{56,40},{64,48},{72,56},{80,... | collective-permute-start | bytes 6291464 | tf_op jit(solution)/shard_map/ppermute | solution.py:17
  162.6 49.2 %collective-permute-start = (bf16[32,16,2048]{2,1,0:T(8,128)(2,1)S(1)}, bf16[32,16,2048]{2,1,0:T(8,128)(2,1)S(1)}, u32[]{:S(2)}, u32[]{:S(2)}) collective-permute-start(bf16[32,16,2048]{2,1,0:T(8,128)(2,1)S(1)} %bitcast.113), channel_id=1, source_target_pairs={{8,0},{16,8},{24,16},{32,24},{40,32},{48,40},{56,48},{64,56},{72,6... | collective-permute-start | bytes 6291464 | tf_op jit(solution)/shard_map/ppermute | solution.py:17
  255.3 1.9 copy-start.23
  255.3 2.2 copy-start.24
  255.3 2.5 copy-start.21
  255.3 2.8 copy-start.22
  482.8 1.6 copy-start.11
  482.8 2.2 copy-start.12
  555.5 6.0 copy-start.19
  555.5 6.0 copy-start.20
  557.3 77.6 %collective-permute-start.5 = (bf16[32,16,2048]{2,1,0:T(8,128)(2,1)S(1)}, bf16[32,16,2048]{2,1,0:T(8,128)(2,1)}, u32[]{:S(2)}, u32[]{:S(2)}) collective-permute-start(bf16[32,16,2048]{2,1,0:T(8,128)(2,1)S(1)} %pad_maximum_fusion.5), channel_id=1, source_target_pairs={{0,24},{8,32},{16,40},{24,48},{32,56},{40,64},{48,72},{56,80},{64,... | collective-permute-start | bytes 6291464 | tf_op jit(solution)/shard_map/ppermute | solution.py:17
  561.5 10.0 %copy-start.9 = (f32[32,16,1024]{2,1,0:T(8,128)S(1)}, f32[32,16,1024]{2,1,0:T(8,128)}, u32[]{:S(2)}) copy-start(f32[32,16,1024]{2,1,0:T(8,128)} %get-tuple-element.43) | copy-start | bytes 6291460
  561.5 10.0 %copy-start.10 = (f32[32,16,1024]{2,1,0:T(8,128)S(1)}, f32[32,16,1024]{2,1,0:T(8,128)}, u32[]{:S(2)}) copy-start(f32[32,16,1024]{2,1,0:T(8,128)} %get-tuple-element.44) | copy-start | bytes 6291460
  561.7 87.8 %collective-permute-start.4 = (bf16[32,16,2048]{2,1,0:T(8,128)(2,1)S(1)}, bf16[32,16,2048]{2,1,0:T(8,128)(2,1)}, u32[]{:S(2)}, u32[]{:S(2)}) collective-permute-start(bf16[32,16,2048]{2,1,0:T(8,128)(2,1)S(1)} %pad_maximum_fusion.4), channel_id=1, source_target_pairs={{0,16},{8,24},{16,32},{24,40},{32,48},{40,56},{48,64},{56,72},{64,... | collective-permute-start | bytes 6291464 | tf_op jit(solution)/shard_map/ppermute | solution.py:17
  568.2 81.3 %collective-permute-start.3 = (bf16[32,16,2048]{2,1,0:T(8,128)(2,1)}, bf16[32,16,2048]{2,1,0:T(8,128)(2,1)}, u32[]{:S(2)}, u32[]{:S(2)}) collective-permute-start(bf16[32,16,2048]{2,1,0:T(8,128)(2,1)} %pad_maximum_fusion.3), channel_id=1, source_target_pairs={{0,8},{8,16},{16,24},{24,32},{32,40},{40,48},{48,56},{56,64},{64,7... | collective-permute-start | bytes 6291464 | tf_op jit(solution)/shard_map/ppermute | solution.py:17
  571.6 20.6 %copy-start.7 = (f32[32,16,1024]{2,1,0:T(8,128)S(1)}, f32[32,16,1024]{2,1,0:T(8,128)}, u32[]{:S(2)}) copy-start(f32[32,16,1024]{2,1,0:T(8,128)} %get-tuple-element.68) | copy-start | bytes 6291460
  571.6 20.6 %copy-start.8 = (f32[32,16,1024]{2,1,0:T(8,128)S(1)}, f32[32,16,1024]{2,1,0:T(8,128)}, u32[]{:S(2)}) copy-start(f32[32,16,1024]{2,1,0:T(8,128)} %get-tuple-element.69) | copy-start | bytes 6291460
  592.2 20.6 %copy-start.18 = (bf16[16,16,2048]{2,1,0:T(8,128)(2,1)S(1)}, bf16[16,16,2048]{2,1,0:T(8,128)(2,1)}, u32[]{:S(2)}) copy-start(bf16[16,16,2048]{2,1,0:T(8,128)(2,1)} %get-tuple-element.42) | copy-start | bytes 3145732
  612.8 1.6 copy-start.4
  655.3 62.6 %all-to-all-start.1 = ((bf16[32,16,2048]{2,1,0:T(8,128)(2,1)}), bf16[32,16,2048]{2,1,0:T(8,128)(2,1)S(1)}, u32[]{:S(2)}, u32[]{:S(2)}) async-start(bf16[32,16,2048]{2,1,0:T(8,128)(2,1)} %fusion.25), calls=%async_computation.1 | async-start | bytes 4194304 | tf_op jit(solution)/shard_map/all_to_all | solution.py:142
  720.4 5.5 copy-start.14
  720.4 5.5 copy-start.16
  730.2 3.5 copy-start.2
  730.2 4.1 copy-start.6
  789.4 19.0 %copy-start.1 = (bf16[1,512,2048]{2,1,0:T(8,128)(2,1)S(1)}, bf16[1,512,2048]{2,1,0:T(8,128)(2,1)}, u32[]{:S(2)}) copy-start(bf16[1,512,2048]{2,1,0:T(8,128)(2,1)} %param.3) | copy-start | bytes 6291460
Sparse Core Ops, SparseCore 0:
  261.9 212.0 all-reduce.3
where the time goes:
time: 826 us; the launch traced here: 815 us
  waiting for transfers between devices  290 us (35%)
  other arithmetic  230 us (28%)
  matrix products  142 us (17%)
  starting transfers between devices  49.1 us (6%)
  local copies, waits for them, and re-layouts  43.9 us (5%)
  blocking collectives  35.9 us (4%)
  between operations  24 us (3%)
    psum x1, waiting for transfers between devices, on_device(): totals = lax.psum(correl, 'grp')  205 us
    dot_general x4, matrix products, on_device(): jnp.dot(flat_grad[:, start_col:start_col + column_step], tables[table_ind...  72.6 us
    reduce_sum x1, other arithmetic, pull_second(): real_part = jnp.sum(left_real * right_real - left_imag * right_imag, axis=1)  70.5 us
    dot_general x4, matrix products, on_device(): jnp.dot(flat_traces, table_part, preferred_element_type=jnp.float32)  69.4 us
    reduce_sum x3, other arithmetic, pull_first(): real_part = jnp.sum(left_real * right_real + left_imag * right_imag, axis=2)  61.7 us
    ppermute x6, waiting for transfers between devices, passed_along(): return lax.ppermute(array, axis, pairs)  57.5 us
    all_to_all x1, blocking collectives, on_device(): lax.all_to_all(whitened, 'win', split_axis=1, concat_axis=0, tiled=True)  35.9 us
    reduce_sum x1, other arithmetic, correlate(): real_sum = jnp.sum(left_real * right_real + left_imag * right_imag, axis=0)  35.8 us
  transfers between devices with their start and end apart: 8, of which 5 were waited for; matrix products, arithmetic and copies ran while one was open for 8% of the time, Pallas kernels for 0%

commit v1 on v0

v1 whole, which is shorter than its diff:
```python
import functools
import math

import jax
import jax.numpy as jnp
import numpy as np
from jax import lax
from jax.experimental import pallas as pl
from jax.experimental.pallas import tpu as pltpu
from jax.sharding import PartitionSpec as P

SEG = 2048
FREQ = 1024
BAND = 64
OFFSETS = 4
CB = 16
SLOTS = 3
CH = 512
WINS = 256
NB = 32
GRP = 8
KB = 4
LANES = 128
HALF = 64
EMPTY = 64.0
VMEM_LIMIT = 56 << 20

F32 = jnp.float32
BF16 = jnp.bfloat16


def plane_of(q, h):
    return (q + 3) % GRP if h == 0 else (q + 7) % GRP


def table_parts():
    row = np.arange(2 * BAND)
    j = (row // 8) * KB + row % KB
    imag = (row % 8) >= KB
    n = np.arange(SEG)
    ang = 2.0 * math.pi * ((n[None, :] * j[:, None]) % SEG) / SEG
    a = np.where(imag[:, None], -np.sin(ang), np.cos(ang))
    b = np.where(imag[:, None], -np.cos(ang), -np.sin(ang))
    band = np.arange(FREQ // BAND)
    bang = 2.0 * math.pi * ((n[None, :] * (BAND * band[:, None])) % SEG) / SEG
    return [np.asarray(v, np.float32) for v in (a, b, np.cos(bang), np.sin(bang))]


def dot(x, y, cx=1, cy=0):
    return lax.dot_general(x, y, (((cx,), (cy,)), ((), ())), preferred_element_type=F32)


def regroup(inverse):
    out = lax.broadcasted_iota(jnp.int32, (256, 256), 0)
    src = lax.broadcasted_iota(jnp.int32, (256, 256), 1)
    if inverse:
        hit = (src % 32) * 8 + src // 32 == out
    else:
        hit = (out % 32) * 8 + out // 32 == src
    return jnp.where(hit, 1.0, 0.0).astype(BF16)


def full(shape):
    return pl.BlockSpec(shape, lambda *i: (0,) * len(shape))


def forward_kernel(x_ref, a_ref, b_ref, c_ref, s_ref, y_ref, r_ref):
    step = pl.program_id(0)
    parts = []
    for wh in range(2):
        band = step * 2 + wh
        c = c_ref[pl.ds(band, 1), :]
        s = s_ref[pl.ds(band, 1), :]
        parts.append((a_ref[...] * c + b_ref[...] * s).astype(BF16))
    table = jnp.concatenate(parts, axis=0)
    spec = dot(table, x_ref[...], 1, 1)
    for wh in range(2):
        rows = spec[wh * 128 : (wh + 1) * 128]
        level = jnp.sum(rows * rows, axis=0, keepdims=True) * (1.0 / BAND) + 1e-05
        inv = lax.rsqrt(level)
        r_ref[0, wh : wh + 1, :] = inv
        y_ref[wh * 16 : (wh + 1) * 16, 0] = (rows * inv).reshape(16, 8, CH).astype(BF16)


def plane_index(step):
    q, h = step // 2, step % 2
    return jnp.where(h == 0, q + 3, (q + 7) % GRP)


def forward(x, consts):
    return pl.pallas_call(
        forward_kernel,
        grid=(8,),
        in_specs=[full((CH, SEG)), full((128, SEG)), full((128, SEG)), full((16, SEG)), full((16, SEG))],
        out_specs=[
            pl.BlockSpec((32, 1, 8, CH), lambda i: (0, plane_index(i), 0, 0)),
            pl.BlockSpec((1, 2, CH), lambda i: (i, 0, 0)),
        ],
        out_shape=[
            jax.ShapeDtypeStruct((32, GRP, 8, CH), BF16),
            jax.ShapeDtypeStruct((8, 2, CH), F32),
        ],
        compiler_params=pltpu.CompilerParams(vmem_limit_bytes=VMEM_LIMIT),
        cost_estimate=pl.CostEstimate(flops=2 * CH * SEG * SEG, bytes_accessed=8 << 20, transcendentals=0),
        name="forward",
    )(x, *consts)


def backward_kernel(g_ref, y_ref, r_ref, a_ref, b_ref, c_ref, s_ref, o_ref, d_ref):
    @pl.when(pl.program_id(0) == 0)
    def _():
        for step in range(8):
            plane = plane_of(step // 2, step % 2)
            for wh in range(2):
                g = g_ref[wh * 16 : (wh + 1) * 16, plane].astype(F32).reshape(128, CH)
                y = y_ref[wh * 16 : (wh + 1) * 16, plane].astype(F32).reshape(128, CH)
                mean = jnp.sum(g * y, axis=0, keepdims=True) * (1.0 / BAND)
                d = (g - y * mean) * r_ref[step, wh : wh + 1, :]
                row = (step * 2 + wh) * 128
                d_ref[:, row : row + 128] = d.T.astype(BF16)

    parts = []
    for band in range(16):
        c = c_ref[band : band + 1, :]
        s = s_ref[band : band + 1, :]
        parts.append((a_ref[...] * c + b_ref[...] * s).astype(BF16))
    table = jnp.concatenate(parts, axis=0)
    o_ref[...] = dot(d_ref[...], table).astype(BF16)


def backward(g, y, r, consts):
    tile = 256
    col = lambda rows: pl.BlockSpec((rows, tile), lambda i: (0, i))
    return pl.pallas_call(
        backward_kernel,
        grid=(SEG // tile,),
        in_specs=[
            full((32, GRP, 8, CH)),
            full((32, GRP, 8, CH)),
            full((8, 2, CH)),
            col(128),
            col(128),
            col(16),
            col(16),
        ],
        out_specs=pl.BlockSpec((CH, tile), lambda i: (0, i)),
        out_shape=jax.ShapeDtypeStruct((CH, SEG), BF16),
        scratch_shapes=[pltpu.VMEM((CH, SEG), BF16)],
        compiler_params=pltpu.CompilerParams(vmem_limit_bytes=VMEM_LIMIT),
        cost_estimate=pl.CostEstimate(flops=2 * CH * SEG * SEG, bytes_accessed=10 << 20, transcendentals=0),
        name="backward",
    )(g, y, r, *consts)


def pack_kernel(sc_ref, re_ref, im_ref, o_ref):
    perm = regroup(True)
    for ri, src in enumerate((re_ref, im_ref)):
        turned = []
        for i in range(8):
            rows = []
            for ih in range(2):
                for o in range(OFFSETS):
                    val = jnp.full((CB, LANES), EMPTY, F32)
                    for s in range(SLOTS):
                        val = jnp.where(sc_ref[s] == o, src[s, ih * 8 + i], val)
                    rows.append(val)
            turned.append(jnp.concatenate(rows, axis=0).T.astype(BF16))
        for gr in range(4):
            stack = jnp.concatenate([t[gr * 32 : (gr + 1) * 32] for t in turned], axis=0)
            tile = dot(perm, stack).reshape(8, KB, 8, LANES)
            o_ref[gr * 8 : (gr + 1) * 8, ri] = tile.astype(BF16)


def pack_observed(scalars, observed):
    spec = lambda base: pl.BlockSpec((SLOTS, CB, CB, LANES), lambda i, sc: (0, 0, 0, base + sc[3]))
    return pl.pallas_call(
        pack_kernel,
        grid_spec=pltpu.PrefetchScalarGridSpec(
            num_scalar_prefetch=1,
            grid=(1,),
            in_specs=[spec(0), spec(8)],
            out_specs=pl.BlockSpec((32, 2, KB, 8, LANES), lambda i, sc: (0, 0, 0, 0, 0)),
        ),
        out_shape=jax.ShapeDtypeStruct((32, 2, KB, 8, LANES), BF16),
        compiler_params=pltpu.CompilerParams(vmem_limit_bytes=VMEM_LIMIT),
        name="pack_observed",
    )(scalars, observed, observed)


def middle_kernel(sc_ref, x_ref, obs_ref, corr_ref, out_ref, u_ref, d_ref):
    half = sc_ref[4]
    perm = regroup(False)
    for gr in range(8):
        y = dot(perm, x_ref[gr * 256 : (gr + 1) * 256, :]).astype(BF16)
        for r8 in range(8):
            ri, k = r8 // KB, r8 % KB
            row = ri * WINS + gr * 32
            u_ref[k, row : row + 32, :] = y[r8 * 32 : (r8 + 1) * 32]

    lane8 = lax.broadcasted_iota(jnp.int32, (8, LANES), 1)
    lane16 = lax.broadcasted_iota(jnp.int32, (16, LANES), 1)

    def one_bin(k, carry):
        later = None
        for b in range(4):
            width = 2 if b < 3 else 1
            cols = slice(b * LANES, (b + width) * LANES)
            lead = u_ref[k, :, b * LANES : (b + 1) * LANES]
            re_rows = u_ref[k, :WINS, cols]
            im_rows = u_ref[k, WINS:, cols]
            straight = jnp.concatenate([re_rows, im_rows], axis=0)
            crossed = jnp.concatenate([im_rows, -re_rows], axis=0)
            gram = dot(lead.T, jnp.concatenate([straight, crossed], axis=1))
            tiles = ([], [])
            for blk in range(8):
                a, shift = b * 8 + blk, blk * CB
                for ri in range(2):
                    base = ri * width * LANES
                    here = gram[shift : shift + 16, base : base + LANES]
                    if shift > 0:
                        if shift > HALF and width == 2:
                            there = gram[shift : shift + 16, base + LANES : base + 2 * LANES]
                            here = jnp.where(lane16 >= shift, here, there)
                        here = pltpu.roll(here, LANES - shift, 1)
                    packed = jnp.where(lane8 < HALF, here[:8], pltpu.roll(here[8:], HALF, 1))
                    packed = packed * (1.0 / WINS)
                    seen = obs_ref[a, ri, k].astype(F32)
                    live = seen < EMPTY / 2
                    slot = 1 - half if ri == 0 else half
                    corr_ref[slot, a, k] = packed.astype(BF16)
                    resid = jnp.where(live, packed - seen, 0.0)
                    spread = jnp.concatenate([resid, pltpu.roll(resid, HALF, 1)], axis=0)
                    spread = jnp.where(lane16 < HALF, spread, 0.0)
                    if shift > 0:
                        spread = pltpu.roll(spread, shift, 1)
                    if shift > HALF:
                        first = jnp.where(lane16 >= shift, spread, 0.0)
                        second = jnp.where(lane16 < shift, spread, 0.0)
                    else:
                        first, second = spread, jnp.zeros_like(spread)
                    tiles[ri].append([first, second][:width])
            res = [
                [jnp.concatenate([t[p] for t in tiles[ri]], axis=0).astype(BF16) for p in range(width)]
                for ri in range(2)
            ]
            top = jnp.concatenate([m for p in range(width) for m in (res[0][p], res[1][p])], axis=1)
            low = jnp.concatenate([m for p in range(width) for m in (-res[1][p], res[0][p])], axis=1)
            weights = jnp.concatenate([top, low], axis=0)
            waves = [
                u_ref[k, ri * WINS : (ri + 1) * WINS, (b + p) * LANES : (b + p + 1) * LANES]
                for p in range(width)
                for ri in range(2)
            ]
            pulled = dot(jnp.concatenate(waves, axis=1), weights, 1, 1)
            pushed = dot(jnp.concatenate(waves[:2], axis=1), weights)
            grad = pulled + pushed[:, :256]
            if later is not None:
                grad = grad + later
            later = pushed[:, 256:] if width == 2 else None
            d_ref[k, :WINS, b * LANES : (b + 1) * LANES] = grad[:, :LANES].astype(BF16)
            d_ref[k, WINS:, b * LANES : (b + 1) * LANES] = grad[:, LANES:].astype(BF16)
        return carry

    lax.fori_loop(0, KB, one_bin, 0)
    back = regroup(True)
    for gr in range(8):
        rows = jnp.concatenate(
            [
                d_ref[r8 % KB, (r8 // KB) * WINS + gr * 32 : (r8 // KB) * WINS + gr * 32 + 32, :]
                for r8 in range(8)
            ],
            axis=0,
        )
        out_ref[gr * 256 : (gr + 1) * 256, :] = dot(back, rows).astype(BF16)


def middle(scalars, x, obs):
    block = lambda shape: pl.BlockSpec(shape, lambda i, sc: (0,) * len(shape))
    return pl.pallas_call(
        middle_kernel,
        grid_spec=pltpu.PrefetchScalarGridSpec(
            num_scalar_prefetch=1,
            grid=(1,),
            in_specs=[block((2048, CH)), block((NB, 2, KB, 8, LANES))],
            out_specs=[block((2, NB, KB, 8, LANES)), block((2048, CH))],
            scratch_shapes=[pltpu.VMEM((KB, 2 * WINS, CH), BF16), pltpu.VMEM((KB, 2 * WINS, CH), BF16)],
        ),
        out_shape=[
            jax.ShapeDtypeStruct((2, NB, KB, 8, LANES), BF16),
            jax.ShapeDtypeStruct((2048, CH), BF16),
        ],
        compiler_params=pltpu.CompilerParams(vmem_limit_bytes=VMEM_LIMIT),
        name="middle",
    )(scalars, x, obs)


def unpack_kernel(sc_ref, x_ref, o_ref):
    perm = regroup(False)
    for h in range(2):
        first = sc_ref[5]
        index = first if h == 0 else 1 - first
        regrouped = []
        for gr in range(4):
            rows = x_ref[gr * 8 : (gr + 1) * 8, index].astype(F32).reshape(256, LANES).astype(BF16)
            regrouped.append(dot(perm, rows))
        for i in range(8):
            page = jnp.concatenate([r[i * 32 : (i + 1) * 32] for r in regrouped], axis=0)
            turned = page.T
            for ih in range(2):
                for s in range(SLOTS):
                    val = jnp.zeros((CB, LANES), F32)
                    for o in range(OFFSETS):
                        row = ih * HALF + o * CB
                        val = jnp.where(sc_ref[s] == o, turned[row : row + CB], val)
                    o_ref[s, ih * 8 + i, :, h * LANES : (h + 1) * LANES] = val


def unpack_correl(scalars, x):
    block = lambda shape: pl.BlockSpec(shape, lambda i, sc: (0,) * len(shape))
    return pl.pallas_call(
        unpack_kernel,
        grid_spec=pltpu.PrefetchScalarGridSpec(
            num_scalar_prefetch=1,
            grid=(1,),
            in_specs=[block((32, 2, KB, 8, LANES))],
            out_specs=block((SLOTS, CB, CB, 2 * LANES)),
        ),
        out_shape=jax.ShapeDtypeStruct((SLOTS, CB, CB, 2 * LANES), F32),
        compiler_params=pltpu.CompilerParams(vmem_limit_bytes=VMEM_LIMIT),
        name="unpack_correl",
    )(scalars, x)


def on_device(traces, pair_lists, observed):
    consts = [jnp.asarray(v) for v in table_parts()]
    g = lax.axis_index("grp")
    half = jnp.where(jnp.logical_and(g >= 3, g <= 6), 0, 1)
    q = jnp.where(half == 0, g - 3, (g + 1) % GRP)
    low = jnp.where(g < 4, 1, 0)
    scalars = jnp.concatenate([pair_lists[0], jnp.stack([2 * q + half, half, low]).astype(jnp.int32)])

    packed = pack_observed(scalars, observed[0])
    seen = lax.all_to_all(packed, "win", 0, 0)
    white, inverse = forward(traces[0], consts)
    moved = lax.all_to_all(white.reshape(WINS, 8, CH), ("win", "grp"), 0, 0)
    corr, grad = middle(scalars, moved.reshape(2048, CH), seen)
    up = lax.ppermute(corr[0], "grp", [(i, (i + 1) % GRP) for i in range(GRP)])
    down = lax.ppermute(corr[1], "grp", [(i, (i - 3) % GRP) for i in range(GRP)])
    returned = lax.all_to_all(grad.reshape(WINS, 8, CH), ("win", "grp"), 0, 0)
    owned = lax.all_to_all(jnp.stack([up, down], axis=1), "win", 0, 0)
    trace_grad = backward(returned.reshape(32, GRP, 8, CH), white, inverse, consts)
    correl = unpack_correl(scalars, owned)
    return correl[None], trace_grad[None]


def solution(mesh):
    return jax.shard_map(
        on_device,
        mesh=mesh,
        in_specs=(P(("win", "grp"), None, None), P("win", None), P("win", None, None, None, None)),
        out_specs=(P("win", None, None, None, "grp"), P(("win", "grp"), None, None)),
        check_vma=False,
    )
```

time: 826 us -> 221 us (0.27)
  other arithmetic: 230 us -> 1.37 us
  waiting for transfers between devices: 290 us -> 69.2 us
  matrix products: 142 us -> 0 us
  blocking collectives: 35.9 us -> 80.4 us
  Pallas kernels: 0 us -> 43.4 us
  local copies, waits for them, and re-layouts: 43.9 us -> 2.39 us
  starting transfers between devices: 49.1 us -> 19.9 us
  between operations: 24 us -> 0.69 us
    psum x1 -> x0, waiting for transfers between devices: 205 us -> none  [on_device(): totals = lax.psum(correl, 'grp')]
    reduce_sum x7 -> x0, other arithmetic: 169 us -> none  [the longest x1 70.5 us: pull_second(): real_part = jnp.sum(left_real * right_real - left_imag * right_imag, axis=1)]
    dot_general x8 -> x0, matrix products: 142 us -> none  [the longest x4 72.6 us: on_device(): jnp.dot(flat_grad[:, start_col:start_col + column_step], tables[table_ind...]
    all_to_all x1 -> x2, blocking collectives: 35.9 us -> 80.4 us  [the longest x1 65 us: on_device(): moved = lax.all_to_all(white.reshape(WINS, 8, CH), ('win', 'grp'), 0, 0)]
    pallas_call x0 -> x5, Pallas kernels: none -> 43.4 us  [the longest x1 15.6 us: middle(): pl.pallas_call(middle_kernel, grid_spec=pltpu.PrefetchScalarGridSpec(num_...]
    ppermute x6 -> x2, waiting for transfers between devices: 57.5 us -> 17.6 us  [the longest x1 14.8 us: on_device(): lax.ppermute(corr[1], 'grp', [(i, (i - 3) % GRP) for i in range(GRP)])]
    convert_element_type x15 -> x0, other arithmetic: 28 us -> none  [the longest x10 9.5 us: widen(): return operand.astype(jnp.float32)]
    all_to_all x1 -> x2, waiting for transfers between devices: 27.9 us -> 51.5 us  [the longest x1 49.5 us: on_device(): returned = lax.all_to_all(grad.reshape(WINS, 8, CH), ('win', 'grp'), 0, 0)]
  transfers between devices with their start and end apart: 8 -> 4, of which waited for: 5 -> 4; matrix products, arithmetic and copies ran while one was open for 8% -> 0% of each run, Pallas kernels for 0% -> 6%
where the time goes in v1:
time: 221 us; the launch traced here: 217 us
  blocking collectives  80.4 us (36%)
  waiting for transfers between devices  69.2 us (31%)
  Pallas kernels  43.4 us (20%)
  starting transfers between devices  19.9 us (9%)
  local copies, waits for them, and re-layouts  2.39 us (1%)
    all_to_all x1, blocking collectives, on_device(): moved = lax.all_to_all(white.reshape(WINS, 8, CH), ('win', 'grp'), 0, 0)  65 us
    all_to_all x1, waiting for transfers between devices, on_device(): returned = lax.all_to_all(grad.reshape(WINS, 8, CH), ('win', 'grp'), 0, 0)  49.5 us
    pallas_call x1, Pallas kernels, middle(): pl.pallas_call(middle_kernel, grid_spec=pltpu.PrefetchScalarGridSpec(num_...  15.6 us
    all_to_all x1, blocking collectives, on_device(): owned = lax.all_to_all(jnp.stack([up, down], axis=1), 'win', 0, 0)  15.4 us
    ppermute x1, waiting for transfers between devices, on_device(): lax.ppermute(corr[1], 'grp', [(i, (i - 3) % GRP) for i in range(GRP)])  14.8 us
    pallas_call x1, Pallas kernels, backward(): pl.pallas_call(backward_kernel, grid=(SEG // tile,), in_specs=[full((32,...  11.8 us
    pallas_call x1, Pallas kernels, forward(): pl.pallas_call(forward_kernel, grid=(8,), in_specs=[full((CH, SEG)), full...  9.72 us
    all_to_all x1, starting transfers between devices, on_device(): returned = lax.all_to_all(grad.reshape(WINS, 8, CH), ('win', 'grp'), 0, 0)  7.85 us
  transfers between devices with their start and end apart: 4, of which 4 were waited for; matrix products, arithmetic and copies ran while one was open for 0% of the time, Pallas kernels for 6%

profile of v1, /device:TPU:64, one launch (start us, length us, event | category | flops | bytes accessed | tf_op | source)
XLA Modules:
  0.0 217.3 jit_solution(10906272948107963666)
XLA Ops:
  0.7 1.3 pad_add_fusion.sc_ref
  2.0 3.1 %pack_observed.1 = bf16[32,2,4,8,128]{4,3,2,1,0:T(8,128)(2,1)} custom-call(s32[6]{0:T(128)} %pad_add_fusion.sc_ref, f32[3,16,16,2048]{3,2,1,0:T(8,128)} %bitcast.18, f32[3,16,16,2048]{3,2,1,0:T(8,128)} %bitcast.19), custom_call_target="tpu_custom_call" | custom-call | tf_op jit(solution)/shard_map/pack_observed/pallas_call | solution.py:176
  5.1 7.3 %all-to-all-start.1 = ((bf16[32,2,4,8,128]{4,3,2,1,0:T(8,128)(2,1)}), bf16[32,2,4,8,128]{4,3,2,1,0:T(8,128)(2,1)S(1)}, u32[]{:S(2)}, u32[]{:S(2)}) async-start(bf16[32,2,4,8,128]{4,3,2,1,0:T(8,128)(2,1)} %pack_observed.1), calls=%async_computation.1 | async-start | bytes 1048576 | tf_op jit(solution)/shard_map/all_to_all | solution.py:343
  12.4 9.7 %forward.1 = (bf16[32,8,8,512]{3,2,1,0:T(8,128)(2,1)}, f32[8,2,512]{2,1,0:T(2,128)}) custom-call(bf16[512,2048]{1,0:T(8,128)(2,1)} %bitcast.27, f32[128,2048]{1,0:T(8,128)} %constant.38.clone.a_ref, f32[128,2048]{1,0:T(8,128)} %constant.39.clone.b_ref, f32[16,2048]{1,0:T(8,128)} %constant.40.clone.c_ref, f32[16,2048]{1,0:T(8,128)} %constant.41.clone.s_ref), custom_call_target="tpu_custom_call" | custom-call | flops 4294967296 | bytes 8388608 | tf_op jit(solution)/shard_map/forward/pallas_call | solution.py:91
  22.2 2.0 all-to-all-done.1.obs_ref
  24.2 0.0 copy-start.1
  24.2 65.0 %all_to_all.20 = bf16[256,8,512]{2,1,0:T(8,128)(2,1)} all-to-all(bf16[256,8,512]{2,1,0:T(8,128)(2,1)} %bitcast.21), channel_id=1, replica_groups=mesh['win'=32,'grp'=8] {'win','grp'}, dimensions={0} | all-to-all | bytes 4194304 | tf_op jit(solution)/shard_map/all_to_all | solution.py:345
  89.2 0.0 copy-done.1
  89.2 15.6 %middle.1 = (bf16[2,32,4,8,128]{4,3,2,1,0:T(8,128)(2,1)}, bf16[2048,512]{1,0:T(8,128)(2,1)}) custom-call(s32[6]{0:T(128)} %pad_add_fusion.sc_ref, bf16[2048,512]{1,0:T(8,128)(2,1)} %bitcast.20, bf16[32,2,4,8,128]{4,3,2,1,0:T(8,128)(2,1)} %copy-done.1), custom_call_target="tpu_custom_call" | custom-call | tf_op jit(solution)/shard_map/middle/pallas_call | solution.py:279
  104.8 1.1 slice_bitcast_fusion.1
  105.9 1.4 collective-permute-start
  107.3 3.3 %collective-permute-start.1 = (bf16[32,4,8,128]{3,2,1,0:T(8,128)(2,1)S(1)}, bf16[32,4,8,128]{3,2,1,0:T(8,128)(2,1)S(1)}, u32[]{:S(2)}, u32[]{:S(2)}) collective-permute-start(bf16[32,4,8,128]{3,2,1,0:T(8,128)(2,1)S(1)} %get-tuple-element.11), channel_id=1, source_target_pairs={{0,5},{1,6},{2,7},{3,0},{4,1},{5,2},{6,3},{7,4},{8,13},{9,14},{10,... | collective-permute-start | bytes 786440 | tf_op jit(solution)/shard_map/ppermute | solution.py:348
  110.6 2.8 %collective-permute-done = bf16[32,4,8,128]{3,2,1,0:T(8,128)(2,1)S(1)} collective-permute-done((bf16[32,4,8,128]{3,2,1,0:T(8,128)(2,1)S(1)}, bf16[32,4,8,128]{3,2,1,0:T(8,128)(2,1)S(1)}, u32[]{:S(2)}, u32[]{:S(2)}) %collective-permute-start) | collective-permute-done | bytes 262176 | tf_op jit(solution)/shard_map/ppermute | solution.py:347
  113.4 14.8 %collective-permute-done.1 = bf16[32,4,8,128]{3,2,1,0:T(8,128)(2,1)S(1)} collective-permute-done((bf16[32,4,8,128]{3,2,1,0:T(8,128)(2,1)S(1)}, bf16[32,4,8,128]{3,2,1,0:T(8,128)(2,1)S(1)}, u32[]{:S(2)}, u32[]{:S(2)}) %collective-permute-start.1) | collective-permute-done | bytes 262176 | tf_op jit(solution)/shard_map/ppermute | solution.py:348
  128.3 15.4 %all_to_all.21.x_ref = bf16[32,2,4,8,128]{4,3,2,1,0:T(8,128)(2,1)} all-to-all(bf16[32,2,4,8,128]{4,3,2,1,0:T(8,128)(2,1)S(1)} %pad_maximum_fusion), channel_id=1, replica_groups=mesh['win'=32,'grp'=8] {'win'}, dimensions={0} | all-to-all | bytes 1048576 | tf_op jit(solution)/shard_map/all_to_all | solution.py:350
  143.7 7.9 %all-to-all-start.3 = ((bf16[256,8,512]{2,1,0:T(8,128)(2,1)}), bf16[256,8,512]{2,1,0:T(8,128)(2,1)S(1)}, u32[]{:S(2)}, u32[]{:S(2)}) async-start(bf16[256,8,512]{2,1,0:T(8,128)(2,1)} %bitcast.13), calls=%async_computation.3 | async-start | bytes 4194304 | tf_op jit(solution)/shard_map/all_to_all | solution.py:349
  151.6 3.1 %unpack_correl.1 = f32[3,16,16,256]{3,2,1,0:T(8,128)} custom-call(s32[6]{0:T(128)} %pad_add_fusion.sc_ref, bf16[32,2,4,8,128]{4,3,2,1,0:T(8,128)(2,1)} %all_to_all.21.x_ref), custom_call_target="tpu_custom_call" | custom-call | tf_op jit(solution)/shard_map/unpack_correl/pallas_call | solution.py:320
  154.7 49.5 %all-to-all-done.3 = bf16[256,8,512]{2,1,0:T(8,128)(2,1)S(1)} async-done(((bf16[256,8,512]{2,1,0:T(8,128)(2,1)}), bf16[256,8,512]{2,1,0:T(8,128)(2,1)S(1)}, u32[]{:S(2)}, u32[]{:S(2)}) %all-to-all-start.3) | async-done | bytes 2097184 | tf_op jit(solution)/shard_map/all_to_all | solution.py:349
  204.2 0.0 copy-start
  204.2 1.3 copy-done
  205.6 11.8 %backward.1 = bf16[512,2048]{1,0:T(8,128)(2,1)} custom-call(bf16[32,8,8,512]{3,2,1,0:T(8,128)(2,1)} %bitcast.22, bf16[32,8,8,512]{3,2,1,0:T(8,128)(2,1)} %get-tuple-element.6.y_ref, f32[8,2,512]{2,1,0:T(2,128)} %get-tuple-element.9.r_ref, f32[128,2048]{1,0:T(8,128)} %constant.38.clone.a_ref, f32[128,2048]{1,0:T(8,128)} %constant.39.clone.b_ref, ...), custom_call_target="tpu_custom_call" | custom-call | flops 4294967296 | bytes 10485760 | tf_op jit(solution)/shard_map/backward/pallas_call | solution.py:134
  (1 shorter events, 0.0 us)
Async XLA Ops:
  5.1 19.1 %all-to-all-start.1 = ((bf16[32,2,4,8,128]{4,3,2,1,0:T(8,128)(2,1)}), bf16[32,2,4,8,128]{4,3,2,1,0:T(8,128)(2,1)S(1)}, u32[]{:S(2)}, u32[]{:S(2)}) async-start(bf16[32,2,4,8,128]{4,3,2,1,0:T(8,128)(2,1)} %pack_observed.1), calls=%async_computation.1 | async-start | bytes 1048576 | tf_op jit(solution)/shard_map/all_to_all | solution.py:343
  24.2 65.0 %copy-start.1 = (bf16[32,2,4,8,128]{4,3,2,1,0:T(8,128)(2,1)}, bf16[32,2,4,8,128]{4,3,2,1,0:T(8,128)(2,1)S(1)}, u32[]{:S(2)}) copy-start(bf16[32,2,4,8,128]{4,3,2,1,0:T(8,128)(2,1)S(1)} %all-to-all-done.1.obs_ref) | copy-start | bytes 1572868
  105.9 7.5 %collective-permute-start = (bf16[32,4,8,128]{3,2,1,0:T(8,128)(2,1)S(1)}, bf16[32,4,8,128]{3,2,1,0:T(8,128)(2,1)S(1)}, u32[]{:S(2)}, u32[]{:S(2)}) collective-permute-start(bf16[32,4,8,128]{3,2,1,0:T(8,128)(2,1)S(1)} %get-tuple-element.10), channel_id=1, source_target_pairs={{0,1},{1,2},{2,3},{3,4},{4,5},{5,6},{6,7},{7,0},{8,9},{9,10},{10,1... | collective-permute-start | bytes 786440 | tf_op jit(solution)/shard_map/ppermute | solution.py:347
  107.3 21.0 %collective-permute-start.1 = (bf16[32,4,8,128]{3,2,1,0:T(8,128)(2,1)S(1)}, bf16[32,4,8,128]{3,2,1,0:T(8,128)(2,1)S(1)}, u32[]{:S(2)}, u32[]{:S(2)}) collective-permute-start(bf16[32,4,8,128]{3,2,1,0:T(8,128)(2,1)S(1)} %get-tuple-element.11), channel_id=1, source_target_pairs={{0,5},{1,6},{2,7},{3,0},{4,1},{5,2},{6,3},{7,4},{8,13},{9,14},{10,... | collective-permute-start | bytes 786440 | tf_op jit(solution)/shard_map/ppermute | solution.py:348
  143.7 60.5 %all-to-all-start.3 = ((bf16[256,8,512]{2,1,0:T(8,128)(2,1)}), bf16[256,8,512]{2,1,0:T(8,128)(2,1)S(1)}, u32[]{:S(2)}, u32[]{:S(2)}) async-start(bf16[256,8,512]{2,1,0:T(8,128)(2,1)} %bitcast.13), calls=%async_computation.3 | async-start | bytes 4194304 | tf_op jit(solution)/shard_map/all_to_all | solution.py:349
  204.2 1.3 copy-start

commit v2 on v1

--- a/solution.py
+++ b/solution.py
@@ -347,6 +347,7 @@
     up = lax.ppermute(corr[0], "grp", [(i, (i + 1) % GRP) for i in range(GRP)])
     down = lax.ppermute(corr[1], "grp", [(i, (i - 3) % GRP) for i in range(GRP)])
     returned = lax.all_to_all(grad.reshape(WINS, 8, CH), ("win", "grp"), 0, 0)
+    up, down, returned = lax.optimization_barrier((up, down, returned))
     owned = lax.all_to_all(jnp.stack([up, down], axis=1), "win", 0, 0)
     trace_grad = backward(returned.reshape(32, GRP, 8, CH), white, inverse, consts)
     correl = unpack_correl(scalars, owned)

time: 221 us -> 203 us (0.919); the launches traced: 217 us -> 202 us
  blocking collectives: 80.4 us -> 65 us
  starting transfers between devices: 19.9 us -> 26.5 us
  waiting for transfers between devices: 69.2 us -> 63.4 us
    all_to_all x1, waiting for transfers between devices: 49.5 us -> 0.01 us  [on_device(): returned = lax.all_to_all(grad.reshape(WINS, 8, CH), ('win', 'grp'), 0, 0)]
    ppermute x1, waiting for transfers between devices: 14.8 us -> 61.3 us  [on_device(): lax.ppermute(corr[1], 'grp', [(i, (i - 3) % GRP) for i in range(GRP)])]
    all_to_all x1 -> x0, blocking collectives: 15.4 us -> none  [on_device(): owned = lax.all_to_all(jnp.stack([up, down], axis=1), 'win', 0, 0)]
    all_to_all x0 -> x1, starting transfers between devices: none -> 7.38 us  [on_device(): owned = lax.all_to_all(jnp.stack([up, down], axis=1), 'win', 0, 0)]
    ppermute x1, waiting for transfers between devices: 2.82 us -> 0.01 us  [on_device(): up = lax.ppermute(corr[0], 'grp', [(i, (i + 1) % GRP) for i in range(GRP)])]
  transfers between devices with their start and end apart: 4 -> 5, of which waited for: 4 -> 2; matrix products, arithmetic and copies ran while one was open for 0% -> 0% of each run, Pallas kernels for 6% -> 11%
where the time goes in v2:
time: 203 us; the launch traced here: 202 us
  blocking collectives  65 us (32%)
  waiting for transfers between devices  63.4 us (31%)
  Pallas kernels  43.4 us (21%)
  starting transfers between devices  26.5 us (13%)
  other arithmetic  2.22 us (1%)
    all_to_all x1, blocking collectives, on_device(): moved = lax.all_to_all(white.reshape(WINS, 8, CH), ('win', 'grp'), 0, 0)  65 us
    ppermute x1, waiting for transfers between devices, on_device(): lax.ppermute(corr[1], 'grp', [(i, (i - 3) % GRP) for i in range(GRP)])  61.3 us
    pallas_call x1, Pallas kernels, middle(): pl.pallas_call(middle_kernel, grid_spec=pltpu.PrefetchScalarGridSpec(num_...  15.6 us
    pallas_call x1, Pallas kernels, backward(): pl.pallas_call(backward_kernel, grid=(SEG // tile,), in_specs=[full((32,...  11.8 us
    pallas_call x1, Pallas kernels, forward(): pl.pallas_call(forward_kernel, grid=(8,), in_specs=[full((CH, SEG)), full...  9.72 us
    all_to_all x1, starting transfers between devices, on_device(): returned = lax.all_to_all(grad.reshape(WINS, 8, CH), ('win', 'grp'), 0, 0)  7.69 us
    all_to_all x1, starting transfers between devices, on_device(): owned = lax.all_to_all(jnp.stack([up, down], axis=1), 'win', 0, 0)  7.38 us
    all_to_all x1, starting transfers between devices, on_device(): seen = lax.all_to_all(packed, 'win', 0, 0)  7.32 us
  transfers between devices with their start and end apart: 5, of which 2 were waited for; matrix products, arithmetic and copies ran while one was open for 0% of the time, Pallas kernels for 11%

profile of v2, /device:TPU:64, one launch (start us, length us, event | category | flops | bytes accessed | tf_op | source)
XLA Modules:
  0.0 202.0 jit_solution(11149506569610686786)
XLA Ops:
  0.7 1.3 pad_add_fusion.sc_ref
  2.0 3.1 %pack_observed.1 = bf16[32,2,4,8,128]{4,3,2,1,0:T(8,128)(2,1)} custom-call(s32[6]{0:T(128)} %pad_add_fusion.sc_ref, f32[3,16,16,2048]{3,2,1,0:T(8,128)} %bitcast.18, f32[3,16,16,2048]{3,2,1,0:T(8,128)} %bitcast.19), custom_call_target="tpu_custom_call" | custom-call | tf_op jit(solution)/shard_map/pack_observed/pallas_call | solution.py:176
  5.1 7.3 %all-to-all-start.1 = ((bf16[32,2,4,8,128]{4,3,2,1,0:T(8,128)(2,1)}), bf16[32,2,4,8,128]{4,3,2,1,0:T(8,128)(2,1)S(1)}, u32[]{:S(2)}, u32[]{:S(2)}) async-start(bf16[32,2,4,8,128]{4,3,2,1,0:T(8,128)(2,1)} %pack_observed.1), calls=%async_computation.1 | async-start | bytes 1048576 | tf_op jit(solution)/shard_map/all_to_all | solution.py:343
  12.4 9.7 %forward.1 = (bf16[32,8,8,512]{3,2,1,0:T(8,128)(2,1)}, f32[8,2,512]{2,1,0:T(2,128)}) custom-call(bf16[512,2048]{1,0:T(8,128)(2,1)} %bitcast.28, f32[128,2048]{1,0:T(8,128)} %constant.38.clone.a_ref, f32[128,2048]{1,0:T(8,128)} %constant.39.clone.b_ref, f32[16,2048]{1,0:T(8,128)} %constant.40.clone.c_ref, f32[16,2048]{1,0:T(8,128)} %constant.41.clone.s_ref), custom_call_target="tpu_custom_call" | custom-call | flops 4294967296 | bytes 8388608 | tf_op jit(solution)/shard_map/forward/pallas_call | solution.py:91
  22.1 2.0 %all-to-all-done.1.obs_ref = bf16[32,2,4,8,128]{4,3,2,1,0:T(8,128)(2,1)S(1)} async-done(((bf16[32,2,4,8,128]{4,3,2,1,0:T(8,128)(2,1)}), bf16[32,2,4,8,128]{4,3,2,1,0:T(8,128)(2,1)S(1)}, u32[]{:S(2)}, u32[]{:S(2)}) %all-to-all-start.1) | async-done | bytes 524320 | tf_op jit(solution)/shard_map/all_to_all | solution.py:343
  24.2 0.0 copy-start.2
  24.2 65.0 %all_to_all.20 = bf16[256,8,512]{2,1,0:T(8,128)(2,1)} all-to-all(bf16[256,8,512]{2,1,0:T(8,128)(2,1)} %bitcast.21), channel_id=1, replica_groups=mesh['win'=32,'grp'=8] {'win','grp'}, dimensions={0} | all-to-all | bytes 4194304 | tf_op jit(solution)/shard_map/all_to_all | solution.py:345
  89.2 0.0 copy-done.2
  89.2 15.6 %middle.1 = (bf16[2,32,4,8,128]{4,3,2,1,0:T(8,128)(2,1)}, bf16[2048,512]{1,0:T(8,128)(2,1)}) custom-call(s32[6]{0:T(128)} %pad_add_fusion.sc_ref, bf16[2048,512]{1,0:T(8,128)(2,1)} %bitcast.20, bf16[32,2,4,8,128]{4,3,2,1,0:T(8,128)(2,1)} %copy-done.2), custom_call_target="tpu_custom_call" | custom-call | tf_op jit(solution)/shard_map/middle/pallas_call | solution.py:279
  104.8 0.0 copy-start.3
  104.8 7.7 %all-to-all-start.2 = ((bf16[256,8,512]{2,1,0:T(8,128)(2,1)}), bf16[256,8,512]{2,1,0:T(8,128)(2,1)S(1)}, u32[]{:S(2)}, u32[]{:S(2)}) async-start(bf16[256,8,512]{2,1,0:T(8,128)(2,1)} %bitcast.23), calls=%async_computation.2 | async-start | bytes 4194304 | tf_op jit(solution)/shard_map/all_to_all | solution.py:349
  112.5 0.0 copy-done.3
  112.6 4.1 %collective-permute-start.1 = (bf16[32,4,8,128]{3,2,1,0:T(8,128)(2,1)S(1)}, bf16[32,4,8,128]{3,2,1,0:T(8,128)(2,1)S(1)}, u32[]{:S(2)}, u32[]{:S(2)}) collective-permute-start(bf16[32,4,8,128]{3,2,1,0:T(8,128)(2,1)S(1)} %get-tuple-element.16), channel_id=1, source_target_pairs={{0,5},{1,6},{2,7},{3,0},{4,1},{5,2},{6,3},{7,4},{8,13},{9,14},{10,... | collective-permute-start | bytes 786440 | tf_op jit(solution)/shard_map/ppermute | solution.py:348
  116.7 0.0 collective-permute-start
  116.7 61.3 %collective-permute-done.1 = bf16[32,4,8,128]{3,2,1,0:T(8,128)(2,1)S(1)} collective-permute-done((bf16[32,4,8,128]{3,2,1,0:T(8,128)(2,1)S(1)}, bf16[32,4,8,128]{3,2,1,0:T(8,128)(2,1)S(1)}, u32[]{:S(2)}, u32[]{:S(2)}) %collective-permute-start.1) | collective-permute-done | bytes 262176 | tf_op jit(solution)/shard_map/ppermute | solution.py:348
  178.0 0.0 collective-permute-done
  178.0 0.0 all-to-all-done.2
  178.0 0.0 copy-start.1
  178.0 0.9 pad_maximum_fusion
  178.9 7.4 %all-to-all-start.3 = ((bf16[32,2,4,8,128]{4,3,2,1,0:T(8,128)(2,1)}), bf16[32,2,4,8,128]{4,3,2,1,0:T(8,128)(2,1)S(1)}, u32[]{:S(2)}, u32[]{:S(2)}) async-start(bf16[32,2,4,8,128]{4,3,2,1,0:T(8,128)(2,1)} %pad_maximum_fusion), calls=%async_computation.3 | async-start | bytes 1048576 | tf_op jit(solution)/shard_map/all_to_all | solution.py:351
  186.3 0.0 copy-done.1
  186.3 11.8 %backward.1 = bf16[512,2048]{1,0:T(8,128)(2,1)} custom-call(bf16[32,8,8,512]{3,2,1,0:T(8,128)(2,1)} %bitcast.22, bf16[32,8,8,512]{3,2,1,0:T(8,128)(2,1)} %get-tuple-element.9.y_ref, f32[8,2,512]{2,1,0:T(2,128)} %get-tuple-element.15.r_ref, f32[128,2048]{1,0:T(8,128)} %constant.38.clone.a_ref, f32[128,2048]{1,0:T(8,128)} %constant.39.clone.b_ref, ...), custom_call_target="tpu_custom_call" | custom-call | flops 4294967296 | bytes 10485760 | tf_op jit(solution)/shard_map/backward/pallas_call | solution.py:134
  198.1 0.0 all-to-all-done.3.x_ref
  198.1 0.0 copy-start
  198.1 0.8 copy-done
  198.9 3.1 %unpack_correl.1 = f32[3,16,16,256]{3,2,1,0:T(8,128)} custom-call(s32[6]{0:T(128)} %pad_add_fusion.sc_ref, bf16[32,2,4,8,128]{4,3,2,1,0:T(8,128)(2,1)} %copy-done), custom_call_target="tpu_custom_call" | custom-call | tf_op jit(solution)/shard_map/unpack_correl/pallas_call | solution.py:320
  (1 shorter events, 0.0 us)
Async XLA Ops:
  5.1 19.1 %all-to-all-start.1 = ((bf16[32,2,4,8,128]{4,3,2,1,0:T(8,128)(2,1)}), bf16[32,2,4,8,128]{4,3,2,1,0:T(8,128)(2,1)S(1)}, u32[]{:S(2)}, u32[]{:S(2)}) async-start(bf16[32,2,4,8,128]{4,3,2,1,0:T(8,128)(2,1)} %pack_observed.1), calls=%async_computation.1 | async-start | bytes 1048576 | tf_op jit(solution)/shard_map/all_to_all | solution.py:343
  24.2 65.0 %copy-start.2 = (bf16[32,2,4,8,128]{4,3,2,1,0:T(8,128)(2,1)}, bf16[32,2,4,8,128]{4,3,2,1,0:T(8,128)(2,1)S(1)}, u32[]{:S(2)}) copy-start(bf16[32,2,4,8,128]{4,3,2,1,0:T(8,128)(2,1)S(1)} %all-to-all-done.1.obs_ref) | copy-start | bytes 1572868
  104.8 7.7 %copy-start.3 = (bf16[2,32,4,8,128]{4,3,2,1,0:T(8,128)(2,1)S(1)}, bf16[2,32,4,8,128]{4,3,2,1,0:T(8,128)(2,1)}, u32[]{:S(2)}) copy-start(bf16[2,32,4,8,128]{4,3,2,1,0:T(8,128)(2,1)} %get-tuple-element.10) | copy-start | bytes 1572868
  104.8 73.2 %all-to-all-start.2 = ((bf16[256,8,512]{2,1,0:T(8,128)(2,1)}), bf16[256,8,512]{2,1,0:T(8,128)(2,1)S(1)}, u32[]{:S(2)}, u32[]{:S(2)}) async-start(bf16[256,8,512]{2,1,0:T(8,128)(2,1)} %bitcast.23), calls=%async_computation.2 | async-start | bytes 4194304 | tf_op jit(solution)/shard_map/all_to_all | solution.py:349
  112.6 65.4 %collective-permute-start.1 = (bf16[32,4,8,128]{3,2,1,0:T(8,128)(2,1)S(1)}, bf16[32,4,8,128]{3,2,1,0:T(8,128)(2,1)S(1)}, u32[]{:S(2)}, u32[]{:S(2)}) collective-permute-start(bf16[32,4,8,128]{3,2,1,0:T(8,128)(2,1)S(1)} %get-tuple-element.16), channel_id=1, source_target_pairs={{0,5},{1,6},{2,7},{3,0},{4,1},{5,2},{6,3},{7,4},{8,13},{9,14},{10,... | collective-permute-start | bytes 786440 | tf_op jit(solution)/shard_map/ppermute | solution.py:348
  116.7 61.4 %collective-permute-start = (bf16[32,4,8,128]{3,2,1,0:T(8,128)(2,1)S(1)}, bf16[32,4,8,128]{3,2,1,0:T(8,128)(2,1)S(1)}, u32[]{:S(2)}, u32[]{:S(2)}) collective-permute-start(bf16[32,4,8,128]{3,2,1,0:T(8,128)(2,1)S(1)} %get-tuple-element.17), channel_id=1, source_target_pairs={{0,1},{1,2},{2,3},{3,4},{4,5},{5,6},{6,7},{7,0},{8,9},{9,10},{10,1... | collective-permute-start | bytes 786440 | tf_op jit(solution)/shard_map/ppermute | solution.py:347
  178.0 8.3 %copy-start.1 = (bf16[256,8,512]{2,1,0:T(8,128)(2,1)}, bf16[256,8,512]{2,1,0:T(8,128)(2,1)S(1)}, u32[]{:S(2)}) copy-start(bf16[256,8,512]{2,1,0:T(8,128)(2,1)S(1)} %all-to-all-done.2) | copy-start | bytes 6291460
  178.9 19.2 %all-to-all-start.3 = ((bf16[32,2,4,8,128]{4,3,2,1,0:T(8,128)(2,1)}), bf16[32,2,4,8,128]{4,3,2,1,0:T(8,128)(2,1)S(1)}, u32[]{:S(2)}, u32[]{:S(2)}) async-start(bf16[32,2,4,8,128]{4,3,2,1,0:T(8,128)(2,1)} %pad_maximum_fusion), calls=%async_computation.3 | async-start | bytes 1048576 | tf_op jit(solution)/shard_map/all_to_all | solution.py:351
  198.1 0.8 copy-start

commit v3 on v2

--- a/solution.py
+++ b/solution.py
@@ -29,15 +29,19 @@
 BF16 = jnp.bfloat16
 
 
-def plane_of(q, h):
-    return (q + 3) % GRP if h == 0 else (q + 7) % GRP
+def half_of(g):
+    return jnp.where(jnp.logical_and(g >= 3, g <= 6), 0, 1)
+
+
+def quarter_of(g):
+    return jnp.where(half_of(g) == 0, g - 3, (g + 1) % GRP)
 
 
 def table_parts():
     row = np.arange(2 * BAND)
-    j = (row // 8) * KB + row % KB
+    j = (row % 64) // 8 * 8 + row % KB * 2 + row // 64
     imag = (row % 8) >= KB
-    n = np.arange(SEG)
+    n = np.arange(SEG // 2)
     ang = 2.0 * math.pi * ((n[None, :] * j[:, None]) % SEG) / SEG
     a = np.where(imag[:, None], -np.sin(ang), np.cos(ang))
     b = np.where(imag[:, None], -np.cos(ang), -np.sin(ang))
@@ -50,110 +54,139 @@
     return lax.dot_general(x, y, (((cx,), (cy,)), ((), ())), preferred_element_type=F32)
 
 
-def regroup(inverse):
-    out = lax.broadcasted_iota(jnp.int32, (256, 256), 0)
-    src = lax.broadcasted_iota(jnp.int32, (256, 256), 1)
-    if inverse:
-        hit = (src % 32) * 8 + src // 32 == out
-    else:
-        hit = (out % 32) * 8 + out // 32 == src
-    return jnp.where(hit, 1.0, 0.0).astype(BF16)
+def regroup(inverse, bins=False):
+    shape = (256, 256)
+    near = lax.broadcasted_iota(jnp.int32, shape, 1 if inverse else 0)
+    far = lax.broadcasted_iota(jnp.int32, shape, 0 if inverse else 1)
+    c = near % 32
+    if bins:
+        c = c // 8 * 8 + c % 2 * KB + c % 8 // 2
+    return jnp.where(c * 8 + near // 32 == far, 1.0, 0.0).astype(BF16)
 
 
 def full(shape):
     return pl.BlockSpec(shape, lambda *i: (0,) * len(shape))
 
 
-def forward_kernel(x_ref, a_ref, b_ref, c_ref, s_ref, y_ref, r_ref):
+def forward_kernel(x_ref, a_ref, b_ref, c_ref, s_ref, y_ref, r_ref, h_ref):
     step = pl.program_id(0)
-    parts = []
-    for wh in range(2):
-        band = step * 2 + wh
-        c = c_ref[pl.ds(band, 1), :]
-        s = s_ref[pl.ds(band, 1), :]
-        parts.append((a_ref[...] * c + b_ref[...] * s).astype(BF16))
-    table = jnp.concatenate(parts, axis=0)
-    spec = dot(table, x_ref[...], 1, 1)
-    for wh in range(2):
-        rows = spec[wh * 128 : (wh + 1) * 128]
-        level = jnp.sum(rows * rows, axis=0, keepdims=True) * (1.0 / BAND) + 1e-05
-        inv = lax.rsqrt(level)
-        r_ref[0, wh : wh + 1, :] = inv
-        y_ref[wh * 16 : (wh + 1) * 16, 0] = (rows * inv).reshape(16, 8, CH).astype(BF16)
-
-
-def plane_index(step):
-    q, h = step // 2, step % 2
-    return jnp.where(h == 0, q + 3, (q + 7) % GRP)
+
+    @pl.when(step == 0)
+    def _():
+        early = x_ref[:, : SEG // 2].astype(F32)
+        late = x_ref[:, SEG // 2 :].astype(F32)
+        h_ref[0] = (early + late).astype(BF16)
+        h_ref[1] = (early - late).astype(BF16)
+
+    waves = []
+    for p in range(2):
+        a = a_ref[p * 64 : (p + 1) * 64]
+        b = b_ref[p * 64 : (p + 1) * 64]
+        parts = []
+        for gi in range(2):
+            g = step * 2 + gi
+            for wh in range(2):
+                band = quarter_of(g) * 4 + half_of(g) * 2 + wh
+                parts.append((a * c_ref[pl.ds(band, 1), :] + b * s_ref[pl.ds(band, 1), :]).astype(BF16))
+        waves.append(dot(jnp.concatenate(parts, axis=0), h_ref[p], 1, 1))
+    for gi in range(2):
+        for wh in range(2):
+            row = (gi * 2 + wh) * 64
+            rows = [w[row : row + 64] for w in waves]
+            level = jnp.sum(rows[0] * rows[0] + rows[1] * rows[1], axis=0, keepdims=True)
+            inv = lax.rsqrt(level * (1.0 / BAND) + 1e-05)
+            r_ref[gi, wh : wh + 1, :] = inv
+            for p in range(2):
+                y_ref[wh * 8 : (wh + 1) * 8, p, gi] = (rows[p] * inv).reshape(8, 8, CH).astype(BF16)
 
 
 def forward(x, consts):
     return pl.pallas_call(
         forward_kernel,
-        grid=(8,),
-        in_specs=[full((CH, SEG)), full((128, SEG)), full((128, SEG)), full((16, SEG)), full((16, SEG))],
+        grid=(4,),
+        in_specs=[full((CH, SEG)), full((128, SEG // 2)), full((128, SEG // 2)), full((16, SEG // 2)), full((16, SEG // 2))],
         out_specs=[
-            pl.BlockSpec((32, 1, 8, CH), lambda i: (0, plane_index(i), 0, 0)),
-            pl.BlockSpec((1, 2, CH), lambda i: (i, 0, 0)),
+            pl.BlockSpec((16, 2, 2, 8, CH), lambda i: (0, 0, i, 0, 0)),
+            pl.BlockSpec((2, 2, CH), lambda i: (i, 0, 0)),
         ],
         out_shape=[
-            jax.ShapeDtypeStruct((32, GRP, 8, CH), BF16),
-            jax.ShapeDtypeStruct((8, 2, CH), F32),
+            jax.ShapeDtypeStruct((16, 2, GRP, 8, CH), BF16),
+            jax.ShapeDtypeStruct((GRP, 2, CH), F32),
         ],
-        compiler_params=pltpu.CompilerParams(vmem_limit_bytes=VMEM_LIMIT),
-        cost_estimate=pl.CostEstimate(flops=2 * CH * SEG * SEG, bytes_accessed=8 << 20, transcendentals=0),
+        scratch_shapes=[pltpu.VMEM((2, CH, SEG // 2), BF16)],
+        compiler_params=pltpu.CompilerParams(vmem_limit_bytes=VMEM_LIMIT),
+        cost_estimate=pl.CostEstimate(flops=CH * SEG * SEG, bytes_accessed=8 << 20, transcendentals=0),
         name="forward",
     )(x, *consts)
 
 
-def backward_kernel(g_ref, y_ref, r_ref, a_ref, b_ref, c_ref, s_ref, o_ref, d_ref):
-    @pl.when(pl.program_id(0) == 0)
+def backward_kernel(g_ref, y_ref, r_ref, a_ref, b_ref, c_ref, s_ref, o_ref, d_ref, late_ref):
+    step = pl.program_id(0)
+
+    @pl.when(step == 0)
     def _():
-        for step in range(8):
-            plane = plane_of(step // 2, step % 2)
+        for plane in range(GRP):
+            sides = ([], [])
             for wh in range(2):
-                g = g_ref[wh * 16 : (wh + 1) * 16, plane].astype(F32).reshape(128, CH)
-                y = y_ref[wh * 16 : (wh + 1) * 16, plane].astype(F32).reshape(128, CH)
-                mean = jnp.sum(g * y, axis=0, keepdims=True) * (1.0 / BAND)
-                d = (g - y * mean) * r_ref[step, wh : wh + 1, :]
-                row = (step * 2 + wh) * 128
-                d_ref[:, row : row + 128] = d.T.astype(BF16)
-
-    parts = []
-    for band in range(16):
-        c = c_ref[band : band + 1, :]
-        s = s_ref[band : band + 1, :]
-        parts.append((a_ref[...] * c + b_ref[...] * s).astype(BF16))
-    table = jnp.concatenate(parts, axis=0)
-    o_ref[...] = dot(d_ref[...], table).astype(BF16)
+                at = slice(wh * 8, (wh + 1) * 8)
+                g = [g_ref[at, p, plane].astype(F32).reshape(64, CH) for p in range(2)]
+                y = [y_ref[at, p, plane].astype(F32).reshape(64, CH) for p in range(2)]
+                inv = r_ref[plane, wh : wh + 1, :]
+                mean = jnp.sum(g[0] * y[0] + g[1] * y[1], axis=0, keepdims=True) * (1.0 / BAND)
+                for p in range(2):
+                    sides[p].append((g[p] - y[p] * mean) * inv)
+            for p in range(2):
+                turned = jnp.concatenate(sides[p], axis=0).T
+                d_ref[p, :, plane * 128 : (plane + 1) * 128] = turned.astype(BF16)
+
+    @pl.when(step % 2 == 0)
+    def _():
+        waves = []
+        for p in range(2):
+            a = a_ref[p * 64 : (p + 1) * 64]
+            b = b_ref[p * 64 : (p + 1) * 64]
+            parts = []
+            for plane in range(GRP):
+                h = 0 if 3 <= plane <= 6 else 1
+                q = plane - 3 if h == 0 else (plane + 1) % GRP
+                for band in (q * 4 + h * 2, q * 4 + h * 2 + 1):
+                    parts.append((a * c_ref[band : band + 1, :] + b * s_ref[band : band + 1, :]).astype(BF16))
+            waves.append(dot(d_ref[p], jnp.concatenate(parts, axis=0)))
+        o_ref[...] = (waves[0] + waves[1]).astype(BF16)
+        late_ref[...] = (waves[0] - waves[1]).astype(BF16)
+
+    @pl.when(step % 2 == 1)
+    def _():
+        o_ref[...] = late_ref[...]
 
 
 def backward(g, y, r, consts):
     tile = 256
-    col = lambda rows: pl.BlockSpec((rows, tile), lambda i: (0, i))
+    tiles = SEG // 2 // tile
+    col = lambda rows: pl.BlockSpec((rows, tile), lambda i: (0, i // 2))
     return pl.pallas_call(
         backward_kernel,
-        grid=(SEG // tile,),
+        grid=(2 * tiles,),
         in_specs=[
-            full((32, GRP, 8, CH)),
-            full((32, GRP, 8, CH)),
-            full((8, 2, CH)),
+            full((16, 2, GRP, 8, CH)),
+            full((16, 2, GRP, 8, CH)),
+            full((GRP, 2, CH)),
             col(128),
             col(128),
             col(16),
             col(16),
         ],
-        out_specs=pl.BlockSpec((CH, tile), lambda i: (0, i)),
+        out_specs=pl.BlockSpec((CH, tile), lambda i: (0, i // 2 + i % 2 * tiles)),
         out_shape=jax.ShapeDtypeStruct((CH, SEG), BF16),
-        scratch_shapes=[pltpu.VMEM((CH, SEG), BF16)],
-        compiler_params=pltpu.CompilerParams(vmem_limit_bytes=VMEM_LIMIT),
-        cost_estimate=pl.CostEstimate(flops=2 * CH * SEG * SEG, bytes_accessed=10 << 20, transcendentals=0),
+        scratch_shapes=[pltpu.VMEM((2, CH, SEG // 2), BF16), pltpu.VMEM((CH, tile), BF16)],
+        compiler_params=pltpu.CompilerParams(vmem_limit_bytes=VMEM_LIMIT),
+        cost_estimate=pl.CostEstimate(flops=CH * SEG * SEG, bytes_accessed=10 << 20, transcendentals=0),
         name="backward",
     )(g, y, r, *consts)
 
 
 def pack_kernel(sc_ref, re_ref, im_ref, o_ref):
-    perm = regroup(True)
+    perm = regroup(True, True)
     for ri, src in enumerate((re_ref, im_ref)):
         turned = []
         for i in range(8):
@@ -295,7 +328,7 @@
 
 
 def unpack_kernel(sc_ref, x_ref, o_ref):
-    perm = regroup(False)
+    perm = regroup(False, True)
     for h in range(2):
         first = sc_ref[5]
         index = first if h == 0 else 1 - first
@@ -334,8 +367,7 @@
 def on_device(traces, pair_lists, observed):
     consts = [jnp.asarray(v) for v in table_parts()]
     g = lax.axis_index("grp")
-    half = jnp.where(jnp.logical_and(g >= 3, g <= 6), 0, 1)
-    q = jnp.where(half == 0, g - 3, (g + 1) % GRP)
+    half, q = half_of(g), quarter_of(g)
     low = jnp.where(g < 4, 1, 0)
     scalars = jnp.concatenate([pair_lists[0], jnp.stack([2 * q + half, half, low]).astype(jnp.int32)])
 
@@ -349,7 +381,7 @@
     returned = lax.all_to_all(grad.reshape(WINS, 8, CH), ("win", "grp"), 0, 0)
     up, down, returned = lax.optimization_barrier((up, down, returned))
     owned = lax.all_to_all(jnp.stack([up, down], axis=1), "win", 0, 0)
-    trace_grad = backward(returned.reshape(32, GRP, 8, CH), white, inverse, consts)
+    trace_grad = backward(returned.reshape(16, 2, GRP, 8, CH), white, inverse, consts)
     correl = unpack_correl(scalars, owned)
     return correl[None], trace_grad[None]
 

time: 203 us -> 201 us (level)
  waiting for transfers between devices: 63.4 us -> 66.4 us
  Pallas kernels: 43.4 us -> 40.4 us
    pallas_call x2, Pallas kernels: 21.5 us -> 18.5 us  [the longest x1 11.8 us: backward(): pl.pallas_call(backward_kernel, grid=(2 * tiles,), in_specs=[full((16, 2,...]
    all_to_all x1, waiting for transfers between devices: 2.04 us -> 5.07 us  [on_device(): seen = lax.all_to_all(packed, 'win', 0, 0)]
  transfers between devices with their start and end apart: 5 -> 5, of which waited for: 2 -> 2; matrix products, arithmetic and copies ran while one was open for 0% -> 0% of each run, Pallas kernels for 11% -> 9%
where the time goes in v3:
time: 201 us; the launch traced here: 200 us
  waiting for transfers between devices  66.4 us (33%)
  blocking collectives  63.3 us (31%)
  Pallas kernels  40.4 us (20%)
  starting transfers between devices  26.5 us (13%)
  other arithmetic  2.22 us (1%)
    all_to_all x1, blocking collectives, on_device(): moved = lax.all_to_all(white.reshape(WINS, 8, CH), ('win', 'grp'), 0, 0)  63.3 us
    ppermute x1, waiting for transfers between devices, on_device(): lax.ppermute(corr[1], 'grp', [(i, (i - 3) % GRP) for i in range(GRP)])  61.3 us
    pallas_call x1, Pallas kernels, middle(): pl.pallas_call(middle_kernel, grid_spec=pltpu.PrefetchScalarGridSpec(num_...  15.6 us
    pallas_call x1, Pallas kernels, backward(): pl.pallas_call(backward_kernel, grid=(2 * tiles,), in_specs=[full((16, 2,...  11.8 us
    all_to_all x1, starting transfers between devices, on_device(): returned = lax.all_to_all(grad.reshape(WINS, 8, CH), ('win', 'grp'), 0, 0)  7.69 us
    all_to_all x1, starting transfers between devices, on_device(): owned = lax.all_to_all(jnp.stack([up, down], axis=1), 'win', 0, 0)  7.38 us
    all_to_all x1, starting transfers between devices, on_device(): seen = lax.all_to_all(packed, 'win', 0, 0)  7.32 us
    pallas_call x1, Pallas kernels, forward(): pl.pallas_call(forward_kernel, grid=(4,), in_specs=[full((CH, SEG)), full...  6.69 us
  transfers between devices with their start and end apart: 5, of which 2 were waited for; matrix products, arithmetic and copies ran while one was open for 0% of the time, Pallas kernels for 9%

profile of v3, /device:TPU:64, one launch (start us, length us, event | category | flops | bytes accessed | tf_op | source)
XLA Modules:
  0.0 200.4 jit_solution(16203594904268574461)
XLA Ops:
  0.7 1.3 pad_add_fusion.sc_ref
  2.0 3.1 %pack_observed.1 = bf16[32,2,4,8,128]{4,3,2,1,0:T(8,128)(2,1)} custom-call(s32[6]{0:T(128)} %pad_add_fusion.sc_ref, f32[3,16,16,2048]{3,2,1,0:T(8,128)} %bitcast.18, f32[3,16,16,2048]{3,2,1,0:T(8,128)} %bitcast.19), custom_call_target="tpu_custom_call" | custom-call | tf_op jit(solution)/shard_map/pack_observed/pallas_call | solution.py:209
  5.1 7.3 %all-to-all-start.1 = ((bf16[32,2,4,8,128]{4,3,2,1,0:T(8,128)(2,1)}), bf16[32,2,4,8,128]{4,3,2,1,0:T(8,128)(2,1)S(1)}, u32[]{:S(2)}, u32[]{:S(2)}) async-start(bf16[32,2,4,8,128]{4,3,2,1,0:T(8,128)(2,1)} %pack_observed.1), calls=%async_computation.1 | async-start | bytes 1048576 | tf_op jit(solution)/shard_map/all_to_all | solution.py:375
  12.4 6.7 %forward.1 = (bf16[16,2,8,8,512]{4,3,2,1,0:T(8,128)(2,1)}, f32[8,2,512]{2,1,0:T(2,128)}) custom-call(bf16[512,2048]{1,0:T(8,128)(2,1)} %bitcast.28, f32[128,1024]{1,0:T(8,128)} %constant.38.clone.a_ref, f32[128,1024]{1,0:T(8,128)} %constant.39.clone.b_ref, f32[16,1024]{1,0:T(8,128)} %constant.40.clone.c_ref, f32[16,1024]{1,0:T(8,128)} %constant.41.clone.s_ref), custom_call_target="tpu_custom_call" | custom-call | flops 2147483648 | bytes 8388608 | tf_op jit(solution)/shard_map/forward/pallas_call | solution.py:104
  19.1 5.1 %all-to-all-done.1.obs_ref = bf16[32,2,4,8,128]{4,3,2,1,0:T(8,128)(2,1)S(1)} async-done(((bf16[32,2,4,8,128]{4,3,2,1,0:T(8,128)(2,1)}), bf16[32,2,4,8,128]{4,3,2,1,0:T(8,128)(2,1)S(1)}, u32[]{:S(2)}, u32[]{:S(2)}) %all-to-all-start.1) | async-done | bytes 524320 | tf_op jit(solution)/shard_map/all_to_all | solution.py:375
  24.2 0.0 copy-start.2
  24.2 63.3 %all_to_all.20 = bf16[256,8,512]{2,1,0:T(8,128)(2,1)} all-to-all(bf16[256,8,512]{2,1,0:T(8,128)(2,1)} %bitcast.21), channel_id=1, replica_groups=mesh['win'=32,'grp'=8] {'win','grp'}, dimensions={0} | all-to-all | bytes 4194304 | tf_op jit(solution)/shard_map/all_to_all | solution.py:377
  87.5 0.0 copy-done.2
  87.5 15.6 %middle.1 = (bf16[2,32,4,8,128]{4,3,2,1,0:T(8,128)(2,1)}, bf16[2048,512]{1,0:T(8,128)(2,1)}) custom-call(s32[6]{0:T(128)} %pad_add_fusion.sc_ref, bf16[2048,512]{1,0:T(8,128)(2,1)} %bitcast.20, bf16[32,2,4,8,128]{4,3,2,1,0:T(8,128)(2,1)} %copy-done.2), custom_call_target="tpu_custom_call" | custom-call | tf_op jit(solution)/shard_map/middle/pallas_call | solution.py:312
  103.1 0.0 copy-start.3
  103.1 7.7 %all-to-all-start.2 = ((bf16[256,8,512]{2,1,0:T(8,128)(2,1)}), bf16[256,8,512]{2,1,0:T(8,128)(2,1)S(1)}, u32[]{:S(2)}, u32[]{:S(2)}) async-start(bf16[256,8,512]{2,1,0:T(8,128)(2,1)} %bitcast.23), calls=%async_computation.2 | async-start | bytes 4194304 | tf_op jit(solution)/shard_map/all_to_all | solution.py:381
  110.8 0.0 copy-done.3
  110.9 4.1 %collective-permute-start.1 = (bf16[32,4,8,128]{3,2,1,0:T(8,128)(2,1)S(1)}, bf16[32,4,8,128]{3,2,1,0:T(8,128)(2,1)S(1)}, u32[]{:S(2)}, u32[]{:S(2)}) collective-permute-start(bf16[32,4,8,128]{3,2,1,0:T(8,128)(2,1)S(1)} %get-tuple-element.16), channel_id=1, source_target_pairs={{0,5},{1,6},{2,7},{3,0},{4,1},{5,2},{6,3},{7,4},{8,13},{9,14},{10,... | collective-permute-start | bytes 786440 | tf_op jit(solution)/shard_map/ppermute | solution.py:380
  115.0 0.0 collective-permute-start
  115.0 61.3 %collective-permute-done.1 = bf16[32,4,8,128]{3,2,1,0:T(8,128)(2,1)S(1)} collective-permute-done((bf16[32,4,8,128]{3,2,1,0:T(8,128)(2,1)S(1)}, bf16[32,4,8,128]{3,2,1,0:T(8,128)(2,1)S(1)}, u32[]{:S(2)}, u32[]{:S(2)}) %collective-permute-start.1) | collective-permute-done | bytes 262176 | tf_op jit(solution)/shard_map/ppermute | solution.py:380
  176.3 0.0 collective-permute-done
  176.3 0.0 all-to-all-done.2
  176.3 0.0 copy-start.1
  176.3 0.9 pad_maximum_fusion
  177.2 7.4 %all-to-all-start.3 = ((bf16[32,2,4,8,128]{4,3,2,1,0:T(8,128)(2,1)}), bf16[32,2,4,8,128]{4,3,2,1,0:T(8,128)(2,1)S(1)}, u32[]{:S(2)}, u32[]{:S(2)}) async-start(bf16[32,2,4,8,128]{4,3,2,1,0:T(8,128)(2,1)} %pad_maximum_fusion), calls=%async_computation.3 | async-start | bytes 1048576 | tf_op jit(solution)/shard_map/all_to_all | solution.py:383
  184.6 0.0 copy-done.1
  184.7 11.8 %backward.1 = bf16[512,2048]{1,0:T(8,128)(2,1)} custom-call(bf16[16,2,8,8,512]{4,3,2,1,0:T(8,128)(2,1)} %bitcast.22, bf16[16,2,8,8,512]{4,3,2,1,0:T(8,128)(2,1)} %get-tuple-element.9.y_ref, f32[8,2,512]{2,1,0:T(2,128)} %get-tuple-element.15.r_ref, f32[128,1024]{1,0:T(8,128)} %constant.38.clone.a_ref, f32[128,1024]{1,0:T(8,128)} %constant.39.clone.b_ref, ...), custom_call_target="tpu_custom_call" | custom-call | flops 2147483648 | bytes 10485760 | tf_op jit(solution)/shard_map/backward/pallas_call | solution.py:167
  196.4 0.0 all-to-all-done.3.x_ref
  196.4 0.0 copy-start
  196.4 0.8 copy-done
  197.2 3.2 %unpack_correl.1 = f32[3,16,16,256]{3,2,1,0:T(8,128)} custom-call(s32[6]{0:T(128)} %pad_add_fusion.sc_ref, bf16[32,2,4,8,128]{4,3,2,1,0:T(8,128)(2,1)} %copy-done), custom_call_target="tpu_custom_call" | custom-call | tf_op jit(solution)/shard_map/unpack_correl/pallas_call | solution.py:353
  (1 shorter events, 0.0 us)
Async XLA Ops:
  5.1 19.1 %all-to-all-start.1 = ((bf16[32,2,4,8,128]{4,3,2,1,0:T(8,128)(2,1)}), bf16[32,2,4,8,128]{4,3,2,1,0:T(8,128)(2,1)S(1)}, u32[]{:S(2)}, u32[]{:S(2)}) async-start(bf16[32,2,4,8,128]{4,3,2,1,0:T(8,128)(2,1)} %pack_observed.1), calls=%async_computation.1 | async-start | bytes 1048576 | tf_op jit(solution)/shard_map/all_to_all | solution.py:375
  24.2 63.3 %copy-start.2 = (bf16[32,2,4,8,128]{4,3,2,1,0:T(8,128)(2,1)}, bf16[32,2,4,8,128]{4,3,2,1,0:T(8,128)(2,1)S(1)}, u32[]{:S(2)}) copy-start(bf16[32,2,4,8,128]{4,3,2,1,0:T(8,128)(2,1)S(1)} %all-to-all-done.1.obs_ref) | copy-start | bytes 1572868
  103.1 7.7 %copy-start.3 = (bf16[2,32,4,8,128]{4,3,2,1,0:T(8,128)(2,1)S(1)}, bf16[2,32,4,8,128]{4,3,2,1,0:T(8,128)(2,1)}, u32[]{:S(2)}) copy-start(bf16[2,32,4,8,128]{4,3,2,1,0:T(8,128)(2,1)} %get-tuple-element.10) | copy-start | bytes 1572868
  103.1 73.2 %all-to-all-start.2 = ((bf16[256,8,512]{2,1,0:T(8,128)(2,1)}), bf16[256,8,512]{2,1,0:T(8,128)(2,1)S(1)}, u32[]{:S(2)}, u32[]{:S(2)}) async-start(bf16[256,8,512]{2,1,0:T(8,128)(2,1)} %bitcast.23), calls=%async_computation.2 | async-start | bytes 4194304 | tf_op jit(solution)/shard_map/all_to_all | solution.py:381
  110.9 65.4 %collective-permute-start.1 = (bf16[32,4,8,128]{3,2,1,0:T(8,128)(2,1)S(1)}, bf16[32,4,8,128]{3,2,1,0:T(8,128)(2,1)S(1)}, u32[]{:S(2)}, u32[]{:S(2)}) collective-permute-start(bf16[32,4,8,128]{3,2,1,0:T(8,128)(2,1)S(1)} %get-tuple-element.16), channel_id=1, source_target_pairs={{0,5},{1,6},{2,7},{3,0},{4,1},{5,2},{6,3},{7,4},{8,13},{9,14},{10,... | collective-permute-start | bytes 786440 | tf_op jit(solution)/shard_map/ppermute | solution.py:380
  115.0 61.4 %collective-permute-start = (bf16[32,4,8,128]{3,2,1,0:T(8,128)(2,1)S(1)}, bf16[32,4,8,128]{3,2,1,0:T(8,128)(2,1)S(1)}, u32[]{:S(2)}, u32[]{:S(2)}) collective-permute-start(bf16[32,4,8,128]{3,2,1,0:T(8,128)(2,1)S(1)} %get-tuple-element.17), channel_id=1, source_target_pairs={{0,1},{1,2},{2,3},{3,4},{4,5},{5,6},{6,7},{7,0},{8,9},{9,10},{10,1... | collective-permute-start | bytes 786440 | tf_op jit(solution)/shard_map/ppermute | solution.py:379
  176.3 8.3 %copy-start.1 = (bf16[256,8,512]{2,1,0:T(8,128)(2,1)}, bf16[256,8,512]{2,1,0:T(8,128)(2,1)S(1)}, u32[]{:S(2)}) copy-start(bf16[256,8,512]{2,1,0:T(8,128)(2,1)S(1)} %all-to-all-done.2) | copy-start | bytes 6291460
  177.2 19.2 %all-to-all-start.3 = ((bf16[32,2,4,8,128]{4,3,2,1,0:T(8,128)(2,1)}), bf16[32,2,4,8,128]{4,3,2,1,0:T(8,128)(2,1)S(1)}, u32[]{:S(2)}, u32[]{:S(2)}) async-start(bf16[32,2,4,8,128]{4,3,2,1,0:T(8,128)(2,1)} %pad_maximum_fusion), calls=%async_computation.3 | async-start | bytes 1048576 | tf_op jit(solution)/shard_map/all_to_all | solution.py:383
  196.4 0.8 copy-start

commit v4 on v3

--- a/solution.py
+++ b/solution.py
@@ -48,6 +48,34 @@
     band = np.arange(FREQ // BAND)
     bang = 2.0 * math.pi * ((n[None, :] * (BAND * band[:, None])) % SEG) / SEG
     return [np.asarray(v, np.float32) for v in (a, b, np.cos(bang), np.sin(bang))]
+
+
+NSC = 7
+
+
+def target_slot(me, w):
+    return ((me + w) % 2) * 16 + ((w // 2 - me // 2 + 4) % 4) * 4 + (w // 8 - me // 8 + 4) % 4
+
+
+def source_slot(me, w):
+    return ((me // 8 - w // 8 + 4) % 4) * 8 + ((me // 2 - w // 2 + 4) % 4) * 2 + (me + w) % 2
+
+
+def exchange(blocks):
+    def hop(array, dy, dx, dc):
+        pairs = []
+        for w in range(NB):
+            y, x, c = w // 8, w // 2 % 4, w % 2
+            pairs.append((w, ((y + dy) % 4 * 4 + (x + dx) % 4) * 2 + (c + dc) % 2))
+        return lax.ppermute(array, "win", pairs)
+
+    blocks = blocks.reshape((2, 4, 4) + blocks.shape[1:])
+    blocks = jnp.stack([blocks[0], hop(blocks[1], 0, 0, 1)])
+    along_x = [blocks[:, 0]] + [hop(blocks[:, d], 0, d, 0) for d in range(1, 4)]
+    blocks = jnp.stack(along_x)
+    along_y = [blocks[:, :, 0]] + [hop(blocks[:, :, d], d, 0, 0) for d in range(1, 4)]
+    blocks = jnp.stack(along_y)
+    return blocks.reshape((NB,) + blocks.shape[3:])
 
 
 def dot(x, y, cx=1, cy=0):
@@ -201,7 +229,8 @@
         for gr in range(4):
             stack = jnp.concatenate([t[gr * 32 : (gr + 1) * 32] for t in turned], axis=0)
             tile = dot(perm, stack).reshape(8, KB, 8, LANES)
-            o_ref[gr * 8 : (gr + 1) * 8, ri] = tile.astype(BF16)
+            for j in range(8):
+                o_ref[target_slot(sc_ref[6], gr * 8 + j), ri] = tile[j].astype(BF16)
 
 
 def pack_observed(scalars, observed):
@@ -221,7 +250,7 @@
 
 
 def middle_kernel(sc_ref, x_ref, obs_ref, corr_ref, out_ref, u_ref, d_ref):
-    half = sc_ref[4]
+    half, me = sc_ref[4], sc_ref[6]
     perm = regroup(False)
     for gr in range(8):
         y = dot(perm, x_ref[gr * 256 : (gr + 1) * 256, :]).astype(BF16)
@@ -257,10 +286,10 @@
                         here = pltpu.roll(here, LANES - shift, 1)
                     packed = jnp.where(lane8 < HALF, here[:8], pltpu.roll(here[8:], HALF, 1))
                     packed = packed * (1.0 / WINS)
-                    seen = obs_ref[a, ri, k].astype(F32)
+                    seen = obs_ref[source_slot(me, a), ri, k].astype(F32)
                     live = seen < EMPTY / 2
                     slot = 1 - half if ri == 0 else half
-                    corr_ref[slot, a, k] = packed.astype(BF16)
+                    corr_ref[target_slot(me, a), slot, k] = packed.astype(BF16)
                     resid = jnp.where(live, packed - seen, 0.0)
                     spread = jnp.concatenate([resid, pltpu.roll(resid, HALF, 1)], axis=0)
                     spread = jnp.where(lane16 < HALF, spread, 0.0)
@@ -315,11 +344,11 @@
             num_scalar_prefetch=1,
             grid=(1,),
             in_specs=[block((2048, CH)), block((NB, 2, KB, 8, LANES))],
-            out_specs=[block((2, NB, KB, 8, LANES)), block((2048, CH))],
+            out_specs=[block((NB, 2, KB, 8, LANES)), block((2048, CH))],
             scratch_shapes=[pltpu.VMEM((KB, 2 * WINS, CH), BF16), pltpu.VMEM((KB, 2 * WINS, CH), BF16)],
         ),
         out_shape=[
-            jax.ShapeDtypeStruct((2, NB, KB, 8, LANES), BF16),
+            jax.ShapeDtypeStruct((NB, 2, KB, 8, LANES), BF16),
             jax.ShapeDtypeStruct((2048, CH), BF16),
         ],
         compiler_params=pltpu.CompilerParams(vmem_limit_bytes=VMEM_LIMIT),
@@ -327,17 +356,20 @@
     )(scalars, x, obs)
 
 
-def unpack_kernel(sc_ref, x_ref, o_ref):
+def unpack_kernel(sc_ref, up_ref, down_ref, o_ref):
     perm = regroup(False, True)
+    low, me = sc_ref[5], sc_ref[6]
+    regrouped = ([], [])
+    for gr in range(4):
+        sides = []
+        for ref in (up_ref, down_ref):
+            rows = [ref[source_slot(me, gr * 8 + j)].astype(F32).reshape(32, LANES) for j in range(8)]
+            sides.append(jnp.concatenate(rows, axis=0))
+        regrouped[0].append(dot(perm, jnp.where(low == 1, sides[1], sides[0]).astype(BF16)))
+        regrouped[1].append(dot(perm, jnp.where(low == 1, sides[0], sides[1]).astype(BF16)))
     for h in range(2):
-        first = sc_ref[5]
-        index = first if h == 0 else 1 - first
-        regrouped = []
-        for gr in range(4):
-            rows = x_ref[gr * 8 : (gr + 1) * 8, index].astype(F32).reshape(256, LANES).astype(BF16)
-            regrouped.append(dot(perm, rows))
         for i in range(8):
-            page = jnp.concatenate([r[i * 32 : (i + 1) * 32] for r in regrouped], axis=0)
+            page = jnp.concatenate([r[i * 32 : (i + 1) * 32] for r in regrouped[h]], axis=0)
             turned = page.T
             for ih in range(2):
                 for s in range(SLOTS):
@@ -348,20 +380,20 @@
                     o_ref[s, ih * 8 + i, :, h * LANES : (h + 1) * LANES] = val
 
 
-def unpack_correl(scalars, x):
+def unpack_correl(scalars, up, down):
     block = lambda shape: pl.BlockSpec(shape, lambda i, sc: (0,) * len(shape))
     return pl.pallas_call(
         unpack_kernel,
         grid_spec=pltpu.PrefetchScalarGridSpec(
             num_scalar_prefetch=1,
             grid=(1,),
-            in_specs=[block((32, 2, KB, 8, LANES))],
+            in_specs=[block((NB, KB, 8, LANES))] * 2,
             out_specs=block((SLOTS, CB, CB, 2 * LANES)),
         ),
         out_shape=jax.ShapeDtypeStruct((SLOTS, CB, CB, 2 * LANES), F32),
         compiler_params=pltpu.CompilerParams(vmem_limit_bytes=VMEM_LIMIT),
         name="unpack_correl",
-    )(scalars, x)
+    )(scalars, up, down)
 
 
 def on_device(traces, pair_lists, observed):
@@ -369,20 +401,20 @@
     g = lax.axis_index("grp")
     half, q = half_of(g), quarter_of(g)
     low = jnp.where(g < 4, 1, 0)
-    scalars = jnp.concatenate([pair_lists[0], jnp.stack([2 * q + half, half, low]).astype(jnp.int32)])
-
-    packed = pack_observed(scalars, observed[0])
-    seen = lax.all_to_all(packed, "win", 0, 0)
+    me = lax.axis_index("win")
+    scalars = jnp.concatenate([pair_lists[0], jnp.stack([2 * q + half, half, low, me]).astype(jnp.int32)])
+
     white, inverse = forward(traces[0], consts)
+    white, scalars = lax.optimization_barrier((white, scalars))
     moved = lax.all_to_all(white.reshape(WINS, 8, CH), ("win", "grp"), 0, 0)
+    seen = exchange(pack_observed(scalars, observed[0]))
     corr, grad = middle(scalars, moved.reshape(2048, CH), seen)
-    up = lax.ppermute(corr[0], "grp", [(i, (i + 1) % GRP) for i in range(GRP)])
-    down = lax.ppermute(corr[1], "grp", [(i, (i - 3) % GRP) for i in range(GRP)])
     returned = lax.all_to_all(grad.reshape(WINS, 8, CH), ("win", "grp"), 0, 0)
-    up, down, returned = lax.optimization_barrier((up, down, returned))
-    owned = lax.all_to_all(jnp.stack([up, down], axis=1), "win", 0, 0)
+    corr = exchange(corr)
+    up = lax.ppermute(corr[:, 0], "grp", [(i, (i + 1) % GRP) for i in range(GRP)])
+    down = lax.ppermute(corr[:, 1], "grp", [(i, (i - 3) % GRP) for i in range(GRP)])
     trace_grad = backward(returned.reshape(16, 2, GRP, 8, CH), white, inverse, consts)
-    correl = unpack_correl(scalars, owned)
+    correl = unpack_correl(scalars, up, down)
     return correl[None], trace_grad[None]
 
 

time: 201 us -> 184 us (0.915)
  blocking collectives: 63.3 us -> 0 us
  waiting for transfers between devices: 66.4 us -> 88 us
  starting transfers between devices: 26.5 us -> 46.4 us
  local copies, waits for them, and re-layouts: 0.84 us -> 6.53 us
    all_to_all x1 -> x0, blocking collectives: 63.3 us -> none  [on_device(): moved = lax.all_to_all(white.reshape(WINS, 8, CH), ('win', 'grp'), 0, 0)]
    ppermute x2 -> x16, starting transfers between devices: 4.1 us -> 24.4 us  [the longest x14 19.9 us: hop(): return lax.ppermute(array, 'win', pairs)]
    ppermute x2 -> x16, waiting for transfers between devices: 61.3 us -> 72.6 us  [the longest x14 44.9 us: hop(): return lax.ppermute(array, 'win', pairs)]
    all_to_all x2 -> x1, waiting for transfers between devices: 5.07 us -> 15.4 us  [on_device(): moved = lax.all_to_all(white.reshape(WINS, 8, CH), ('win', 'grp'), 0, 0)]
    unnamed x8 -> x10, local copies, waits for them, and re-layouts: 0.8 us -> 4.04 us
    all_to_all x2 -> x1, starting transfers between devices: 14.7 us -> 14.2 us  [on_device(): moved = lax.all_to_all(white.reshape(WINS, 8, CH), ('win', 'grp'), 0, 0)]
  transfers between devices with their start and end apart: 5 -> 18, of which waited for: 2 -> 16; matrix products, arithmetic and copies ran while one was open for 0% -> 1% of each run, Pallas kernels for 9% -> 4%
where the time goes in v4:
time: 184 us
  waiting for transfers between devices  88 us (48%)
  starting transfers between devices  46.4 us (25%)
  Pallas kernels  40.7 us (22%)
  local copies, waits for them, and re-layouts  6.53 us (4%)
    ppermute x14, waiting for transfers between devices, hop(): return lax.ppermute(array, 'win', pairs)  44.9 us
    ppermute x1, waiting for transfers between devices, on_device(): lax.ppermute(corr[:, 1], 'grp', [(i, (i - 3) % GRP) for i in range(GRP)])  27.7 us
    ppermute x14, starting transfers between devices, hop(): return lax.ppermute(array, 'win', pairs)  19.9 us
    pallas_call x1, Pallas kernels, middle(): pl.pallas_call(middle_kernel, grid_spec=pltpu.PrefetchScalarGridSpec(num_...  15.6 us
    all_to_all x1, waiting for transfers between devices, on_device(): moved = lax.all_to_all(white.reshape(WINS, 8, CH), ('win', 'grp'), 0, 0)  15.4 us
    all_to_all x1, starting transfers between devices, on_device(): moved = lax.all_to_all(white.reshape(WINS, 8, CH), ('win', 'grp'), 0, 0)  14.2 us
    pallas_call x1, Pallas kernels, backward(): pl.pallas_call(backward_kernel, grid=(2 * tiles,), in_specs=[full((16, 2,...  11.7 us
    all_to_all x1, starting transfers between devices, on_device(): returned = lax.all_to_all(grad.reshape(WINS, 8, CH), ('win', 'grp'), 0, 0)  7.87 us
  transfers between devices with their start and end apart: 18, of which 16 were waited for; matrix products, arithmetic and copies ran while one was open for 1% of the time, Pallas kernels for 4%

profile of v4, /device:TPU:64, one launch (start us, length us, event | category | flops | bytes accessed | tf_op | source)
XLA Modules:
  0.0 183.6 jit_solution(7231370840815004381)
XLA Ops:
  0.7 1.3 concatenate.3.sc_ref
  1.9 6.6 %forward.1 = (bf16[16,2,8,8,512]{4,3,2,1,0:T(8,128)(2,1)}, f32[8,2,512]{2,1,0:T(2,128)}) custom-call(bf16[512,2048]{1,0:T(8,128)(2,1)} %bitcast.119, f32[128,1024]{1,0:T(8,128)} %constant.43.clone.a_ref, f32[128,1024]{1,0:T(8,128)} %constant.44.clone.b_ref, f32[16,1024]{1,0:T(8,128)} %constant.45.clone.c_ref, f32[16,1024]{1,0:T(8,128)} %constant.46.clone.s_ref), custom_call_target="tpu_custom_call" | custom-call | flops 2147483648 | bytes 8388608 | tf_op jit(solution)/shard_map/forward/pallas_call | solution.py:132
  8.6 14.2 %all-to-all-start = ((bf16[256,8,512]{2,1,0:T(8,128)(2,1)}), bf16[256,8,512]{2,1,0:T(8,128)(2,1)S(1)}, u32[]{:S(2)}, u32[]{:S(2)}) async-start(bf16[256,8,512]{2,1,0:T(8,128)(2,1)} %bitcast.94), calls=%async_computation | async-start | bytes 4194304 | tf_op jit(solution)/shard_map/all_to_all | solution.py:409
  22.8 3.3 %pack_observed.1 = bf16[32,2,4,8,128]{4,3,2,1,0:T(8,128)(2,1)} custom-call(s32[7]{0:T(128)} %concatenate.3.sc_ref, f32[3,16,16,2048]{3,2,1,0:T(8,128)} %bitcast.91, f32[3,16,16,2048]{3,2,1,0:T(8,128)} %bitcast.92), custom_call_target="tpu_custom_call" | custom-call | tf_op jit(solution)/shard_map/pack_observed/pallas_call | solution.py:238
  26.1 1.1 fusion.15
  27.2 0.2 collective-permute-start
  27.4 1.4 collective-permute-done
  28.8 1.6 collective-permute-start.1
  30.4 1.8 collective-permute-start.3
  32.1 1.8 collective-permute-start.2
  33.9 4.2 %collective-permute-done.1 = bf16[2,4,2,4,8,128]{5,4,3,2,0,1:T(8,128)(2,1)S(1)} collective-permute-done((bf16[2,4,2,4,8,128]{5,4,3,2,0,1:T(8,128)(2,1)S(1)}, bf16[2,4,2,4,8,128]{5,4,3,2,0,1:T(8,128)(2,1)S(1)}, u32[]{:S(2)}, u32[]{:S(2)}) %collective-permute-start.1) | collective-permute-done | bytes 131104 | tf_op jit(solution)/shard_map/ppermute | solution.py:70
  38.2 3.8 %collective-permute-done.3 = bf16[2,4,2,4,8,128]{5,4,3,2,0,1:T(8,128)(2,1)S(1)} collective-permute-done((bf16[2,4,2,4,8,128]{5,4,3,2,0,1:T(8,128)(2,1)S(1)}, bf16[2,4,2,4,8,128]{5,4,3,2,0,1:T(8,128)(2,1)S(1)}, u32[]{:S(2)}, u32[]{:S(2)}) %collective-permute-start.3) | collective-permute-done | bytes 131104 | tf_op jit(solution)/shard_map/ppermute | solution.py:70
  41.9 1.8 collective-permute-done.2
  43.7 0.1 pad_maximum_fusion
  43.8 3.0 %collective-permute-start.6 = (bf16[4,2,2,4,8,128]{5,4,3,2,1,0:T(8,128)(2,1)S(1)}, bf16[4,2,2,4,8,128]{5,4,3,2,1,0:T(8,128)(2,1)S(1)}, u32[]{:S(2)}, u32[]{:S(2)}) collective-permute-start(bf16[4,2,2,4,8,128]{5,4,3,2,1,0:T(8,128)(2,1)S(1)} %get-tuple-element.27), channel_id=1, source_target_pairs={{0,192},{8,200},{16,208},{24,216},{32,224},{40,232},{48,240},{56,2... | collective-permute-start | bytes 393224 | tf_op jit(solution)/shard_map/ppermute | solution.py:70
  46.7 0.7 collective-permute-start.5
  47.5 0.9 collective-permute-start.4
  48.4 7.2 %collective-permute-done.6 = bf16[4,2,2,4,8,128]{5,4,3,2,1,0:T(8,128)(2,1)S(1)} collective-permute-done((bf16[4,2,2,4,8,128]{5,4,3,2,1,0:T(8,128)(2,1)S(1)}, bf16[4,2,2,4,8,128]{5,4,3,2,1,0:T(8,128)(2,1)S(1)}, u32[]{:S(2)}, u32[]{:S(2)}) %collective-permute-start.6) | collective-permute-done | bytes 131104 | tf_op jit(solution)/shard_map/ppermute | solution.py:70
  55.6 1.3 collective-permute-done.5
  56.9 2.3 %collective-permute-done.4 = bf16[4,2,2,4,8,128]{5,4,3,2,1,0:T(8,128)(2,1)S(1)} collective-permute-done((bf16[4,2,2,4,8,128]{5,4,3,2,1,0:T(8,128)(2,1)S(1)}, bf16[4,2,2,4,8,128]{5,4,3,2,1,0:T(8,128)(2,1)S(1)}, u32[]{:S(2)}, u32[]{:S(2)}) %collective-permute-start.4) | collective-permute-done | bytes 131104 | tf_op jit(solution)/shard_map/ppermute | solution.py:70
  59.2 0.9 pad_maximum_fusion.1
  60.0 15.4 %all-to-all-done = bf16[256,8,512]{2,1,0:T(8,128)(2,1)S(1)} async-done(((bf16[256,8,512]{2,1,0:T(8,128)(2,1)}), bf16[256,8,512]{2,1,0:T(8,128)(2,1)S(1)}, u32[]{:S(2)}, u32[]{:S(2)}) %all-to-all-start) | async-done | bytes 2097184 | tf_op jit(solution)/shard_map/all_to_all | solution.py:409
  75.4 1.3 copy-done
  76.7 15.6 %middle.1 = (bf16[32,2,4,8,128]{4,3,2,1,0:T(8,128)(2,1)}, bf16[2048,512]{1,0:T(8,128)(2,1)}) custom-call(s32[7]{0:T(128)} %concatenate.3.sc_ref, bf16[2048,512]{1,0:T(8,128)(2,1)} %bitcast.93, bf16[32,2,4,8,128]{4,3,2,1,0:T(8,128)(2,1)} %bitcast.98), custom_call_target="tpu_custom_call" | custom-call | tf_op jit(solution)/shard_map/middle/pallas_call | solution.py:341
  92.4 7.9 %all-to-all-start.1 = ((bf16[256,8,512]{2,1,0:T(8,128)(2,1)}), bf16[256,8,512]{2,1,0:T(8,128)(2,1)S(1)}, u32[]{:S(2)}, u32[]{:S(2)}) async-start(bf16[256,8,512]{2,1,0:T(8,128)(2,1)} %bitcast.96), calls=%async_computation.1 | async-start | bytes 4194304 | tf_op jit(solution)/shard_map/all_to_all | solution.py:412
  100.3 0.2 collective-permute-start.7
  100.5 1.4 collective-permute-done.7
  102.0 1.6 collective-permute-start.8
  103.5 1.8 collective-permute-start.10
  105.3 1.8 collective-permute-start.9
  107.1 4.3 %collective-permute-done.8 = bf16[2,4,2,4,8,128]{5,4,3,0,2,1:T(8,128)(2,1)S(1)} collective-permute-done((bf16[2,4,2,4,8,128]{5,4,3,0,2,1:T(8,128)(2,1)S(1)}, bf16[2,4,2,4,8,128]{5,4,3,0,2,1:T(8,128)(2,1)S(1)}, u32[]{:S(2)}, u32[]{:S(2)}) %collective-permute-start.8) | collective-permute-done | bytes 131104 | tf_op jit(solution)/shard_map/ppermute | solution.py:70
  111.4 0.6 collective-permute-done.10
  112.0 4.7 %collective-permute-done.9 = bf16[2,4,2,4,8,128]{5,4,3,0,2,1:T(8,128)(2,1)S(1)} collective-permute-done((bf16[2,4,2,4,8,128]{5,4,3,0,2,1:T(8,128)(2,1)S(1)}, bf16[2,4,2,4,8,128]{5,4,3,0,2,1:T(8,128)(2,1)S(1)}, u32[]{:S(2)}, u32[]{:S(2)}) %collective-permute-start.9) | collective-permute-done | bytes 131104 | tf_op jit(solution)/shard_map/ppermute | solution.py:70
  116.7 0.1 pad_maximum_fusion.2
  116.8 3.0 %collective-permute-start.13 = (bf16[4,2,2,4,8,128]{5,4,3,1,0,2:T(8,128)(2,1)S(1)}, bf16[4,2,2,4,8,128]{5,4,3,1,0,2:T(8,128)(2,1)S(1)}, u32[]{:S(2)}, u32[]{:S(2)}) collective-permute-start(bf16[4,2,2,4,8,128]{5,4,3,1,0,2:T(8,128)(2,1)S(1)} %get-tuple-element.17), channel_id=1, source_target_pairs={{0,192},{8,200},{16,208},{24,216},{32,224},{40,232},{48,240},{56,2... | collective-permute-start | bytes 393224 | tf_op jit(solution)/shard_map/ppermute | solution.py:70
  119.8 0.7 collective-permute-start.12
  120.5 0.9 collective-permute-start.11
  121.4 7.8 %collective-permute-done.13 = bf16[4,2,2,4,8,128]{5,4,3,1,0,2:T(8,128)(2,1)S(1)} collective-permute-done((bf16[4,2,2,4,8,128]{5,4,3,1,0,2:T(8,128)(2,1)S(1)}, bf16[4,2,2,4,8,128]{5,4,3,1,0,2:T(8,128)(2,1)S(1)}, u32[]{:S(2)}, u32[]{:S(2)}) %collective-permute-start.13) | collective-permute-done | bytes 131104 | tf_op jit(solution)/shard_map/ppermute | solution.py:70
  129.2 0.6 collective-permute-done.12
  129.8 3.6 %collective-permute-done.11 = bf16[4,2,2,4,8,128]{5,4,3,1,0,2:T(8,128)(2,1)S(1)} collective-permute-done((bf16[4,2,2,4,8,128]{5,4,3,1,0,2:T(8,128)(2,1)S(1)}, bf16[4,2,2,4,8,128]{5,4,3,1,0,2:T(8,128)(2,1)S(1)}, u32[]{:S(2)}, u32[]{:S(2)}) %collective-permute-start.11) | collective-permute-done | bytes 131104 | tf_op jit(solution)/shard_map/ppermute | solution.py:70
  133.4 0.1 pad_maximum_fusion.3
  133.5 4.5 %collective-permute-start.15 = (bf16[32,4,8,128]{3,2,1,0:T(8,128)(2,1)S(1)}, bf16[32,4,8,128]{3,2,1,0:T(8,128)(2,1)S(1)}, u32[]{:S(2)}, u32[]{:S(2)}) collective-permute-start(bf16[32,4,8,128]{3,2,1,0:T(8,128)(2,1)S(1)} %get-tuple-element.14), channel_id=1, source_target_pairs={{0,5},{1,6},{2,7},{3,0},{4,1},{5,2},{6,3},{7,4},{8,13},{9,14},{10,... | collective-permute-start | bytes 786440 | tf_op jit(solution)/shard_map/ppermute | solution.py:415
  138.0 27.7 %collective-permute-done.15.down_ref = bf16[32,4,8,128]{3,2,1,0:T(8,128)(2,1)S(1)} collective-permute-done((bf16[32,4,8,128]{3,2,1,0:T(8,128)(2,1)S(1)}, bf16[32,4,8,128]{3,2,1,0:T(8,128)(2,1)S(1)}, u32[]{:S(2)}, u32[]{:S(2)}) %collective-permute-start.15) | collective-permute-done | bytes 262176 | tf_op jit(solution)/shard_map/ppermute | solution.py:415
  165.7 0.7 copy-done.3
  166.4 0.7 copy-done.4
  167.1 3.4 %unpack_correl.1 = f32[3,16,16,256]{3,2,1,0:T(8,128)} custom-call(s32[7]{0:T(128)} %concatenate.3.sc_ref, bf16[32,4,8,128]{3,2,1,0:T(8,128)(2,1)} %copy-done.4, bf16[32,4,8,128]{3,2,1,0:T(8,128)(2,1)} %copy-done.3), custom_call_target="tpu_custom_call" | custom-call | tf_op jit(solution)/shard_map/unpack_correl/pallas_call | solution.py:385
  170.5 1.3 copy-done.1
  171.8 11.7 %backward.1 = bf16[512,2048]{1,0:T(8,128)(2,1)} custom-call(bf16[16,2,8,8,512]{4,3,2,1,0:T(8,128)(2,1)} %bitcast.95, bf16[16,2,8,8,512]{4,3,2,1,0:T(8,128)(2,1)} %get-tuple-element.10.y_ref, f32[8,2,512]{2,1,0:T(2,128)} %get-tuple-element.13.r_ref, f32[128,1024]{1,0:T(8,128)} %constant.43.clone.a_ref, f32[128,1024]{1,0:T(8,128)} %constant.44.clone.b_ref, ...), custom_call_target="tpu_custom_call" | custom-call | flops 2147483648 | bytes 10485760 | tf_op jit(solution)/shard_map/backward/pallas_call | solution.py:195
  (15 shorter events, 0.3 us)
Async XLA Ops:
  8.6 66.8 %all-to-all-start = ((bf16[256,8,512]{2,1,0:T(8,128)(2,1)}), bf16[256,8,512]{2,1,0:T(8,128)(2,1)S(1)}, u32[]{:S(2)}, u32[]{:S(2)}) async-start(bf16[256,8,512]{2,1,0:T(8,128)(2,1)} %bitcast.94), calls=%async_computation | async-start | bytes 4194304 | tf_op jit(solution)/shard_map/all_to_all | solution.py:409
  27.2 1.6 collective-permute-start
  28.8 9.3 %collective-permute-start.1 = (bf16[2,4,2,4,8,128]{5,4,3,2,0,1:T(8,128)(2,1)S(1)}, bf16[2,4,2,4,8,128]{5,4,3,2,0,1:T(8,128)(2,1)S(1)}, u32[]{:S(2)}, u32[]{:S(2)}) collective-permute-start(bf16[2,4,2,4,8,128]{5,4,3,2,0,1:T(8,128)(2,1)S(1)} %get-tuple-element.31), channel_id=1, source_target_pairs={{0,16},{8,24},{16,32},{24,40},{32,48},{40,56},{48,0},{56,8},{64,80... | collective-permute-start | bytes 393224 | tf_op jit(solution)/shard_map/ppermute | solution.py:70
  30.4 11.5 %collective-permute-start.3 = (bf16[2,4,2,4,8,128]{5,4,3,2,0,1:T(8,128)(2,1)S(1)}, bf16[2,4,2,4,8,128]{5,4,3,2,0,1:T(8,128)(2,1)S(1)}, u32[]{:S(2)}, u32[]{:S(2)}) collective-permute-start(bf16[2,4,2,4,8,128]{5,4,3,2,0,1:T(8,128)(2,1)S(1)} %get-tuple-element.32), channel_id=1, source_target_pairs={{0,48},{8,56},{16,0},{24,8},{32,16},{40,24},{48,32},{56,40},{64,11... | collective-permute-start | bytes 393224 | tf_op jit(solution)/shard_map/ppermute | solution.py:70
  32.1 11.5 %collective-permute-start.2 = (bf16[2,4,2,4,8,128]{5,4,3,2,0,1:T(8,128)(2,1)S(1)}, bf16[2,4,2,4,8,128]{5,4,3,2,0,1:T(8,128)(2,1)S(1)}, u32[]{:S(2)}, u32[]{:S(2)}) collective-permute-start(bf16[2,4,2,4,8,128]{5,4,3,2,0,1:T(8,128)(2,1)S(1)} %get-tuple-element.33), channel_id=1, source_target_pairs={{0,32},{8,40},{16,48},{24,56},{32,0},{40,8},{48,16},{56,24},{64,96... | collective-permute-start | bytes 393224 | tf_op jit(solution)/shard_map/ppermute | solution.py:70
  43.8 11.8 %collective-permute-start.6 = (bf16[4,2,2,4,8,128]{5,4,3,2,1,0:T(8,128)(2,1)S(1)}, bf16[4,2,2,4,8,128]{5,4,3,2,1,0:T(8,128)(2,1)S(1)}, u32[]{:S(2)}, u32[]{:S(2)}) collective-permute-start(bf16[4,2,2,4,8,128]{5,4,3,2,1,0:T(8,128)(2,1)S(1)} %get-tuple-element.27), channel_id=1, source_target_pairs={{0,192},{8,200},{16,208},{24,216},{32,224},{40,232},{48,240},{56,2... | collective-permute-start | bytes 393224 | tf_op jit(solution)/shard_map/ppermute | solution.py:70
  46.7 10.2 %collective-permute-start.5 = (bf16[4,2,2,4,8,128]{5,4,3,2,1,0:T(8,128)(2,1)S(1)}, bf16[4,2,2,4,8,128]{5,4,3,2,1,0:T(8,128)(2,1)S(1)}, u32[]{:S(2)}, u32[]{:S(2)}) collective-permute-start(bf16[4,2,2,4,8,128]{5,4,3,2,1,0:T(8,128)(2,1)S(1)} %get-tuple-element.28), channel_id=1, source_target_pairs={{0,128},{8,136},{16,144},{24,152},{32,160},{40,168},{48,176},{56,1... | collective-permute-start | bytes 393224 | tf_op jit(solution)/shard_map/ppermute | solution.py:70
  47.5 11.7 %collective-permute-start.4 = (bf16[4,2,2,4,8,128]{5,4,3,2,1,0:T(8,128)(2,1)S(1)}, bf16[4,2,2,4,8,128]{5,4,3,2,1,0:T(8,128)(2,1)S(1)}, u32[]{:S(2)}, u32[]{:S(2)}) collective-permute-start(bf16[4,2,2,4,8,128]{5,4,3,2,1,0:T(8,128)(2,1)S(1)} %get-tuple-element.29), channel_id=1, source_target_pairs={{0,64},{8,72},{16,80},{24,88},{32,96},{40,104},{48,112},{56,120},{... | collective-permute-start | bytes 393224 | tf_op jit(solution)/shard_map/ppermute | solution.py:70
  75.4 1.3 copy-start
  92.4 7.9 %copy-start.2 = (bf16[32,2,4,8,128]{4,3,2,1,0:T(8,128)(2,1)S(1)}, bf16[32,2,4,8,128]{4,3,2,1,0:T(8,128)(2,1)}, u32[]{:S(2)}) copy-start(bf16[32,2,4,8,128]{4,3,2,1,0:T(8,128)(2,1)} %get-tuple-element.11) | copy-start | bytes 1572868
  92.4 78.1 %all-to-all-start.1 = ((bf16[256,8,512]{2,1,0:T(8,128)(2,1)}), bf16[256,8,512]{2,1,0:T(8,128)(2,1)S(1)}, u32[]{:S(2)}, u32[]{:S(2)}) async-start(bf16[256,8,512]{2,1,0:T(8,128)(2,1)} %bitcast.96), calls=%async_computation.1 | async-start | bytes 4194304 | tf_op jit(solution)/shard_map/all_to_all | solution.py:412
  100.3 1.6 collective-permute-start.7
  102.0 9.4 %collective-permute-start.8 = (bf16[2,4,2,4,8,128]{5,4,3,0,2,1:T(8,128)(2,1)S(1)}, bf16[2,4,2,4,8,128]{5,4,3,0,2,1:T(8,128)(2,1)S(1)}, u32[]{:S(2)}, u32[]{:S(2)}) collective-permute-start(bf16[2,4,2,4,8,128]{5,4,3,0,2,1:T(8,128)(2,1)S(1)} %get-tuple-element.21), channel_id=1, source_target_pairs={{0,16},{8,24},{16,32},{24,40},{32,48},{40,56},{48,0},{56,8},{64,80... | collective-permute-start | bytes 393224 | tf_op jit(solution)/shard_map/ppermute | solution.py:70
  103.5 8.4 %collective-permute-start.10 = (bf16[2,4,2,4,8,128]{5,4,3,0,2,1:T(8,128)(2,1)S(1)}, bf16[2,4,2,4,8,128]{5,4,3,0,2,1:T(8,128)(2,1)S(1)}, u32[]{:S(2)}, u32[]{:S(2)}) collective-permute-start(bf16[2,4,2,4,8,128]{5,4,3,0,2,1:T(8,128)(2,1)S(1)} %get-tuple-element.22), channel_id=1, source_target_pairs={{0,48},{8,56},{16,0},{24,8},{32,16},{40,24},{48,32},{56,40},{64,11... | collective-permute-start | bytes 393224 | tf_op jit(solution)/shard_map/ppermute | solution.py:70
  105.3 11.4 %collective-permute-start.9 = (bf16[2,4,2,4,8,128]{5,4,3,0,2,1:T(8,128)(2,1)S(1)}, bf16[2,4,2,4,8,128]{5,4,3,0,2,1:T(8,128)(2,1)S(1)}, u32[]{:S(2)}, u32[]{:S(2)}) collective-permute-start(bf16[2,4,2,4,8,128]{5,4,3,0,2,1:T(8,128)(2,1)S(1)} %get-tuple-element.23), channel_id=1, source_target_pairs={{0,32},{8,40},{16,48},{24,56},{32,0},{40,8},{48,16},{56,24},{64,96... | collective-permute-start | bytes 393224 | tf_op jit(solution)/shard_map/ppermute | solution.py:70
  116.8 12.4 %collective-permute-start.13 = (bf16[4,2,2,4,8,128]{5,4,3,1,0,2:T(8,128)(2,1)S(1)}, bf16[4,2,2,4,8,128]{5,4,3,1,0,2:T(8,128)(2,1)S(1)}, u32[]{:S(2)}, u32[]{:S(2)}) collective-permute-start(bf16[4,2,2,4,8,128]{5,4,3,1,0,2:T(8,128)(2,1)S(1)} %get-tuple-element.17), channel_id=1, source_target_pairs={{0,192},{8,200},{16,208},{24,216},{32,224},{40,232},{48,240},{56,2... | collective-permute-start | bytes 393224 | tf_op jit(solution)/shard_map/ppermute | solution.py:70
  119.8 10.0 %collective-permute-start.12 = (bf16[4,2,2,4,8,128]{5,4,3,1,0,2:T(8,128)(2,1)S(1)}, bf16[4,2,2,4,8,128]{5,4,3,1,0,2:T(8,128)(2,1)S(1)}, u32[]{:S(2)}, u32[]{:S(2)}) collective-permute-start(bf16[4,2,2,4,8,128]{5,4,3,1,0,2:T(8,128)(2,1)S(1)} %get-tuple-element.18), channel_id=1, source_target_pairs={{0,128},{8,136},{16,144},{24,152},{32,160},{40,168},{48,176},{56,1... | collective-permute-start | bytes 393224 | tf_op jit(solution)/shard_map/ppermute | solution.py:70
  120.5 12.9 %collective-permute-start.11 = (bf16[4,2,2,4,8,128]{5,4,3,1,0,2:T(8,128)(2,1)S(1)}, bf16[4,2,2,4,8,128]{5,4,3,1,0,2:T(8,128)(2,1)S(1)}, u32[]{:S(2)}, u32[]{:S(2)}) collective-permute-start(bf16[4,2,2,4,8,128]{5,4,3,1,0,2:T(8,128)(2,1)S(1)} %get-tuple-element.19), channel_id=1, source_target_pairs={{0,64},{8,72},{16,80},{24,88},{32,96},{40,104},{48,112},{56,120},{... | collective-permute-start | bytes 393224 | tf_op jit(solution)/shard_map/ppermute | solution.py:70
  133.5 32.2 %collective-permute-start.15 = (bf16[32,4,8,128]{3,2,1,0:T(8,128)(2,1)S(1)}, bf16[32,4,8,128]{3,2,1,0:T(8,128)(2,1)S(1)}, u32[]{:S(2)}, u32[]{:S(2)}) collective-permute-start(bf16[32,4,8,128]{3,2,1,0:T(8,128)(2,1)S(1)} %get-tuple-element.14), channel_id=1, source_target_pairs={{0,5},{1,6},{2,7},{3,0},{4,1},{5,2},{6,3},{7,4},{8,13},{9,14},{10,... | collective-permute-start | bytes 786440 | tf_op jit(solution)/shard_map/ppermute | solution.py:415
  138.0 27.7 %collective-permute-start.14 = (bf16[32,4,8,128]{3,2,1,0:T(8,128)(2,1)S(1)}, bf16[32,4,8,128]{3,2,1,0:T(8,128)(2,1)S(1)}, u32[]{:S(2)}, u32[]{:S(2)}) collective-permute-start(bf16[32,4,8,128]{3,2,1,0:T(8,128)(2,1)S(1)} %get-tuple-element.15), channel_id=1, source_target_pairs={{0,1},{1,2},{2,3},{3,4},{4,5},{5,6},{6,7},{7,0},{8,9},{9,10},{10,1... | collective-permute-start | bytes 786440 | tf_op jit(solution)/shard_map/ppermute | solution.py:414
  165.7 0.7 copy-start.3
  166.4 0.7 copy-start.4
  170.5 1.3 copy-start.1

commit v5 on v4

--- a/solution.py
+++ b/solution.py
@@ -23,7 +23,7 @@
 LANES = 128
 HALF = 64
 EMPTY = 64.0
-VMEM_LIMIT = 56 << 20
+VMEM_LIMIT = 24 << 20
 
 F32 = jnp.float32
 BF16 = jnp.bfloat16
@@ -38,16 +38,27 @@
 
 
 def table_parts():
-    row = np.arange(2 * BAND)
-    j = (row % 64) // 8 * 8 + row % KB * 2 + row // 64
+    row = np.arange(BAND)
+    j = row // 8 * 8 + row % KB * 2
     imag = (row % 8) >= KB
     n = np.arange(SEG // 2)
     ang = 2.0 * math.pi * ((n[None, :] * j[:, None]) % SEG) / SEG
     a = np.where(imag[:, None], -np.sin(ang), np.cos(ang))
-    b = np.where(imag[:, None], -np.cos(ang), -np.sin(ang))
-    band = np.arange(FREQ // BAND)
-    bang = 2.0 * math.pi * ((n[None, :] * (BAND * band[:, None])) % SEG) / SEG
-    return [np.asarray(v, np.float32) for v in (a, b, np.cos(bang), np.sin(bang))]
+    bins = np.concatenate([BAND * np.arange(FREQ // BAND), np.ones(8, np.int64)])
+    turn = 2.0 * math.pi * ((n[None, :] * bins[:, None]) % SEG) / SEG
+    return [np.asarray(v, np.float32) for v in (a, np.cos(turn), np.sin(turn))]
+
+
+def other_part(a):
+    imag = lax.broadcasted_iota(jnp.int32, a.shape, 0) % 8 >= KB
+    return jnp.where(imag, -pltpu.roll(a, KB, 0), pltpu.roll(a, BAND - KB, 0))
+
+
+def band_pairs(a_ref, c_ref, s_ref, cols):
+    even = a_ref[:, cols]
+    turned = other_part(even)
+    odd = even * c_ref[16:17, cols] + turned * s_ref[16:17, cols]
+    return (even, turned), (odd, other_part(odd))
 
 
 NSC = 7
@@ -96,117 +107,128 @@
     return pl.BlockSpec(shape, lambda *i: (0,) * len(shape))
 
 
-def forward_kernel(x_ref, a_ref, b_ref, c_ref, s_ref, y_ref, r_ref, h_ref):
-    step = pl.program_id(0)
-
-    @pl.when(step == 0)
-    def _():
-        early = x_ref[:, : SEG // 2].astype(F32)
-        late = x_ref[:, SEG // 2 :].astype(F32)
-        h_ref[0] = (early + late).astype(BF16)
-        h_ref[1] = (early - late).astype(BF16)
-
-    waves = []
-    for p in range(2):
-        a = a_ref[p * 64 : (p + 1) * 64]
-        b = b_ref[p * 64 : (p + 1) * 64]
-        parts = []
+def plane_bands(g):
+    h = 0 if 3 <= g <= 6 else 1
+    q = g - 3 if h == 0 else (g + 1) % GRP
+    return (q * 4 + h * 2, q * 4 + h * 2 + 1)
+
+
+def forward_kernel(x_ref, a_ref, c_ref, s_ref, y_hbm, r_ref, y_ref, sem):
+    copies = []
+    early = x_ref[:, : SEG // 2].astype(F32)
+    late = x_ref[:, SEG // 2 :].astype(F32)
+    pairs = band_pairs(a_ref, c_ref, s_ref, slice(None))
+    halves = ((early + late).astype(BF16), (early - late).astype(BF16))
+    for step in range(4):
+        waves = []
+        for p in range(2):
+            a, b = pairs[p]
+            parts = []
+            for g in (step * 2, step * 2 + 1):
+                for band in plane_bands(g):
+                    parts.append((a * c_ref[band : band + 1, :] + b * s_ref[band : band + 1, :]).astype(BF16))
+            waves.append(dot(jnp.concatenate(parts, axis=0), halves[p], 1, 1))
         for gi in range(2):
-            g = step * 2 + gi
             for wh in range(2):
-                band = quarter_of(g) * 4 + half_of(g) * 2 + wh
-                parts.append((a * c_ref[pl.ds(band, 1), :] + b * s_ref[pl.ds(band, 1), :]).astype(BF16))
-        waves.append(dot(jnp.concatenate(parts, axis=0), h_ref[p], 1, 1))
-    for gi in range(2):
-        for wh in range(2):
-            row = (gi * 2 + wh) * 64
-            rows = [w[row : row + 64] for w in waves]
-            level = jnp.sum(rows[0] * rows[0] + rows[1] * rows[1], axis=0, keepdims=True)
-            inv = lax.rsqrt(level * (1.0 / BAND) + 1e-05)
-            r_ref[gi, wh : wh + 1, :] = inv
-            for p in range(2):
-                y_ref[wh * 8 : (wh + 1) * 8, p, gi] = (rows[p] * inv).reshape(8, 8, CH).astype(BF16)
+                row = (gi * 2 + wh) * 64
+                rows = [w[row : row + 64] for w in waves]
+                level = jnp.sum(rows[0] * rows[0] + rows[1] * rows[1], axis=0, keepdims=True)
+                inv = lax.rsqrt(level * (1.0 / BAND) + 1e-05)
+                r_ref[step * 2 + gi, wh : wh + 1, :] = inv
+                for p in range(2):
+                    tile = (rows[p] * inv).reshape(8, 8, CH).astype(BF16)
+                    y_ref[wh * 8 : (wh + 1) * 8, p, step * 2 + gi] = tile
+        planes = (slice(None), slice(None), slice(step * 2, step * 2 + 2))
+        copy = pltpu.make_async_copy(y_ref.at[planes], y_hbm.at[planes], sem.at[step])
+        copy.start()
+        copies.append(copy)
+    for copy in copies:
+        copy.wait()
+
+
+IN_VMEM = pl.BlockSpec(memory_space=pltpu.VMEM)
+IN_HBM = pl.BlockSpec(memory_space=pltpu.HBM)
+IN_SMEM = pl.BlockSpec(memory_space=pltpu.SMEM)
 
 
 def forward(x, consts):
     return pl.pallas_call(
         forward_kernel,
-        grid=(4,),
-        in_specs=[full((CH, SEG)), full((128, SEG // 2)), full((128, SEG // 2)), full((16, SEG // 2)), full((16, SEG // 2))],
-        out_specs=[
-            pl.BlockSpec((16, 2, 2, 8, CH), lambda i: (0, 0, i, 0, 0)),
-            pl.BlockSpec((2, 2, CH), lambda i: (i, 0, 0)),
-        ],
+        in_specs=[IN_VMEM] * 4,
+        out_specs=[IN_HBM, IN_VMEM],
         out_shape=[
-            jax.ShapeDtypeStruct((16, 2, GRP, 8, CH), BF16),
+            pltpu.HBM((16, 2, GRP, 8, CH), BF16),
             jax.ShapeDtypeStruct((GRP, 2, CH), F32),
         ],
-        scratch_shapes=[pltpu.VMEM((2, CH, SEG // 2), BF16)],
+        scratch_shapes=[pltpu.VMEM((16, 2, GRP, 8, CH), BF16), pltpu.SemaphoreType.DMA((4,))],
         compiler_params=pltpu.CompilerParams(vmem_limit_bytes=VMEM_LIMIT),
         cost_estimate=pl.CostEstimate(flops=CH * SEG * SEG, bytes_accessed=8 << 20, transcendentals=0),
         name="forward",
     )(x, *consts)
 
 
-def backward_kernel(g_ref, y_ref, r_ref, a_ref, b_ref, c_ref, s_ref, o_ref, d_ref, late_ref):
-    step = pl.program_id(0)
-
-    @pl.when(step == 0)
-    def _():
-        for plane in range(GRP):
-            sides = ([], [])
-            for wh in range(2):
-                at = slice(wh * 8, (wh + 1) * 8)
-                g = [g_ref[at, p, plane].astype(F32).reshape(64, CH) for p in range(2)]
-                y = [y_ref[at, p, plane].astype(F32).reshape(64, CH) for p in range(2)]
-                inv = r_ref[plane, wh : wh + 1, :]
-                mean = jnp.sum(g[0] * y[0] + g[1] * y[1], axis=0, keepdims=True) * (1.0 / BAND)
-                for p in range(2):
-                    sides[p].append((g[p] - y[p] * mean) * inv)
+def backward_kernel(g_hbm, y_ref, r_ref, a_ref, c_ref, s_ref, o_ref, g_ref, d_ref, stage_ref, sem):
+    loads = []
+    for step in range(4):
+        planes = (slice(None), slice(None), slice(step * 2, step * 2 + 2))
+        load = pltpu.make_async_copy(g_hbm.at[planes], g_ref.at[planes], sem.at[8 + step])
+        load.start()
+        loads.append(load)
+    for plane in range(GRP):
+        if plane % 2 == 0:
+            loads[plane // 2].wait()
+        sides = ([], [])
+        for wh in range(2):
+            at = slice(wh * 8, (wh + 1) * 8)
+            g = [g_ref[at, p, plane].astype(F32).reshape(64, CH) for p in range(2)]
+            y = [y_ref[at, p, plane].astype(F32).reshape(64, CH) for p in range(2)]
+            inv = r_ref[plane, wh : wh + 1, :]
+            mean = jnp.sum(g[0] * y[0] + g[1] * y[1], axis=0, keepdims=True) * (1.0 / BAND)
             for p in range(2):
-                turned = jnp.concatenate(sides[p], axis=0).T
-                d_ref[p, :, plane * 128 : (plane + 1) * 128] = turned.astype(BF16)
-
-    @pl.when(step % 2 == 0)
-    def _():
+                sides[p].append((g[p] - y[p] * mean) * inv)
+        for p in range(2):
+            turned = jnp.concatenate(sides[p], axis=0).astype(BF16).T
+            d_ref[p, :, plane * 128 : (plane + 1) * 128] = turned
+
+    tile = 256
+    tiles = SEG // 2 // tile
+    copies = []
+    for t in range(tiles):
+        cols = slice(t * tile, (t + 1) * tile)
+        pairs = band_pairs(a_ref, c_ref, s_ref, cols)
         waves = []
         for p in range(2):
-            a = a_ref[p * 64 : (p + 1) * 64]
-            b = b_ref[p * 64 : (p + 1) * 64]
+            a, b = pairs[p]
             parts = []
             for plane in range(GRP):
-                h = 0 if 3 <= plane <= 6 else 1
-                q = plane - 3 if h == 0 else (plane + 1) % GRP
-                for band in (q * 4 + h * 2, q * 4 + h * 2 + 1):
-                    parts.append((a * c_ref[band : band + 1, :] + b * s_ref[band : band + 1, :]).astype(BF16))
+                for band in plane_bands(plane):
+                    c = c_ref[band : band + 1, cols]
+                    s = s_ref[band : band + 1, cols]
+                    parts.append((a * c + b * s).astype(BF16))
             waves.append(dot(d_ref[p], jnp.concatenate(parts, axis=0)))
-        o_ref[...] = (waves[0] + waves[1]).astype(BF16)
-        late_ref[...] = (waves[0] - waves[1]).astype(BF16)
-
-    @pl.when(step % 2 == 1)
-    def _():
-        o_ref[...] = late_ref[...]
+        stage_ref[2 * t] = (waves[0] + waves[1]).astype(BF16)
+        stage_ref[2 * t + 1] = (waves[0] - waves[1]).astype(BF16)
+        for part in range(2):
+            to = o_ref.at[:, pl.ds(part * (SEG // 2) + t * tile, tile)]
+            copy = pltpu.make_async_copy(stage_ref.at[2 * t + part], to, sem.at[2 * t + part])
+            copy.start()
+            copies.append(copy)
+    for copy in copies:
+        copy.wait()
 
 
 def backward(g, y, r, consts):
-    tile = 256
-    tiles = SEG // 2 // tile
-    col = lambda rows: pl.BlockSpec((rows, tile), lambda i: (0, i // 2))
     return pl.pallas_call(
         backward_kernel,
-        grid=(2 * tiles,),
-        in_specs=[
-            full((16, 2, GRP, 8, CH)),
-            full((16, 2, GRP, 8, CH)),
-            full((GRP, 2, CH)),
-            col(128),
-            col(128),
-            col(16),
-            col(16),
+        in_specs=[IN_HBM] + [IN_VMEM] * 5,
+        out_specs=pl.BlockSpec(memory_space=pl.ANY),
+        out_shape=jax.ShapeDtypeStruct((CH, SEG), BF16),
+        scratch_shapes=[
+            pltpu.VMEM((16, 2, GRP, 8, CH), BF16),
+            pltpu.VMEM((2, CH, SEG // 2), BF16),
+            pltpu.VMEM((8, CH, 256), BF16),
+            pltpu.SemaphoreType.DMA((12,)),
         ],
-        out_specs=pl.BlockSpec((CH, tile), lambda i: (0, i // 2 + i % 2 * tiles)),
-        out_shape=jax.ShapeDtypeStruct((CH, SEG), BF16),
-        scratch_shapes=[pltpu.VMEM((2, CH, SEG // 2), BF16), pltpu.VMEM((CH, tile), BF16)],
         compiler_params=pltpu.CompilerParams(vmem_limit_bytes=VMEM_LIMIT),
         cost_estimate=pl.CostEstimate(flops=CH * SEG * SEG, bytes_accessed=10 << 20, transcendentals=0),
         name="backward",
@@ -249,7 +271,7 @@
     )(scalars, observed, observed)
 
 
-def middle_kernel(sc_ref, x_ref, obs_ref, corr_ref, out_ref, u_ref, d_ref):
+def middle_kernel(sc_ref, x_ref, obs_ref, corr_ref, out_hbm, u_ref, d_ref, out_ref, sem):
     half, me = sc_ref[4], sc_ref[6]
     perm = regroup(False)
     for gr in range(8):
@@ -262,7 +284,7 @@
     lane8 = lax.broadcasted_iota(jnp.int32, (8, LANES), 1)
     lane16 = lax.broadcasted_iota(jnp.int32, (16, LANES), 1)
 
-    def one_bin(k, carry):
+    def one_bin(k):
         later = None
         for b in range(4):
             width = 2 if b < 3 else 1
@@ -321,10 +343,11 @@
             later = pushed[:, 256:] if width == 2 else None
             d_ref[k, :WINS, b * LANES : (b + 1) * LANES] = grad[:, :LANES].astype(BF16)
             d_ref[k, WINS:, b * LANES : (b + 1) * LANES] = grad[:, LANES:].astype(BF16)
-        return carry
-
-    lax.fori_loop(0, KB, one_bin, 0)
+
+    for k in range(KB):
+        one_bin(k)
     back = regroup(True)
+    copies = []
     for gr in range(8):
         rows = jnp.concatenate(
             [
@@ -333,23 +356,29 @@
             ],
             axis=0,
         )
-        out_ref[gr * 256 : (gr + 1) * 256, :] = dot(back, rows).astype(BF16)
+        place = slice(gr * 256, (gr + 1) * 256)
+        out_ref[place, :] = dot(back, rows).astype(BF16)
+        copy = pltpu.make_async_copy(out_ref.at[place, :], out_hbm.at[place, :], sem.at[gr])
+        copy.start()
+        copies.append(copy)
+    for copy in copies:
+        copy.wait()
 
 
 def middle(scalars, x, obs):
-    block = lambda shape: pl.BlockSpec(shape, lambda i, sc: (0,) * len(shape))
     return pl.pallas_call(
         middle_kernel,
-        grid_spec=pltpu.PrefetchScalarGridSpec(
-            num_scalar_prefetch=1,
-            grid=(1,),
-            in_specs=[block((2048, CH)), block((NB, 2, KB, 8, LANES))],
-            out_specs=[block((NB, 2, KB, 8, LANES)), block((2048, CH))],
-            scratch_shapes=[pltpu.VMEM((KB, 2 * WINS, CH), BF16), pltpu.VMEM((KB, 2 * WINS, CH), BF16)],
-        ),
+        in_specs=[IN_SMEM, IN_VMEM, IN_VMEM],
+        out_specs=[IN_VMEM, IN_HBM],
+        scratch_shapes=[
+            pltpu.VMEM((KB, 2 * WINS, CH), BF16),
+            pltpu.VMEM((KB, 2 * WINS, CH), BF16),
+            pltpu.VMEM((2048, CH), BF16),
+            pltpu.SemaphoreType.DMA((8,)),
+        ],
         out_shape=[
             jax.ShapeDtypeStruct((NB, 2, KB, 8, LANES), BF16),
-            jax.ShapeDtypeStruct((2048, CH), BF16),
+            pltpu.HBM((2048, CH), BF16),
         ],
         compiler_params=pltpu.CompilerParams(vmem_limit_bytes=VMEM_LIMIT),
         name="middle",
@@ -398,14 +427,12 @@
 
 def on_device(traces, pair_lists, observed):
     consts = [jnp.asarray(v) for v in table_parts()]
-    g = lax.axis_index("grp")
+    white, inverse = forward(traces[0], consts)
+    white, pair_lists = lax.optimization_barrier((white, pair_lists))
+    g, me = lax.axis_index("grp"), lax.axis_index("win")
     half, q = half_of(g), quarter_of(g)
     low = jnp.where(g < 4, 1, 0)
-    me = lax.axis_index("win")
     scalars = jnp.concatenate([pair_lists[0], jnp.stack([2 * q + half, half, low, me]).astype(jnp.int32)])
-
-    white, inverse = forward(traces[0], consts)
-    white, scalars = lax.optimization_barrier((white, scalars))
     moved = lax.all_to_all(white.reshape(WINS, 8, CH), ("win", "grp"), 0, 0)
     seen = exchange(pack_observed(scalars, observed[0]))
     corr, grad = middle(scalars, moved.reshape(2048, CH), seen)
@@ -414,6 +441,7 @@
     up = lax.ppermute(corr[:, 0], "grp", [(i, (i + 1) % GRP) for i in range(GRP)])
     down = lax.ppermute(corr[:, 1], "grp", [(i, (i - 3) % GRP) for i in range(GRP)])
     trace_grad = backward(returned.reshape(16, 2, GRP, 8, CH), white, inverse, consts)
+    up, down, trace_grad = lax.optimization_barrier((up, down, trace_grad))
     correl = unpack_correl(scalars, up, down)
     return correl[None], trace_grad[None]
 

time: 184 us -> 164 us (0.89)
  Pallas kernels: 40.7 us -> 25.6 us
  waiting for transfers between devices: 88 us -> 79.7 us
  starting transfers between devices: 46.4 us -> 49.1 us
    ppermute x1, waiting for transfers between devices: 27.7 us -> 3.84 us  [on_device(): lax.ppermute(corr[:, 1], 'grp', [(i, (i - 3) % GRP) for i in range(GRP)])]
    all_to_all x1, waiting for transfers between devices: 0.01 us -> 15.5 us  [on_device(): returned = lax.all_to_all(grad.reshape(WINS, 8, CH), ('win', 'grp'), 0, 0)]
    pallas_call x3, Pallas kernels: 34 us -> 22.2 us  [the longest x1 11.8 us: middle(): pl.pallas_call(middle_kernel, in_specs=[IN_SMEM, IN_VMEM, IN_VMEM], out_s...]
    unnamed x10 -> x20, local copies, waits for them, and re-layouts: 4.04 us -> 7.13 us
    pallas_call x1, Pallas kernels: 3.32 us -> 1.22 us  [pack_observed(): pl.pallas_call(pack_kernel, grid_spec=pltpu.PrefetchScalarGridSpec(num_sc...]
  transfers between devices with their start and end apart: 18 -> 18, of which waited for: 16 -> 17; matrix products, arithmetic and copies ran while one was open for 1% -> 1% of each run, Pallas kernels for 4% -> 5%
where the time goes in v5:
time: 164 us
  waiting for transfers between devices  79.7 us (49%)
  starting transfers between devices  49.1 us (30%)
  Pallas kernels  25.6 us (16%)
  local copies, waits for them, and re-layouts  8.1 us (5%)
    ppermute x14, waiting for transfers between devices, hop(): return lax.ppermute(array, 'win', pairs)  43.9 us
    ppermute x14, starting transfers between devices, hop(): return lax.ppermute(array, 'win', pairs)  19.8 us
    all_to_all x1, waiting for transfers between devices, on_device(): moved = lax.all_to_all(white.reshape(WINS, 8, CH), ('win', 'grp'), 0, 0)  16.4 us
    all_to_all x1, waiting for transfers between devices, on_device(): returned = lax.all_to_all(grad.reshape(WINS, 8, CH), ('win', 'grp'), 0, 0)  15.5 us
    all_to_all x1, starting transfers between devices, on_device(): moved = lax.all_to_all(white.reshape(WINS, 8, CH), ('win', 'grp'), 0, 0)  14.2 us
    pallas_call x1, Pallas kernels, middle(): pl.pallas_call(middle_kernel, in_specs=[IN_SMEM, IN_VMEM, IN_VMEM], out_s...  11.8 us
    all_to_all x1, starting transfers between devices, on_device(): returned = lax.all_to_all(grad.reshape(WINS, 8, CH), ('win', 'grp'), 0, 0)  9.17 us
    unnamed x20, local copies, waits for them, and re-layouts  7.13 us
  transfers between devices with their start and end apart: 18, of which 17 were waited for; matrix products, arithmetic and copies ran while one was open for 1% of the time, Pallas kernels for 5%

profile of v5, /device:TPU:64, one launch (start us, length us, event | category | flops | bytes accessed | tf_op | source)
XLA Modules:
  0.0 163.7 jit_solution(1934008499884991293)
XLA Ops:
  0.6 1.6 copy-done.2
  2.2 0.9 copy-done.3
  3.2 0.9 copy-done.5
  4.1 0.9 copy-done.7
  5.0 4.1 %forward.1 = (bf16[16,2,8,8,512]{4,3,2,1,0:T(8,128)(2,1)}, f32[8,2,512]{2,1,0:T(2,128)S(1)}) custom-call(bf16[512,2048]{1,0:T(8,128)(2,1)S(1)} %bitcast.96, f32[64,1024]{1,0:T(8,128)S(1)} %copy-done.3, f32[24,1024]{1,0:T(8,128)S(1)} %copy-done.7, f32[24,1024]{1,0:T(8,128)S(1)} %copy-done.5), custom_call_target="tpu_custom_call" | custom-call | flops 2147483648 | bytes 8388608 | tf_op jit(solution)/shard_map/forward/pallas_call | solution.py:155
  9.1 14.2 %all-to-all-start = ((bf16[256,8,512]{2,1,0:T(8,128)(2,1)}), bf16[256,8,512]{2,1,0:T(8,128)(2,1)S(1)}, u32[]{:S(2)}, u32[]{:S(2)}) async-start(bf16[256,8,512]{2,1,0:T(8,128)(2,1)} %bitcast.94), calls=%async_computation | async-start | bytes 4194304 | tf_op jit(solution)/shard_map/all_to_all | solution.py:436
  23.3 0.1 concatenate.3.sc_ref
  23.4 2.8 %copy-done = f32[1,3,16,16,2048]{4,3,2,1,0:T(8,128)S(1)} copy-done((f32[1,3,16,16,2048]{4,3,2,1,0:T(8,128)S(1)}, f32[1,3,16,16,2048]{4,3,2,1,0:T(8,128)}, u32[]{:S(2)}) %copy-start) | copy-done | bytes 6291480
  26.2 1.2 pack_observed.1
  27.5 0.2 collective-permute-start
  27.7 1.4 collective-permute-done
  29.1 1.6 collective-permute-start.1
  30.7 1.8 %collective-permute-start.3 = (bf16[2,4,2,4,8,128]{5,4,3,2,0,1:T(8,128)(2,1)S(1)}, bf16[2,4,2,4,8,128]{5,4,3,2,0,1:T(8,128)(2,1)S(1)}, u32[]{:S(2)}, u32[]{:S(2)}) collective-permute-start(bf16[2,4,2,4,8,128]{5,4,3,2,0,1:T(8,128)(2,1)S(1)} %get-tuple-element.38), channel_id=1, source_target_pairs={{0,48},{8,56},{16,0},{24,8},{32,16},{40,24},{48,32},{56,40},{64,11... | collective-permute-start | bytes 393224 | tf_op jit(solution)/shard_map/ppermute | solution.py:81
  32.5 1.8 %collective-permute-start.2 = (bf16[2,4,2,4,8,128]{5,4,3,2,0,1:T(8,128)(2,1)S(1)}, bf16[2,4,2,4,8,128]{5,4,3,2,0,1:T(8,128)(2,1)S(1)}, u32[]{:S(2)}, u32[]{:S(2)}) collective-permute-start(bf16[2,4,2,4,8,128]{5,4,3,2,0,1:T(8,128)(2,1)S(1)} %get-tuple-element.39), channel_id=1, source_target_pairs={{0,32},{8,40},{16,48},{24,56},{32,0},{40,8},{48,16},{56,24},{64,96... | collective-permute-start | bytes 393224 | tf_op jit(solution)/shard_map/ppermute | solution.py:81
  34.2 4.2 %collective-permute-done.1 = bf16[2,4,2,4,8,128]{5,4,3,2,0,1:T(8,128)(2,1)S(1)} collective-permute-done((bf16[2,4,2,4,8,128]{5,4,3,2,0,1:T(8,128)(2,1)S(1)}, bf16[2,4,2,4,8,128]{5,4,3,2,0,1:T(8,128)(2,1)S(1)}, u32[]{:S(2)}, u32[]{:S(2)}) %collective-permute-start.1) | collective-permute-done | bytes 131104 | tf_op jit(solution)/shard_map/ppermute | solution.py:81
  38.5 3.7 %collective-permute-done.3 = bf16[2,4,2,4,8,128]{5,4,3,2,0,1:T(8,128)(2,1)S(1)} collective-permute-done((bf16[2,4,2,4,8,128]{5,4,3,2,0,1:T(8,128)(2,1)S(1)}, bf16[2,4,2,4,8,128]{5,4,3,2,0,1:T(8,128)(2,1)S(1)}, u32[]{:S(2)}, u32[]{:S(2)}) %collective-permute-start.3) | collective-permute-done | bytes 131104 | tf_op jit(solution)/shard_map/ppermute | solution.py:81
  42.1 2.0 %collective-permute-done.2 = bf16[2,4,2,4,8,128]{5,4,3,2,0,1:T(8,128)(2,1)S(1)} collective-permute-done((bf16[2,4,2,4,8,128]{5,4,3,2,0,1:T(8,128)(2,1)S(1)}, bf16[2,4,2,4,8,128]{5,4,3,2,0,1:T(8,128)(2,1)S(1)}, u32[]{:S(2)}, u32[]{:S(2)}) %collective-permute-start.2) | collective-permute-done | bytes 131104 | tf_op jit(solution)/shard_map/ppermute | solution.py:81
  44.2 2.9 %collective-permute-start.6 = (bf16[4,2,2,4,8,128]{5,4,3,2,1,0:T(8,128)(2,1)S(1)}, bf16[4,2,2,4,8,128]{5,4,3,2,1,0:T(8,128)(2,1)S(1)}, u32[]{:S(2)}, u32[]{:S(2)}) collective-permute-start(bf16[4,2,2,4,8,128]{5,4,3,2,1,0:T(8,128)(2,1)S(1)} %get-tuple-element.33), channel_id=1, source_target_pairs={{0,192},{8,200},{16,208},{24,216},{32,224},{40,232},{48,240},{56,2... | collective-permute-start | bytes 393224 | tf_op jit(solution)/shard_map/ppermute | solution.py:81
  47.2 0.8 collective-permute-start.5
  47.9 0.9 collective-permute-start.4
  48.8 6.8 %collective-permute-done.6 = bf16[4,2,2,4,8,128]{5,4,3,2,1,0:T(8,128)(2,1)S(1)} collective-permute-done((bf16[4,2,2,4,8,128]{5,4,3,2,1,0:T(8,128)(2,1)S(1)}, bf16[4,2,2,4,8,128]{5,4,3,2,1,0:T(8,128)(2,1)S(1)}, u32[]{:S(2)}, u32[]{:S(2)}) %collective-permute-start.6) | collective-permute-done | bytes 131104 | tf_op jit(solution)/shard_map/ppermute | solution.py:81
  55.6 1.7 %collective-permute-done.5 = bf16[4,2,2,4,8,128]{5,4,3,2,1,0:T(8,128)(2,1)S(1)} collective-permute-done((bf16[4,2,2,4,8,128]{5,4,3,2,1,0:T(8,128)(2,1)S(1)}, bf16[4,2,2,4,8,128]{5,4,3,2,1,0:T(8,128)(2,1)S(1)}, u32[]{:S(2)}, u32[]{:S(2)}) %collective-permute-start.5) | collective-permute-done | bytes 131104 | tf_op jit(solution)/shard_map/ppermute | solution.py:81
  57.3 2.1 %collective-permute-done.4 = bf16[4,2,2,4,8,128]{5,4,3,2,1,0:T(8,128)(2,1)S(1)} collective-permute-done((bf16[4,2,2,4,8,128]{5,4,3,2,1,0:T(8,128)(2,1)S(1)}, bf16[4,2,2,4,8,128]{5,4,3,2,1,0:T(8,128)(2,1)S(1)}, u32[]{:S(2)}, u32[]{:S(2)}) %collective-permute-start.4) | collective-permute-done | bytes 131104 | tf_op jit(solution)/shard_map/ppermute | solution.py:81
  59.4 0.1 pad_maximum_fusion.1
  59.5 16.4 %all-to-all-done = bf16[256,8,512]{2,1,0:T(8,128)(2,1)S(1)} async-done(((bf16[256,8,512]{2,1,0:T(8,128)(2,1)}), bf16[256,8,512]{2,1,0:T(8,128)(2,1)S(1)}, u32[]{:S(2)}, u32[]{:S(2)}) %all-to-all-start) | async-done | bytes 2097184 | tf_op jit(solution)/shard_map/all_to_all | solution.py:436
  75.9 11.8 %middle.1 = (bf16[32,2,4,8,128]{4,3,2,1,0:T(8,128)(2,1)S(1)}, bf16[2048,512]{1,0:T(8,128)(2,1)}) custom-call(s32[7]{0:T(128)S(1)} %concatenate.3.sc_ref, bf16[2048,512]{1,0:T(8,128)(2,1)S(1)} %bitcast.93, bf16[32,2,4,8,128]{4,3,2,1,0:T(8,128)(2,1)S(1)} %bitcast.95), custom_call_target="tpu_custom_call" | custom-call | tf_op jit(solution)/shard_map/middle/pallas_call | solution.py:369
  87.8 9.2 %all-to-all-start.1 = ((bf16[256,8,512]{2,1,0:T(8,128)(2,1)}), bf16[256,8,512]{2,1,0:T(8,128)(2,1)}, u32[]{:S(2)}, u32[]{:S(2)}) async-start(bf16[256,8,512]{2,1,0:T(8,128)(2,1)} %bitcast.97), calls=%async_computation.1 | async-start | bytes 4194304 | tf_op jit(solution)/shard_map/all_to_all | solution.py:439
  97.0 0.2 collective-permute-start.7
  97.2 1.4 collective-permute-done.7
  98.7 1.6 collective-permute-start.8
  100.2 1.8 %collective-permute-start.10 = (bf16[2,4,2,4,8,128]{5,4,3,0,2,1:T(8,128)(2,1)S(1)}, bf16[2,4,2,4,8,128]{5,4,3,0,2,1:T(8,128)(2,1)S(1)}, u32[]{:S(2)}, u32[]{:S(2)}) collective-permute-start(bf16[2,4,2,4,8,128]{5,4,3,0,2,1:T(8,128)(2,1)S(1)} %get-tuple-element.28), channel_id=1, source_target_pairs={{0,48},{8,56},{16,0},{24,8},{32,16},{40,24},{48,32},{56,40},{64,11... | collective-permute-start | bytes 393224 | tf_op jit(solution)/shard_map/ppermute | solution.py:81
  102.0 1.8 %collective-permute-start.9 = (bf16[2,4,2,4,8,128]{5,4,3,0,2,1:T(8,128)(2,1)S(1)}, bf16[2,4,2,4,8,128]{5,4,3,0,2,1:T(8,128)(2,1)S(1)}, u32[]{:S(2)}, u32[]{:S(2)}) collective-permute-start(bf16[2,4,2,4,8,128]{5,4,3,0,2,1:T(8,128)(2,1)S(1)} %get-tuple-element.29), channel_id=1, source_target_pairs={{0,32},{8,40},{16,48},{24,56},{32,0},{40,8},{48,16},{56,24},{64,96... | collective-permute-start | bytes 393224 | tf_op jit(solution)/shard_map/ppermute | solution.py:81
  103.8 4.3 %collective-permute-done.8 = bf16[2,4,2,4,8,128]{5,4,3,0,2,1:T(8,128)(2,1)S(1)} collective-permute-done((bf16[2,4,2,4,8,128]{5,4,3,0,2,1:T(8,128)(2,1)S(1)}, bf16[2,4,2,4,8,128]{5,4,3,0,2,1:T(8,128)(2,1)S(1)}, u32[]{:S(2)}, u32[]{:S(2)}) %collective-permute-start.8) | collective-permute-done | bytes 131104 | tf_op jit(solution)/shard_map/ppermute | solution.py:81
  108.1 0.3 collective-permute-done.10
  108.4 4.6 %collective-permute-done.9 = bf16[2,4,2,4,8,128]{5,4,3,0,2,1:T(8,128)(2,1)S(1)} collective-permute-done((bf16[2,4,2,4,8,128]{5,4,3,0,2,1:T(8,128)(2,1)S(1)}, bf16[2,4,2,4,8,128]{5,4,3,0,2,1:T(8,128)(2,1)S(1)}, u32[]{:S(2)}, u32[]{:S(2)}) %collective-permute-start.9) | collective-permute-done | bytes 131104 | tf_op jit(solution)/shard_map/ppermute | solution.py:81
  112.9 0.1 pad_maximum_fusion.2
  113.0 3.0 %collective-permute-start.13 = (bf16[4,2,2,4,8,128]{5,4,3,1,0,2:T(8,128)(2,1)S(1)}, bf16[4,2,2,4,8,128]{5,4,3,1,0,2:T(8,128)(2,1)S(1)}, u32[]{:S(2)}, u32[]{:S(2)}) collective-permute-start(bf16[4,2,2,4,8,128]{5,4,3,1,0,2:T(8,128)(2,1)S(1)} %get-tuple-element.23), channel_id=1, source_target_pairs={{0,192},{8,200},{16,208},{24,216},{32,224},{40,232},{48,240},{56,2... | collective-permute-start | bytes 393224 | tf_op jit(solution)/shard_map/ppermute | solution.py:81
  116.0 0.7 collective-permute-start.12
  116.7 0.9 collective-permute-start.11
  117.6 7.1 %collective-permute-done.13 = bf16[4,2,2,4,8,128]{5,4,3,1,0,2:T(8,128)(2,1)S(1)} collective-permute-done((bf16[4,2,2,4,8,128]{5,4,3,1,0,2:T(8,128)(2,1)S(1)}, bf16[4,2,2,4,8,128]{5,4,3,1,0,2:T(8,128)(2,1)S(1)}, u32[]{:S(2)}, u32[]{:S(2)}) %collective-permute-start.13) | collective-permute-done | bytes 131104 | tf_op jit(solution)/shard_map/ppermute | solution.py:81
  124.8 0.9 collective-permute-done.12
  125.7 3.4 %collective-permute-done.11 = bf16[4,2,2,4,8,128]{5,4,3,1,0,2:T(8,128)(2,1)S(1)} collective-permute-done((bf16[4,2,2,4,8,128]{5,4,3,1,0,2:T(8,128)(2,1)S(1)}, bf16[4,2,2,4,8,128]{5,4,3,1,0,2:T(8,128)(2,1)S(1)}, u32[]{:S(2)}, u32[]{:S(2)}) %collective-permute-start.11) | collective-permute-done | bytes 131104 | tf_op jit(solution)/shard_map/ppermute | solution.py:81
  129.2 0.7 slice_bitcast_fusion
  129.9 5.9 %collective-permute-start.15 = (bf16[32,4,8,128]{3,2,1,0:T(8,128)(2,1)}, bf16[32,4,8,128]{3,2,1,0:T(8,128)(2,1)S(1)}, u32[]{:S(2)}, u32[]{:S(2)}) collective-permute-start(bf16[32,4,8,128]{3,2,1,0:T(8,128)(2,1)} %get-tuple-element.20), channel_id=1, source_target_pairs={{0,5},{1,6},{2,7},{3,0},{4,1},{5,2},{6,3},{7,4},{8,13},{9,14},{10,... | collective-permute-start | bytes 786440 | tf_op jit(solution)/shard_map/ppermute | solution.py:442
  135.8 15.5 %all-to-all-done.1 = bf16[256,8,512]{2,1,0:T(8,128)(2,1)} async-done(((bf16[256,8,512]{2,1,0:T(8,128)(2,1)}), bf16[256,8,512]{2,1,0:T(8,128)(2,1)}, u32[]{:S(2)}, u32[]{:S(2)}) %all-to-all-start.1) | async-done | bytes 2097184 | tf_op jit(solution)/shard_map/all_to_all | solution.py:439
  151.3 6.3 %backward.1 = bf16[512,2048]{1,0:T(8,128)(2,1)} custom-call(bf16[16,2,8,8,512]{4,3,2,1,0:T(8,128)(2,1)} %bitcast.59.g_hbm, bf16[16,2,8,8,512]{4,3,2,1,0:T(8,128)(2,1)S(1)} %copy-done.1, f32[8,2,512]{2,1,0:T(2,128)S(1)} %get-tuple-element.16.r_ref, f32[64,1024]{1,0:T(8,128)S(1)} %copy-done.4, f32[24,1024]{1,0:T(8,128)S(1)} %copy-done.8, f32[24,1024]{1,0:T(8,128)S(1)} %copy-done.6), custom_call_target="tpu_custom_call" | custom-call | flops 2147483648 | bytes 10485760 | tf_op jit(solution)/shard_map/backward/pallas_call | solution.py:221
  157.6 3.8 %collective-permute-done.15.down_ref = bf16[32,4,8,128]{3,2,1,0:T(8,128)(2,1)S(1)} collective-permute-done((bf16[32,4,8,128]{3,2,1,0:T(8,128)(2,1)}, bf16[32,4,8,128]{3,2,1,0:T(8,128)(2,1)S(1)}, u32[]{:S(2)}, u32[]{:S(2)}) %collective-permute-start.15) | collective-permute-done | bytes 262176 | tf_op jit(solution)/shard_map/ppermute | solution.py:442
  161.4 2.2 %unpack_correl.1 = f32[3,16,16,256]{3,2,1,0:T(8,128)} custom-call(s32[7]{0:T(128)S(1)} %concatenate.3.sc_ref, bf16[32,4,8,128]{3,2,1,0:T(8,128)(2,1)S(1)} %collective-permute-done.14.up_ref, bf16[32,4,8,128]{3,2,1,0:T(8,128)(2,1)S(1)} %collective-permute-done.15.down_ref), custom_call_target="tpu_custom_call" | custom-call | tf_op jit(solution)/shard_map/unpack_correl/pallas_call | solution.py:414
  (25 shorter events, 0.4 us)
Async XLA Ops:
  0.6 1.6 copy-start.2
  2.2 0.9 copy-start.3
  3.2 0.9 copy-start.5
  4.1 0.9 copy-start.7
  9.1 14.3 %copy-start.9 = (s32[1,3]{1,0:T(1,128)S(1)}, s32[1,3]{1,0:T(1,128)}, u32[]{:S(2)}) copy-start(s32[1,3]{1,0:T(1,128)} %param.7) | copy-start | bytes 40
  9.1 66.9 %all-to-all-start = ((bf16[256,8,512]{2,1,0:T(8,128)(2,1)}), bf16[256,8,512]{2,1,0:T(8,128)(2,1)S(1)}, u32[]{:S(2)}, u32[]{:S(2)}) async-start(bf16[256,8,512]{2,1,0:T(8,128)(2,1)} %bitcast.94), calls=%async_computation | async-start | bytes 4194304 | tf_op jit(solution)/shard_map/all_to_all | solution.py:436
  23.4 2.8 %copy-start = (f32[1,3,16,16,2048]{4,3,2,1,0:T(8,128)S(1)}, f32[1,3,16,16,2048]{4,3,2,1,0:T(8,128)}, u32[]{:S(2)}) copy-start(f32[1,3,16,16,2048]{4,3,2,1,0:T(8,128)} %param.8) | copy-start | bytes 18874372
  27.5 1.6 collective-permute-start
  29.1 9.3 %collective-permute-start.1 = (bf16[2,4,2,4,8,128]{5,4,3,2,0,1:T(8,128)(2,1)S(1)}, bf16[2,4,2,4,8,128]{5,4,3,2,0,1:T(8,128)(2,1)S(1)}, u32[]{:S(2)}, u32[]{:S(2)}) collective-permute-start(bf16[2,4,2,4,8,128]{5,4,3,2,0,1:T(8,128)(2,1)S(1)} %get-tuple-element.37), channel_id=1, source_target_pairs={{0,16},{8,24},{16,32},{24,40},{32,48},{40,56},{48,0},{56,8},{64,80... | collective-permute-start | bytes 393224 | tf_op jit(solution)/shard_map/ppermute | solution.py:81
  30.7 11.4 %collective-permute-start.3 = (bf16[2,4,2,4,8,128]{5,4,3,2,0,1:T(8,128)(2,1)S(1)}, bf16[2,4,2,4,8,128]{5,4,3,2,0,1:T(8,128)(2,1)S(1)}, u32[]{:S(2)}, u32[]{:S(2)}) collective-permute-start(bf16[2,4,2,4,8,128]{5,4,3,2,0,1:T(8,128)(2,1)S(1)} %get-tuple-element.38), channel_id=1, source_target_pairs={{0,48},{8,56},{16,0},{24,8},{32,16},{40,24},{48,32},{56,40},{64,11... | collective-permute-start | bytes 393224 | tf_op jit(solution)/shard_map/ppermute | solution.py:81
  32.5 11.7 %collective-permute-start.2 = (bf16[2,4,2,4,8,128]{5,4,3,2,0,1:T(8,128)(2,1)S(1)}, bf16[2,4,2,4,8,128]{5,4,3,2,0,1:T(8,128)(2,1)S(1)}, u32[]{:S(2)}, u32[]{:S(2)}) collective-permute-start(bf16[2,4,2,4,8,128]{5,4,3,2,0,1:T(8,128)(2,1)S(1)} %get-tuple-element.39), channel_id=1, source_target_pairs={{0,32},{8,40},{16,48},{24,56},{32,0},{40,8},{48,16},{56,24},{64,96... | collective-permute-start | bytes 393224 | tf_op jit(solution)/shard_map/ppermute | solution.py:81
  44.2 11.3 %collective-permute-start.6 = (bf16[4,2,2,4,8,128]{5,4,3,2,1,0:T(8,128)(2,1)S(1)}, bf16[4,2,2,4,8,128]{5,4,3,2,1,0:T(8,128)(2,1)S(1)}, u32[]{:S(2)}, u32[]{:S(2)}) collective-permute-start(bf16[4,2,2,4,8,128]{5,4,3,2,1,0:T(8,128)(2,1)S(1)} %get-tuple-element.33), channel_id=1, source_target_pairs={{0,192},{8,200},{16,208},{24,216},{32,224},{40,232},{48,240},{56,2... | collective-permute-start | bytes 393224 | tf_op jit(solution)/shard_map/ppermute | solution.py:81
  47.2 10.1 %collective-permute-start.5 = (bf16[4,2,2,4,8,128]{5,4,3,2,1,0:T(8,128)(2,1)S(1)}, bf16[4,2,2,4,8,128]{5,4,3,2,1,0:T(8,128)(2,1)S(1)}, u32[]{:S(2)}, u32[]{:S(2)}) collective-permute-start(bf16[4,2,2,4,8,128]{5,4,3,2,1,0:T(8,128)(2,1)S(1)} %get-tuple-element.34), channel_id=1, source_target_pairs={{0,128},{8,136},{16,144},{24,152},{32,160},{40,168},{48,176},{56,1... | collective-permute-start | bytes 393224 | tf_op jit(solution)/shard_map/ppermute | solution.py:81
  47.9 11.5 %collective-permute-start.4 = (bf16[4,2,2,4,8,128]{5,4,3,2,1,0:T(8,128)(2,1)S(1)}, bf16[4,2,2,4,8,128]{5,4,3,2,1,0:T(8,128)(2,1)S(1)}, u32[]{:S(2)}, u32[]{:S(2)}) collective-permute-start(bf16[4,2,2,4,8,128]{5,4,3,2,1,0:T(8,128)(2,1)S(1)} %get-tuple-element.35), channel_id=1, source_target_pairs={{0,64},{8,72},{16,80},{24,88},{32,96},{40,104},{48,112},{56,120},{... | collective-permute-start | bytes 393224 | tf_op jit(solution)/shard_map/ppermute | solution.py:81
  87.8 63.6 %all-to-all-start.1 = ((bf16[256,8,512]{2,1,0:T(8,128)(2,1)}), bf16[256,8,512]{2,1,0:T(8,128)(2,1)}, u32[]{:S(2)}, u32[]{:S(2)}) async-start(bf16[256,8,512]{2,1,0:T(8,128)(2,1)} %bitcast.97), calls=%async_computation.1 | async-start | bytes 4194304 | tf_op jit(solution)/shard_map/all_to_all | solution.py:439
  97.0 1.6 collective-permute-start.7
  98.7 9.5 %collective-permute-start.8 = (bf16[2,4,2,4,8,128]{5,4,3,0,2,1:T(8,128)(2,1)S(1)}, bf16[2,4,2,4,8,128]{5,4,3,0,2,1:T(8,128)(2,1)S(1)}, u32[]{:S(2)}, u32[]{:S(2)}) collective-permute-start(bf16[2,4,2,4,8,128]{5,4,3,0,2,1:T(8,128)(2,1)S(1)} %get-tuple-element.27), channel_id=1, source_target_pairs={{0,16},{8,24},{16,32},{24,40},{32,48},{40,56},{48,0},{56,8},{64,80... | collective-permute-start | bytes 393224 | tf_op jit(solution)/shard_map/ppermute | solution.py:81
  100.2 8.1 %collective-permute-start.10 = (bf16[2,4,2,4,8,128]{5,4,3,0,2,1:T(8,128)(2,1)S(1)}, bf16[2,4,2,4,8,128]{5,4,3,0,2,1:T(8,128)(2,1)S(1)}, u32[]{:S(2)}, u32[]{:S(2)}) collective-permute-start(bf16[2,4,2,4,8,128]{5,4,3,0,2,1:T(8,128)(2,1)S(1)} %get-tuple-element.28), channel_id=1, source_target_pairs={{0,48},{8,56},{16,0},{24,8},{32,16},{40,24},{48,32},{56,40},{64,11... | collective-permute-start | bytes 393224 | tf_op jit(solution)/shard_map/ppermute | solution.py:81
  102.0 10.9 %collective-permute-start.9 = (bf16[2,4,2,4,8,128]{5,4,3,0,2,1:T(8,128)(2,1)S(1)}, bf16[2,4,2,4,8,128]{5,4,3,0,2,1:T(8,128)(2,1)S(1)}, u32[]{:S(2)}, u32[]{:S(2)}) collective-permute-start(bf16[2,4,2,4,8,128]{5,4,3,0,2,1:T(8,128)(2,1)S(1)} %get-tuple-element.29), channel_id=1, source_target_pairs={{0,32},{8,40},{16,48},{24,56},{32,0},{40,8},{48,16},{56,24},{64,96... | collective-permute-start | bytes 393224 | tf_op jit(solution)/shard_map/ppermute | solution.py:81
  112.9 38.4 %copy-start.1 = (bf16[16,2,8,8,512]{4,3,2,1,0:T(8,128)(2,1)S(1)}, bf16[16,2,8,8,512]{4,3,2,1,0:T(8,128)(2,1)}, u32[]{:S(2)}) copy-start(bf16[16,2,8,8,512]{4,3,2,1,0:T(8,128)(2,1)} %get-tuple-element.13.y_ref) | copy-start | bytes 6291460
  112.9 38.4 %copy-start.4 = (f32[64,1024]{1,0:T(8,128)S(1)}, f32[64,1024]{1,0:T(8,128)}, u32[]{:S(2)}) copy-start(f32[64,1024]{1,0:T(8,128)} %constant.41.clone.a_ref) | copy-start | bytes 786436
  112.9 38.4 %copy-start.6 = (f32[24,1024]{1,0:T(8,128)S(1)}, f32[24,1024]{1,0:T(8,128)}, u32[]{:S(2)}) copy-start(f32[24,1024]{1,0:T(8,128)} %constant.43.clone.s_ref) | copy-start | bytes 294916
  112.9 38.4 %copy-start.8 = (f32[24,1024]{1,0:T(8,128)S(1)}, f32[24,1024]{1,0:T(8,128)}, u32[]{:S(2)}) copy-start(f32[24,1024]{1,0:T(8,128)} %constant.42.clone.c_ref) | copy-start | bytes 294916
  113.0 11.7 %collective-permute-start.13 = (bf16[4,2,2,4,8,128]{5,4,3,1,0,2:T(8,128)(2,1)S(1)}, bf16[4,2,2,4,8,128]{5,4,3,1,0,2:T(8,128)(2,1)S(1)}, u32[]{:S(2)}, u32[]{:S(2)}) collective-permute-start(bf16[4,2,2,4,8,128]{5,4,3,1,0,2:T(8,128)(2,1)S(1)} %get-tuple-element.23), channel_id=1, source_target_pairs={{0,192},{8,200},{16,208},{24,216},{32,224},{40,232},{48,240},{56,2... | collective-permute-start | bytes 393224 | tf_op jit(solution)/shard_map/ppermute | solution.py:81
  116.0 9.7 %collective-permute-start.12 = (bf16[4,2,2,4,8,128]{5,4,3,1,0,2:T(8,128)(2,1)S(1)}, bf16[4,2,2,4,8,128]{5,4,3,1,0,2:T(8,128)(2,1)S(1)}, u32[]{:S(2)}, u32[]{:S(2)}) collective-permute-start(bf16[4,2,2,4,8,128]{5,4,3,1,0,2:T(8,128)(2,1)S(1)} %get-tuple-element.24), channel_id=1, source_target_pairs={{0,128},{8,136},{16,144},{24,152},{32,160},{40,168},{48,176},{56,1... | collective-permute-start | bytes 393224 | tf_op jit(solution)/shard_map/ppermute | solution.py:81
  116.7 12.4 %collective-permute-start.11 = (bf16[4,2,2,4,8,128]{5,4,3,1,0,2:T(8,128)(2,1)S(1)}, bf16[4,2,2,4,8,128]{5,4,3,1,0,2:T(8,128)(2,1)S(1)}, u32[]{:S(2)}, u32[]{:S(2)}) collective-permute-start(bf16[4,2,2,4,8,128]{5,4,3,1,0,2:T(8,128)(2,1)S(1)} %get-tuple-element.25), channel_id=1, source_target_pairs={{0,64},{8,72},{16,80},{24,88},{32,96},{40,104},{48,112},{56,120},{... | collective-permute-start | bytes 393224 | tf_op jit(solution)/shard_map/ppermute | solution.py:81
  129.9 31.5 %collective-permute-start.15 = (bf16[32,4,8,128]{3,2,1,0:T(8,128)(2,1)}, bf16[32,4,8,128]{3,2,1,0:T(8,128)(2,1)S(1)}, u32[]{:S(2)}, u32[]{:S(2)}) collective-permute-start(bf16[32,4,8,128]{3,2,1,0:T(8,128)(2,1)} %get-tuple-element.20), channel_id=1, source_target_pairs={{0,5},{1,6},{2,7},{3,0},{4,1},{5,2},{6,3},{7,4},{8,13},{9,14},{10,... | collective-permute-start | bytes 786440 | tf_op jit(solution)/shard_map/ppermute | solution.py:442
  135.8 25.6 %collective-permute-start.14 = (bf16[32,4,8,128]{3,2,1,0:T(8,128)(2,1)S(1)}, bf16[32,4,8,128]{3,2,1,0:T(8,128)(2,1)S(1)}, u32[]{:S(2)}, u32[]{:S(2)}) collective-permute-start(bf16[32,4,8,128]{3,2,1,0:T(8,128)(2,1)S(1)} %get-tuple-element.21), channel_id=1, source_target_pairs={{0,1},{1,2},{2,3},{3,4},{4,5},{5,6},{6,7},{7,0},{8,9},{9,10},{10,1... | collective-permute-start | bytes 786440 | tf_op jit(solution)/shard_map/ppermute | solution.py:441

commit v6 on v5

--- a/solution.py
+++ b/solution.py
@@ -113,21 +113,37 @@
     return (q * 4 + h * 2, q * 4 + h * 2 + 1)
 
 
-def forward_kernel(x_ref, a_ref, c_ref, s_ref, y_hbm, r_ref, y_ref, sem):
-    copies = []
-    early = x_ref[:, : SEG // 2].astype(F32)
-    late = x_ref[:, SEG // 2 :].astype(F32)
+def forward_kernel(x_hbm, a_hbm, c_hbm, s_hbm, y_hbm, r_ref, x_ref, a_ref, c_ref, s_ref, y_ref, sem):
+    pieces = [(a_hbm, a_ref), (c_hbm, c_ref), (s_hbm, s_ref)]
+    for i in range(4):
+        rows = slice(i * 128, (i + 1) * 128)
+        pieces.append((x_hbm.at[rows, :], x_ref.at[rows, :]))
+    loads = [pltpu.make_async_copy(src, dst, sem.at[4 + i]) for i, (src, dst) in enumerate(pieces)]
+    for load in loads:
+        load.start()
+    for load in loads[:3]:
+        load.wait()
     pairs = band_pairs(a_ref, c_ref, s_ref, slice(None))
-    halves = ((early + late).astype(BF16), (early - late).astype(BF16))
-    for step in range(4):
-        waves = []
-        for p in range(2):
-            a, b = pairs[p]
+
+    def tables(step):
+        for a, b in pairs:
             parts = []
             for g in (step * 2, step * 2 + 1):
                 for band in plane_bands(g):
                     parts.append((a * c_ref[band : band + 1, :] + b * s_ref[band : band + 1, :]).astype(BF16))
-            waves.append(dot(jnp.concatenate(parts, axis=0), halves[p], 1, 1))
+            yield jnp.concatenate(parts, axis=0)
+
+    ahead = list(tables(0))
+    for load in loads[3:]:
+        load.wait()
+    early = x_ref[:, : SEG // 2].astype(F32)
+    late = x_ref[:, SEG // 2 :].astype(F32)
+    halves = ((early + late).astype(BF16), (early - late).astype(BF16))
+    copies = []
+    for step in range(4):
+        waves = [dot(ahead[p], halves[p], 1, 1) for p in range(2)]
+        if step < 3:
+            ahead = list(tables(step + 1))
         for gi in range(2):
             for wh in range(2):
                 row = (gi * 2 + wh) * 64
@@ -146,25 +162,32 @@
         copy.wait()
 
 
+IN_HBM = pl.BlockSpec(memory_space=pltpu.HBM)
 IN_VMEM = pl.BlockSpec(memory_space=pltpu.VMEM)
-IN_HBM = pl.BlockSpec(memory_space=pltpu.HBM)
 IN_SMEM = pl.BlockSpec(memory_space=pltpu.SMEM)
 
 
 def forward(x, consts):
     return pl.pallas_call(
         forward_kernel,
-        in_specs=[IN_VMEM] * 4,
+        in_specs=[IN_HBM] * 4,
         out_specs=[IN_HBM, IN_VMEM],
         out_shape=[
             pltpu.HBM((16, 2, GRP, 8, CH), BF16),
             jax.ShapeDtypeStruct((GRP, 2, CH), F32),
         ],
-        scratch_shapes=[pltpu.VMEM((16, 2, GRP, 8, CH), BF16), pltpu.SemaphoreType.DMA((4,))],
+        scratch_shapes=[
+            pltpu.VMEM((CH, SEG), BF16),
+            pltpu.VMEM((BAND, SEG // 2), F32),
+            pltpu.VMEM((24, SEG // 2), F32),
+            pltpu.VMEM((24, SEG // 2), F32),
+            pltpu.VMEM((16, 2, GRP, 8, CH), BF16),
+            pltpu.SemaphoreType.DMA((11,)),
+        ],
         compiler_params=pltpu.CompilerParams(vmem_limit_bytes=VMEM_LIMIT),
         cost_estimate=pl.CostEstimate(flops=CH * SEG * SEG, bytes_accessed=8 << 20, transcendentals=0),
         name="forward",
-    )(x, *consts)
+    )(*(pltpu.with_memory_space_constraint(v, pltpu.HBM) for v in (x, *consts)))
 
 
 def backward_kernel(g_hbm, y_ref, r_ref, a_ref, c_ref, s_ref, o_ref, g_ref, d_ref, stage_ref, sem):
@@ -284,68 +307,74 @@
     lane8 = lax.broadcasted_iota(jnp.int32, (8, LANES), 1)
     lane16 = lax.broadcasted_iota(jnp.int32, (16, LANES), 1)
 
-    def one_bin(k):
-        later = None
-        for b in range(4):
-            width = 2 if b < 3 else 1
-            cols = slice(b * LANES, (b + width) * LANES)
-            lead = u_ref[k, :, b * LANES : (b + 1) * LANES]
-            re_rows = u_ref[k, :WINS, cols]
-            im_rows = u_ref[k, WINS:, cols]
-            straight = jnp.concatenate([re_rows, im_rows], axis=0)
-            crossed = jnp.concatenate([im_rows, -re_rows], axis=0)
-            gram = dot(lead.T, jnp.concatenate([straight, crossed], axis=1))
-            tiles = ([], [])
-            for blk in range(8):
-                a, shift = b * 8 + blk, blk * CB
-                for ri in range(2):
-                    base = ri * width * LANES
-                    here = gram[shift : shift + 16, base : base + LANES]
-                    if shift > 0:
-                        if shift > HALF and width == 2:
-                            there = gram[shift : shift + 16, base + LANES : base + 2 * LANES]
-                            here = jnp.where(lane16 >= shift, here, there)
-                        here = pltpu.roll(here, LANES - shift, 1)
-                    packed = jnp.where(lane8 < HALF, here[:8], pltpu.roll(here[8:], HALF, 1))
-                    packed = packed * (1.0 / WINS)
-                    seen = obs_ref[source_slot(me, a), ri, k].astype(F32)
-                    live = seen < EMPTY / 2
-                    slot = 1 - half if ri == 0 else half
-                    corr_ref[target_slot(me, a), slot, k] = packed.astype(BF16)
-                    resid = jnp.where(live, packed - seen, 0.0)
-                    spread = jnp.concatenate([resid, pltpu.roll(resid, HALF, 1)], axis=0)
-                    spread = jnp.where(lane16 < HALF, spread, 0.0)
-                    if shift > 0:
-                        spread = pltpu.roll(spread, shift, 1)
-                    if shift > HALF:
-                        first = jnp.where(lane16 >= shift, spread, 0.0)
-                        second = jnp.where(lane16 < shift, spread, 0.0)
-                    else:
-                        first, second = spread, jnp.zeros_like(spread)
-                    tiles[ri].append([first, second][:width])
-            res = [
-                [jnp.concatenate([t[p] for t in tiles[ri]], axis=0).astype(BF16) for p in range(width)]
-                for ri in range(2)
-            ]
-            top = jnp.concatenate([m for p in range(width) for m in (res[0][p], res[1][p])], axis=1)
-            low = jnp.concatenate([m for p in range(width) for m in (-res[1][p], res[0][p])], axis=1)
-            weights = jnp.concatenate([top, low], axis=0)
-            waves = [
-                u_ref[k, ri * WINS : (ri + 1) * WINS, (b + p) * LANES : (b + p + 1) * LANES]
-                for p in range(width)
-                for ri in range(2)
-            ]
-            pulled = dot(jnp.concatenate(waves, axis=1), weights, 1, 1)
-            pushed = dot(jnp.concatenate(waves[:2], axis=1), weights)
-            grad = pulled + pushed[:, :256]
-            if later is not None:
-                grad = grad + later
-            later = pushed[:, 256:] if width == 2 else None
-            d_ref[k, :WINS, b * LANES : (b + 1) * LANES] = grad[:, :LANES].astype(BF16)
-            d_ref[k, WINS:, b * LANES : (b + 1) * LANES] = grad[:, LANES:].astype(BF16)
-
-    for k in range(KB):
-        one_bin(k)
+    def correlate(k, b, width):
+        cols = slice(b * LANES, (b + width) * LANES)
+        lead = u_ref[k, :, b * LANES : (b + 1) * LANES]
+        re_rows = u_ref[k, :WINS, cols]
+        im_rows = u_ref[k, WINS:, cols]
+        straight = jnp.concatenate([re_rows, im_rows], axis=0)
+        crossed = jnp.concatenate([im_rows, -re_rows], axis=0)
+        return dot(lead.T, jnp.concatenate([straight, crossed], axis=1))
+
+    def weigh(k, b, width, gram):
+        tiles = ([], [])
+        for blk in range(8):
+            a, shift = b * 8 + blk, blk * CB
+            source, target = source_slot(me, a), target_slot(me, a)
+            for ri in range(2):
+                base = ri * width * LANES
+                here = gram[shift : shift + 16, base : base + LANES]
+                if shift > 0:
+                    if shift > HALF and width == 2:
+                        there = gram[shift : shift + 16, base + LANES : base + 2 * LANES]
+                        here = jnp.where(lane16 >= shift, here, there)
+                    here = pltpu.roll(here, LANES - shift, 1)
+                packed = jnp.where(lane8 < HALF, here[:8], pltpu.roll(here[8:], HALF, 1))
+                packed = packed * (1.0 / WINS)
+                seen = obs_ref[source, ri, k].astype(F32)
+                corr_ref[target, 1 - half if ri == 0 else half, k] = packed.astype(BF16)
+                resid = jnp.where(seen < EMPTY / 2, packed - seen, 0.0)
+                spread = jnp.concatenate([resid, pltpu.roll(resid, HALF, 1)], axis=0)
+                spread = jnp.where(lane16 < HALF, spread, 0.0)
+                if shift > 0:
+                    spread = pltpu.roll(spread, shift, 1)
+                if shift > HALF:
+                    first = jnp.where(lane16 >= shift, spread, 0.0)
+                    second = jnp.where(lane16 < shift, spread, 0.0)
+                else:
+                    first, second = spread, jnp.zeros_like(spread)
+                tiles[ri].append([first, second][:width])
+        res = [
+            [jnp.concatenate([t[p] for t in tiles[ri]], axis=0).astype(BF16) for p in range(width)]
+            for ri in range(2)
+        ]
+        top = jnp.concatenate([m for p in range(width) for m in (res[0][p], res[1][p])], axis=1)
+        low = jnp.concatenate([m for p in range(width) for m in (-res[1][p], res[0][p])], axis=1)
+        return jnp.concatenate([top, low], axis=0)
+
+    def pull(k, b, width, weights, later):
+        waves = [
+            u_ref[k, ri * WINS : (ri + 1) * WINS, (b + p) * LANES : (b + p + 1) * LANES]
+            for p in range(width)
+            for ri in range(2)
+        ]
+        pushed = dot(jnp.concatenate(waves[:2], axis=1), weights)
+        grad = dot(jnp.concatenate(waves, axis=1), weights, 1, 1) + pushed[:, :256]
+        if b > 0:
+            grad = grad + later
+        d_ref[k, :WINS, b * LANES : (b + 1) * LANES] = grad[:, :LANES].astype(BF16)
+        d_ref[k, WINS:, b * LANES : (b + 1) * LANES] = grad[:, LANES:].astype(BF16)
+        return pushed[:, 256:]
+
+    steps = [(k, b, 2 if b < 3 else 1) for k in range(KB) for b in range(4)]
+    gram, weights, later = correlate(*steps[0]), None, None
+    for i in range(len(steps) + 1):
+        ahead = correlate(*steps[i + 1]) if i + 1 < len(steps) else None
+        if i > 0:
+            later = pull(*steps[i - 1], weights, later)
+        if i < len(steps):
+            weights = weigh(*steps[i], gram)
+        gram = ahead
     back = regroup(True)
     copies = []
     for gr in range(8):

time: 164 us -> 158 us (0.963)
  local copies, waits for them, and re-layouts: 8.1 us -> 3.78 us
    unnamed x20 -> x12, local copies, waits for them, and re-layouts: 7.13 us -> 2.81 us
    pallas_call x1, Pallas kernels: 11.8 us -> 9.04 us  [middle(): pl.pallas_call(middle_kernel, in_specs=[IN_SMEM, IN_VMEM, IN_VMEM], out_s...]
where the time goes in v6:
time: 158 us
  waiting for transfers between devices  79.6 us (50%)
  starting transfers between devices  49.1 us (31%)
  Pallas kernels  24.3 us (15%)
  local copies, waits for them, and re-layouts  3.78 us (2%)
    ppermute x14, waiting for transfers between devices, hop(): return lax.ppermute(array, 'win', pairs)  43.9 us
    ppermute x14, starting transfers between devices, hop(): return lax.ppermute(array, 'win', pairs)  19.9 us
    all_to_all x1, waiting for transfers between devices, on_device(): moved = lax.all_to_all(white.reshape(WINS, 8, CH), ('win', 'grp'), 0, 0)  16.4 us
    all_to_all x1, waiting for transfers between devices, on_device(): returned = lax.all_to_all(grad.reshape(WINS, 8, CH), ('win', 'grp'), 0, 0)  15.5 us
    all_to_all x1, starting transfers between devices, on_device(): moved = lax.all_to_all(white.reshape(WINS, 8, CH), ('win', 'grp'), 0, 0)  14.2 us
    all_to_all x1, starting transfers between devices, on_device(): returned = lax.all_to_all(grad.reshape(WINS, 8, CH), ('win', 'grp'), 0, 0)  9.17 us
    pallas_call x1, Pallas kernels, middle(): pl.pallas_call(middle_kernel, in_specs=[IN_SMEM, IN_VMEM, IN_VMEM], out_s...  9.04 us
    pallas_call x1, Pallas kernels, backward(): pl.pallas_call(backward_kernel, in_specs=[IN_HBM] + [IN_VMEM] * 5, out_sp...  6.25 us
  transfers between devices with their start and end apart: 18, of which 17 were waited for; matrix products, arithmetic and copies ran while one was open for 1% of the time, Pallas kernels for 5%

profile of v6, /device:TPU:64, one launch (start us, length us, event | category | flops | bytes accessed | tf_op | source)
XLA Modules:
  0.0 158.0 jit_solution(5039616061901507140)
XLA Ops:
  0.6 5.6 %forward.1 = (bf16[16,2,8,8,512]{4,3,2,1,0:T(8,128)(2,1)}, f32[8,2,512]{2,1,0:T(2,128)S(1)}) custom-call(bf16[512,2048]{1,0:T(8,128)(2,1)} %bitcast.118, f32[64,1024]{1,0:T(8,128)} %constant.41.clone.a_hbm.a_ref, f32[24,1024]{1,0:T(8,128)} %constant.42.clone.c_hbm.c_ref, f32[24,1024]{1,0:T(8,128)} %constant.43.clone.s_hbm.s_ref), custom_call_target="tpu_custom_call" | custom-call | flops 2147483648 | bytes 8388608 | tf_op jit(solution)/shard_map/forward/pallas_call | solution.py:171
  6.2 0.0 copy-start.5
  6.3 14.2 %all-to-all-start = ((bf16[256,8,512]{2,1,0:T(8,128)(2,1)}), bf16[256,8,512]{2,1,0:T(8,128)(2,1)S(1)}, u32[]{:S(2)}, u32[]{:S(2)}) async-start(bf16[256,8,512]{2,1,0:T(8,128)(2,1)} %bitcast.94), calls=%async_computation | async-start | bytes 4194304 | tf_op jit(solution)/shard_map/all_to_all | solution.py:465
  20.5 0.1 concatenate.3.sc_ref
  20.6 2.8 %copy-done = f32[1,3,16,16,2048]{4,3,2,1,0:T(8,128)S(1)} copy-done((f32[1,3,16,16,2048]{4,3,2,1,0:T(8,128)S(1)}, f32[1,3,16,16,2048]{4,3,2,1,0:T(8,128)}, u32[]{:S(2)}) %copy-start) | copy-done | bytes 6291480
  23.4 1.2 pack_observed.1
  24.6 0.2 collective-permute-start
  24.9 1.4 collective-permute-done
  26.3 1.6 collective-permute-start.1
  27.9 1.8 %collective-permute-start.3 = (bf16[2,4,2,4,8,128]{5,4,3,2,0,1:T(8,128)(2,1)S(1)}, bf16[2,4,2,4,8,128]{5,4,3,2,0,1:T(8,128)(2,1)S(1)}, u32[]{:S(2)}, u32[]{:S(2)}) collective-permute-start(bf16[2,4,2,4,8,128]{5,4,3,2,0,1:T(8,128)(2,1)S(1)} %get-tuple-element.38), channel_id=1, source_target_pairs={{0,48},{8,56},{16,0},{24,8},{32,16},{40,24},{48,32},{56,40},{64,11... | collective-permute-start | bytes 393224 | tf_op jit(solution)/shard_map/ppermute | solution.py:81
  29.6 1.8 %collective-permute-start.2 = (bf16[2,4,2,4,8,128]{5,4,3,2,0,1:T(8,128)(2,1)S(1)}, bf16[2,4,2,4,8,128]{5,4,3,2,0,1:T(8,128)(2,1)S(1)}, u32[]{:S(2)}, u32[]{:S(2)}) collective-permute-start(bf16[2,4,2,4,8,128]{5,4,3,2,0,1:T(8,128)(2,1)S(1)} %get-tuple-element.39), channel_id=1, source_target_pairs={{0,32},{8,40},{16,48},{24,56},{32,0},{40,8},{48,16},{56,24},{64,96... | collective-permute-start | bytes 393224 | tf_op jit(solution)/shard_map/ppermute | solution.py:81
  31.4 4.2 %collective-permute-done.1 = bf16[2,4,2,4,8,128]{5,4,3,2,0,1:T(8,128)(2,1)S(1)} collective-permute-done((bf16[2,4,2,4,8,128]{5,4,3,2,0,1:T(8,128)(2,1)S(1)}, bf16[2,4,2,4,8,128]{5,4,3,2,0,1:T(8,128)(2,1)S(1)}, u32[]{:S(2)}, u32[]{:S(2)}) %collective-permute-start.1) | collective-permute-done | bytes 131104 | tf_op jit(solution)/shard_map/ppermute | solution.py:81
  35.6 3.7 %collective-permute-done.3 = bf16[2,4,2,4,8,128]{5,4,3,2,0,1:T(8,128)(2,1)S(1)} collective-permute-done((bf16[2,4,2,4,8,128]{5,4,3,2,0,1:T(8,128)(2,1)S(1)}, bf16[2,4,2,4,8,128]{5,4,3,2,0,1:T(8,128)(2,1)S(1)}, u32[]{:S(2)}, u32[]{:S(2)}) %collective-permute-start.3) | collective-permute-done | bytes 131104 | tf_op jit(solution)/shard_map/ppermute | solution.py:81
  39.3 2.0 %collective-permute-done.2 = bf16[2,4,2,4,8,128]{5,4,3,2,0,1:T(8,128)(2,1)S(1)} collective-permute-done((bf16[2,4,2,4,8,128]{5,4,3,2,0,1:T(8,128)(2,1)S(1)}, bf16[2,4,2,4,8,128]{5,4,3,2,0,1:T(8,128)(2,1)S(1)}, u32[]{:S(2)}, u32[]{:S(2)}) %collective-permute-start.2) | collective-permute-done | bytes 131104 | tf_op jit(solution)/shard_map/ppermute | solution.py:81
  41.3 0.1 pad_maximum_fusion
  41.4 2.9 %collective-permute-start.6 = (bf16[4,2,2,4,8,128]{5,4,3,2,1,0:T(8,128)(2,1)S(1)}, bf16[4,2,2,4,8,128]{5,4,3,2,1,0:T(8,128)(2,1)S(1)}, u32[]{:S(2)}, u32[]{:S(2)}) collective-permute-start(bf16[4,2,2,4,8,128]{5,4,3,2,1,0:T(8,128)(2,1)S(1)} %get-tuple-element.33), channel_id=1, source_target_pairs={{0,192},{8,200},{16,208},{24,216},{32,224},{40,232},{48,240},{56,2... | collective-permute-start | bytes 393224 | tf_op jit(solution)/shard_map/ppermute | solution.py:81
  44.3 0.8 collective-permute-start.5
  45.1 0.9 collective-permute-start.4
  46.0 6.8 %collective-permute-done.6 = bf16[4,2,2,4,8,128]{5,4,3,2,1,0:T(8,128)(2,1)S(1)} collective-permute-done((bf16[4,2,2,4,8,128]{5,4,3,2,1,0:T(8,128)(2,1)S(1)}, bf16[4,2,2,4,8,128]{5,4,3,2,1,0:T(8,128)(2,1)S(1)}, u32[]{:S(2)}, u32[]{:S(2)}) %collective-permute-start.6) | collective-permute-done | bytes 131104 | tf_op jit(solution)/shard_map/ppermute | solution.py:81
  52.8 1.7 %collective-permute-done.5 = bf16[4,2,2,4,8,128]{5,4,3,2,1,0:T(8,128)(2,1)S(1)} collective-permute-done((bf16[4,2,2,4,8,128]{5,4,3,2,1,0:T(8,128)(2,1)S(1)}, bf16[4,2,2,4,8,128]{5,4,3,2,1,0:T(8,128)(2,1)S(1)}, u32[]{:S(2)}, u32[]{:S(2)}) %collective-permute-start.5) | collective-permute-done | bytes 131104 | tf_op jit(solution)/shard_map/ppermute | solution.py:81
  54.5 2.1 %collective-permute-done.4 = bf16[4,2,2,4,8,128]{5,4,3,2,1,0:T(8,128)(2,1)S(1)} collective-permute-done((bf16[4,2,2,4,8,128]{5,4,3,2,1,0:T(8,128)(2,1)S(1)}, bf16[4,2,2,4,8,128]{5,4,3,2,1,0:T(8,128)(2,1)S(1)}, u32[]{:S(2)}, u32[]{:S(2)}) %collective-permute-start.4) | collective-permute-done | bytes 131104 | tf_op jit(solution)/shard_map/ppermute | solution.py:81
  56.6 0.1 pad_maximum_fusion.1
  56.7 16.4 %all-to-all-done = bf16[256,8,512]{2,1,0:T(8,128)(2,1)S(1)} async-done(((bf16[256,8,512]{2,1,0:T(8,128)(2,1)}), bf16[256,8,512]{2,1,0:T(8,128)(2,1)S(1)}, u32[]{:S(2)}, u32[]{:S(2)}) %all-to-all-start) | async-done | bytes 2097184 | tf_op jit(solution)/shard_map/all_to_all | solution.py:465
  73.1 9.0 %middle.1 = (bf16[32,2,4,8,128]{4,3,2,1,0:T(8,128)(2,1)S(1)}, bf16[2048,512]{1,0:T(8,128)(2,1)}) custom-call(s32[7]{0:T(128)S(1)} %concatenate.3.sc_ref, bf16[2048,512]{1,0:T(8,128)(2,1)S(1)} %bitcast.93, bf16[32,2,4,8,128]{4,3,2,1,0:T(8,128)(2,1)S(1)} %bitcast.95), custom_call_target="tpu_custom_call" | custom-call | tf_op jit(solution)/shard_map/middle/pallas_call | solution.py:398
  82.2 9.2 %all-to-all-start.1 = ((bf16[256,8,512]{2,1,0:T(8,128)(2,1)}), bf16[256,8,512]{2,1,0:T(8,128)(2,1)}, u32[]{:S(2)}, u32[]{:S(2)}) async-start(bf16[256,8,512]{2,1,0:T(8,128)(2,1)} %bitcast.96), calls=%async_computation.1 | async-start | bytes 4194304 | tf_op jit(solution)/shard_map/all_to_all | solution.py:468
  91.4 0.2 collective-permute-start.7
  91.6 1.4 collective-permute-done.7
  93.0 1.6 collective-permute-start.8
  94.6 1.8 %collective-permute-start.10 = (bf16[2,4,2,4,8,128]{5,4,3,0,2,1:T(8,128)(2,1)S(1)}, bf16[2,4,2,4,8,128]{5,4,3,0,2,1:T(8,128)(2,1)S(1)}, u32[]{:S(2)}, u32[]{:S(2)}) collective-permute-start(bf16[2,4,2,4,8,128]{5,4,3,0,2,1:T(8,128)(2,1)S(1)} %get-tuple-element.28), channel_id=1, source_target_pairs={{0,48},{8,56},{16,0},{24,8},{32,16},{40,24},{48,32},{56,40},{64,11... | collective-permute-start | bytes 393224 | tf_op jit(solution)/shard_map/ppermute | solution.py:81
  96.4 1.8 %collective-permute-start.9 = (bf16[2,4,2,4,8,128]{5,4,3,0,2,1:T(8,128)(2,1)S(1)}, bf16[2,4,2,4,8,128]{5,4,3,0,2,1:T(8,128)(2,1)S(1)}, u32[]{:S(2)}, u32[]{:S(2)}) collective-permute-start(bf16[2,4,2,4,8,128]{5,4,3,0,2,1:T(8,128)(2,1)S(1)} %get-tuple-element.29), channel_id=1, source_target_pairs={{0,32},{8,40},{16,48},{24,56},{32,0},{40,8},{48,16},{56,24},{64,96... | collective-permute-start | bytes 393224 | tf_op jit(solution)/shard_map/ppermute | solution.py:81
  98.2 4.3 %collective-permute-done.8 = bf16[2,4,2,4,8,128]{5,4,3,0,2,1:T(8,128)(2,1)S(1)} collective-permute-done((bf16[2,4,2,4,8,128]{5,4,3,0,2,1:T(8,128)(2,1)S(1)}, bf16[2,4,2,4,8,128]{5,4,3,0,2,1:T(8,128)(2,1)S(1)}, u32[]{:S(2)}, u32[]{:S(2)}) %collective-permute-start.8) | collective-permute-done | bytes 131104 | tf_op jit(solution)/shard_map/ppermute | solution.py:81
  102.5 0.3 collective-permute-done.10
  102.8 4.6 %collective-permute-done.9 = bf16[2,4,2,4,8,128]{5,4,3,0,2,1:T(8,128)(2,1)S(1)} collective-permute-done((bf16[2,4,2,4,8,128]{5,4,3,0,2,1:T(8,128)(2,1)S(1)}, bf16[2,4,2,4,8,128]{5,4,3,0,2,1:T(8,128)(2,1)S(1)}, u32[]{:S(2)}, u32[]{:S(2)}) %collective-permute-start.9) | collective-permute-done | bytes 131104 | tf_op jit(solution)/shard_map/ppermute | solution.py:81
  107.3 0.1 pad_maximum_fusion.2
  107.4 3.0 %collective-permute-start.13 = (bf16[4,2,2,4,8,128]{5,4,3,1,0,2:T(8,128)(2,1)S(1)}, bf16[4,2,2,4,8,128]{5,4,3,1,0,2:T(8,128)(2,1)S(1)}, u32[]{:S(2)}, u32[]{:S(2)}) collective-permute-start(bf16[4,2,2,4,8,128]{5,4,3,1,0,2:T(8,128)(2,1)S(1)} %get-tuple-element.23), channel_id=1, source_target_pairs={{0,192},{8,200},{16,208},{24,216},{32,224},{40,232},{48,240},{56,2... | collective-permute-start | bytes 393224 | tf_op jit(solution)/shard_map/ppermute | solution.py:81
  110.4 0.7 collective-permute-start.12
  111.1 0.9 collective-permute-start.11
  112.0 7.1 %collective-permute-done.13 = bf16[4,2,2,4,8,128]{5,4,3,1,0,2:T(8,128)(2,1)S(1)} collective-permute-done((bf16[4,2,2,4,8,128]{5,4,3,1,0,2:T(8,128)(2,1)S(1)}, bf16[4,2,2,4,8,128]{5,4,3,1,0,2:T(8,128)(2,1)S(1)}, u32[]{:S(2)}, u32[]{:S(2)}) %collective-permute-start.13) | collective-permute-done | bytes 131104 | tf_op jit(solution)/shard_map/ppermute | solution.py:81
  119.2 0.9 collective-permute-done.12
  120.1 3.4 %collective-permute-done.11 = bf16[4,2,2,4,8,128]{5,4,3,1,0,2:T(8,128)(2,1)S(1)} collective-permute-done((bf16[4,2,2,4,8,128]{5,4,3,1,0,2:T(8,128)(2,1)S(1)}, bf16[4,2,2,4,8,128]{5,4,3,1,0,2:T(8,128)(2,1)S(1)}, u32[]{:S(2)}, u32[]{:S(2)}) %collective-permute-start.11) | collective-permute-done | bytes 131104 | tf_op jit(solution)/shard_map/ppermute | solution.py:81
  123.5 0.1 pad_maximum_fusion.3
  123.6 0.7 slice_bitcast_fusion
  124.3 5.9 %collective-permute-start.15 = (bf16[32,4,8,128]{3,2,1,0:T(8,128)(2,1)}, bf16[32,4,8,128]{3,2,1,0:T(8,128)(2,1)S(1)}, u32[]{:S(2)}, u32[]{:S(2)}) collective-permute-start(bf16[32,4,8,128]{3,2,1,0:T(8,128)(2,1)} %get-tuple-element.20), channel_id=1, source_target_pairs={{0,5},{1,6},{2,7},{3,0},{4,1},{5,2},{6,3},{7,4},{8,13},{9,14},{10,... | collective-permute-start | bytes 786440 | tf_op jit(solution)/shard_map/ppermute | solution.py:471
  130.2 0.0 collective-permute-start.14
  130.2 15.5 %all-to-all-done.1 = bf16[256,8,512]{2,1,0:T(8,128)(2,1)} async-done(((bf16[256,8,512]{2,1,0:T(8,128)(2,1)}), bf16[256,8,512]{2,1,0:T(8,128)(2,1)}, u32[]{:S(2)}, u32[]{:S(2)}) %all-to-all-start.1) | async-done | bytes 2097184 | tf_op jit(solution)/shard_map/all_to_all | solution.py:468
  145.7 6.3 %backward.1 = bf16[512,2048]{1,0:T(8,128)(2,1)} custom-call(bf16[16,2,8,8,512]{4,3,2,1,0:T(8,128)(2,1)} %bitcast.59.g_hbm, bf16[16,2,8,8,512]{4,3,2,1,0:T(8,128)(2,1)S(1)} %copy-done.1, f32[8,2,512]{2,1,0:T(2,128)S(1)} %get-tuple-element.16.r_ref, f32[64,1024]{1,0:T(8,128)S(1)} %copy-done.2, f32[24,1024]{1,0:T(8,128)S(1)} %copy-done.4, f32[24,1024]{1,0:T(8,128)S(1)} %copy-done.3), custom_call_target="tpu_custom_call" | custom-call | flops 2147483648 | bytes 10485760 | tf_op jit(solution)/shard_map/backward/pallas_call | solution.py:244
  152.0 3.8 %collective-permute-done.15.down_ref = bf16[32,4,8,128]{3,2,1,0:T(8,128)(2,1)S(1)} collective-permute-done((bf16[32,4,8,128]{3,2,1,0:T(8,128)(2,1)}, bf16[32,4,8,128]{3,2,1,0:T(8,128)(2,1)S(1)}, u32[]{:S(2)}, u32[]{:S(2)}) %collective-permute-start.15) | collective-permute-done | bytes 262176 | tf_op jit(solution)/shard_map/ppermute | solution.py:471
  155.8 2.2 %unpack_correl.1 = f32[3,16,16,256]{3,2,1,0:T(8,128)} custom-call(s32[7]{0:T(128)S(1)} %concatenate.3.sc_ref, bf16[32,4,8,128]{3,2,1,0:T(8,128)(2,1)S(1)} %collective-permute-done.14.up_ref, bf16[32,4,8,128]{3,2,1,0:T(8,128)(2,1)S(1)} %collective-permute-done.15.down_ref), custom_call_target="tpu_custom_call" | custom-call | tf_op jit(solution)/shard_map/unpack_correl/pallas_call | solution.py:443
  (17 shorter events, 0.3 us)
Async XLA Ops:
  6.2 14.3 %copy-start.5 = (s32[1,3]{1,0:T(1,128)S(1)}, s32[1,3]{1,0:T(1,128)}, u32[]{:S(2)}) copy-start(s32[1,3]{1,0:T(1,128)} %param.7) | copy-start | bytes 40
  6.3 66.8 %all-to-all-start = ((bf16[256,8,512]{2,1,0:T(8,128)(2,1)}), bf16[256,8,512]{2,1,0:T(8,128)(2,1)S(1)}, u32[]{:S(2)}, u32[]{:S(2)}) async-start(bf16[256,8,512]{2,1,0:T(8,128)(2,1)} %bitcast.94), calls=%async_computation | async-start | bytes 4194304 | tf_op jit(solution)/shard_map/all_to_all | solution.py:465
  20.6 2.8 %copy-start = (f32[1,3,16,16,2048]{4,3,2,1,0:T(8,128)S(1)}, f32[1,3,16,16,2048]{4,3,2,1,0:T(8,128)}, u32[]{:S(2)}) copy-start(f32[1,3,16,16,2048]{4,3,2,1,0:T(8,128)} %param.8) | copy-start | bytes 18874372
  24.6 1.6 %collective-permute-start = (bf16[4,4,2,4,8,128]{5,4,3,2,1,0:T(8,128)(2,1)S(1)}, bf16[4,4,2,4,8,128]{5,4,3,2,1,0:T(8,128)(2,1)S(1)}, u32[]{:S(2)}, u32[]{:S(2)}) collective-permute-start(bf16[4,4,2,4,8,128]{5,4,3,2,1,0:T(8,128)(2,1)S(1)} %bitcast.103), channel_id=1, source_target_pairs={{0,8},{8,0},{16,24},{24,16},{32,40},{40,32},{48,56},{56,48},{64,72... | collective-permute-start | bytes 786440 | tf_op jit(solution)/shard_map/ppermute | solution.py:81
  26.3 9.3 %collective-permute-start.1 = (bf16[2,4,2,4,8,128]{5,4,3,2,0,1:T(8,128)(2,1)S(1)}, bf16[2,4,2,4,8,128]{5,4,3,2,0,1:T(8,128)(2,1)S(1)}, u32[]{:S(2)}, u32[]{:S(2)}) collective-permute-start(bf16[2,4,2,4,8,128]{5,4,3,2,0,1:T(8,128)(2,1)S(1)} %get-tuple-element.37), channel_id=1, source_target_pairs={{0,16},{8,24},{16,32},{24,40},{32,48},{40,56},{48,0},{56,8},{64,80... | collective-permute-start | bytes 393224 | tf_op jit(solution)/shard_map/ppermute | solution.py:81
  27.9 11.4 %collective-permute-start.3 = (bf16[2,4,2,4,8,128]{5,4,3,2,0,1:T(8,128)(2,1)S(1)}, bf16[2,4,2,4,8,128]{5,4,3,2,0,1:T(8,128)(2,1)S(1)}, u32[]{:S(2)}, u32[]{:S(2)}) collective-permute-start(bf16[2,4,2,4,8,128]{5,4,3,2,0,1:T(8,128)(2,1)S(1)} %get-tuple-element.38), channel_id=1, source_target_pairs={{0,48},{8,56},{16,0},{24,8},{32,16},{40,24},{48,32},{56,40},{64,11... | collective-permute-start | bytes 393224 | tf_op jit(solution)/shard_map/ppermute | solution.py:81
  29.6 11.7 %collective-permute-start.2 = (bf16[2,4,2,4,8,128]{5,4,3,2,0,1:T(8,128)(2,1)S(1)}, bf16[2,4,2,4,8,128]{5,4,3,2,0,1:T(8,128)(2,1)S(1)}, u32[]{:S(2)}, u32[]{:S(2)}) collective-permute-start(bf16[2,4,2,4,8,128]{5,4,3,2,0,1:T(8,128)(2,1)S(1)} %get-tuple-element.39), channel_id=1, source_target_pairs={{0,32},{8,40},{16,48},{24,56},{32,0},{40,8},{48,16},{56,24},{64,96... | collective-permute-start | bytes 393224 | tf_op jit(solution)/shard_map/ppermute | solution.py:81
  41.4 11.4 %collective-permute-start.6 = (bf16[4,2,2,4,8,128]{5,4,3,2,1,0:T(8,128)(2,1)S(1)}, bf16[4,2,2,4,8,128]{5,4,3,2,1,0:T(8,128)(2,1)S(1)}, u32[]{:S(2)}, u32[]{:S(2)}) collective-permute-start(bf16[4,2,2,4,8,128]{5,4,3,2,1,0:T(8,128)(2,1)S(1)} %get-tuple-element.33), channel_id=1, source_target_pairs={{0,192},{8,200},{16,208},{24,216},{32,224},{40,232},{48,240},{56,2... | collective-permute-start | bytes 393224 | tf_op jit(solution)/shard_map/ppermute | solution.py:81
  44.3 10.1 %collective-permute-start.5 = (bf16[4,2,2,4,8,128]{5,4,3,2,1,0:T(8,128)(2,1)S(1)}, bf16[4,2,2,4,8,128]{5,4,3,2,1,0:T(8,128)(2,1)S(1)}, u32[]{:S(2)}, u32[]{:S(2)}) collective-permute-start(bf16[4,2,2,4,8,128]{5,4,3,2,1,0:T(8,128)(2,1)S(1)} %get-tuple-element.34), channel_id=1, source_target_pairs={{0,128},{8,136},{16,144},{24,152},{32,160},{40,168},{48,176},{56,1... | collective-permute-start | bytes 393224 | tf_op jit(solution)/shard_map/ppermute | solution.py:81
  45.1 11.5 %collective-permute-start.4 = (bf16[4,2,2,4,8,128]{5,4,3,2,1,0:T(8,128)(2,1)S(1)}, bf16[4,2,2,4,8,128]{5,4,3,2,1,0:T(8,128)(2,1)S(1)}, u32[]{:S(2)}, u32[]{:S(2)}) collective-permute-start(bf16[4,2,2,4,8,128]{5,4,3,2,1,0:T(8,128)(2,1)S(1)} %get-tuple-element.35), channel_id=1, source_target_pairs={{0,64},{8,72},{16,80},{24,88},{32,96},{40,104},{48,112},{56,120},{... | collective-permute-start | bytes 393224 | tf_op jit(solution)/shard_map/ppermute | solution.py:81
  82.2 63.6 %all-to-all-start.1 = ((bf16[256,8,512]{2,1,0:T(8,128)(2,1)}), bf16[256,8,512]{2,1,0:T(8,128)(2,1)}, u32[]{:S(2)}, u32[]{:S(2)}) async-start(bf16[256,8,512]{2,1,0:T(8,128)(2,1)} %bitcast.96), calls=%async_computation.1 | async-start | bytes 4194304 | tf_op jit(solution)/shard_map/all_to_all | solution.py:468
  91.4 1.6 %collective-permute-start.7 = (bf16[4,4,2,4,8,128]{5,4,3,2,1,0:T(8,128)(2,1)S(1)}, bf16[4,4,2,4,8,128]{5,4,3,2,1,0:T(8,128)(2,1)S(1)}, u32[]{:S(2)}, u32[]{:S(2)}) collective-permute-start(bf16[4,4,2,4,8,128]{5,4,3,2,1,0:T(8,128)(2,1)S(1)} %bitcast.104), channel_id=1, source_target_pairs={{0,8},{8,0},{16,24},{24,16},{32,40},{40,32},{48,56},{56,48},{64,72... | collective-permute-start | bytes 786440 | tf_op jit(solution)/shard_map/ppermute | solution.py:81
  93.0 9.5 %collective-permute-start.8 = (bf16[2,4,2,4,8,128]{5,4,3,0,2,1:T(8,128)(2,1)S(1)}, bf16[2,4,2,4,8,128]{5,4,3,0,2,1:T(8,128)(2,1)S(1)}, u32[]{:S(2)}, u32[]{:S(2)}) collective-permute-start(bf16[2,4,2,4,8,128]{5,4,3,0,2,1:T(8,128)(2,1)S(1)} %get-tuple-element.27), channel_id=1, source_target_pairs={{0,16},{8,24},{16,32},{24,40},{32,48},{40,56},{48,0},{56,8},{64,80... | collective-permute-start | bytes 393224 | tf_op jit(solution)/shard_map/ppermute | solution.py:81
  94.6 8.1 %collective-permute-start.10 = (bf16[2,4,2,4,8,128]{5,4,3,0,2,1:T(8,128)(2,1)S(1)}, bf16[2,4,2,4,8,128]{5,4,3,0,2,1:T(8,128)(2,1)S(1)}, u32[]{:S(2)}, u32[]{:S(2)}) collective-permute-start(bf16[2,4,2,4,8,128]{5,4,3,0,2,1:T(8,128)(2,1)S(1)} %get-tuple-element.28), channel_id=1, source_target_pairs={{0,48},{8,56},{16,0},{24,8},{32,16},{40,24},{48,32},{56,40},{64,11... | collective-permute-start | bytes 393224 | tf_op jit(solution)/shard_map/ppermute | solution.py:81
  96.4 10.9 %collective-permute-start.9 = (bf16[2,4,2,4,8,128]{5,4,3,0,2,1:T(8,128)(2,1)S(1)}, bf16[2,4,2,4,8,128]{5,4,3,0,2,1:T(8,128)(2,1)S(1)}, u32[]{:S(2)}, u32[]{:S(2)}) collective-permute-start(bf16[2,4,2,4,8,128]{5,4,3,0,2,1:T(8,128)(2,1)S(1)} %get-tuple-element.29), channel_id=1, source_target_pairs={{0,32},{8,40},{16,48},{24,56},{32,0},{40,8},{48,16},{56,24},{64,96... | collective-permute-start | bytes 393224 | tf_op jit(solution)/shard_map/ppermute | solution.py:81
  107.3 38.4 %copy-start.1 = (bf16[16,2,8,8,512]{4,3,2,1,0:T(8,128)(2,1)S(1)}, bf16[16,2,8,8,512]{4,3,2,1,0:T(8,128)(2,1)}, u32[]{:S(2)}) copy-start(bf16[16,2,8,8,512]{4,3,2,1,0:T(8,128)(2,1)} %get-tuple-element.13.y_ref) | copy-start | bytes 6291460
  107.3 38.4 %copy-start.2 = (f32[64,1024]{1,0:T(8,128)S(1)}, f32[64,1024]{1,0:T(8,128)}, u32[]{:S(2)}) copy-start(f32[64,1024]{1,0:T(8,128)} %constant.41.clone.a_hbm.a_ref) | copy-start | bytes 786436
  107.3 38.4 %copy-start.3 = (f32[24,1024]{1,0:T(8,128)S(1)}, f32[24,1024]{1,0:T(8,128)}, u32[]{:S(2)}) copy-start(f32[24,1024]{1,0:T(8,128)} %constant.43.clone.s_hbm.s_ref) | copy-start | bytes 294916
  107.3 38.4 %copy-start.4 = (f32[24,1024]{1,0:T(8,128)S(1)}, f32[24,1024]{1,0:T(8,128)}, u32[]{:S(2)}) copy-start(f32[24,1024]{1,0:T(8,128)} %constant.42.clone.c_hbm.c_ref) | copy-start | bytes 294916
  107.4 11.7 %collective-permute-start.13 = (bf16[4,2,2,4,8,128]{5,4,3,1,0,2:T(8,128)(2,1)S(1)}, bf16[4,2,2,4,8,128]{5,4,3,1,0,2:T(8,128)(2,1)S(1)}, u32[]{:S(2)}, u32[]{:S(2)}) collective-permute-start(bf16[4,2,2,4,8,128]{5,4,3,1,0,2:T(8,128)(2,1)S(1)} %get-tuple-element.23), channel_id=1, source_target_pairs={{0,192},{8,200},{16,208},{24,216},{32,224},{40,232},{48,240},{56,2... | collective-permute-start | bytes 393224 | tf_op jit(solution)/shard_map/ppermute | solution.py:81
  110.4 9.7 %collective-permute-start.12 = (bf16[4,2,2,4,8,128]{5,4,3,1,0,2:T(8,128)(2,1)S(1)}, bf16[4,2,2,4,8,128]{5,4,3,1,0,2:T(8,128)(2,1)S(1)}, u32[]{:S(2)}, u32[]{:S(2)}) collective-permute-start(bf16[4,2,2,4,8,128]{5,4,3,1,0,2:T(8,128)(2,1)S(1)} %get-tuple-element.24), channel_id=1, source_target_pairs={{0,128},{8,136},{16,144},{24,152},{32,160},{40,168},{48,176},{56,1... | collective-permute-start | bytes 393224 | tf_op jit(solution)/shard_map/ppermute | solution.py:81
  111.1 12.4 %collective-permute-start.11 = (bf16[4,2,2,4,8,128]{5,4,3,1,0,2:T(8,128)(2,1)S(1)}, bf16[4,2,2,4,8,128]{5,4,3,1,0,2:T(8,128)(2,1)S(1)}, u32[]{:S(2)}, u32[]{:S(2)}) collective-permute-start(bf16[4,2,2,4,8,128]{5,4,3,1,0,2:T(8,128)(2,1)S(1)} %get-tuple-element.25), channel_id=1, source_target_pairs={{0,64},{8,72},{16,80},{24,88},{32,96},{40,104},{48,112},{56,120},{... | collective-permute-start | bytes 393224 | tf_op jit(solution)/shard_map/ppermute | solution.py:81
  124.3 31.5 %collective-permute-start.15 = (bf16[32,4,8,128]{3,2,1,0:T(8,128)(2,1)}, bf16[32,4,8,128]{3,2,1,0:T(8,128)(2,1)S(1)}, u32[]{:S(2)}, u32[]{:S(2)}) collective-permute-start(bf16[32,4,8,128]{3,2,1,0:T(8,128)(2,1)} %get-tuple-element.20), channel_id=1, source_target_pairs={{0,5},{1,6},{2,7},{3,0},{4,1},{5,2},{6,3},{7,4},{8,13},{9,14},{10,... | collective-permute-start | bytes 786440 | tf_op jit(solution)/shard_map/ppermute | solution.py:471
  130.2 25.6 %collective-permute-start.14 = (bf16[32,4,8,128]{3,2,1,0:T(8,128)(2,1)S(1)}, bf16[32,4,8,128]{3,2,1,0:T(8,128)(2,1)S(1)}, u32[]{:S(2)}, u32[]{:S(2)}) collective-permute-start(bf16[32,4,8,128]{3,2,1,0:T(8,128)(2,1)S(1)} %get-tuple-element.21), channel_id=1, source_target_pairs={{0,1},{1,2},{2,3},{3,4},{4,5},{5,6},{6,7},{7,0},{8,9},{9,10},{10,1... | collective-permute-start | bytes 786440 | tf_op jit(solution)/shard_map/ppermute | solution.py:470

commit v7 on v6

--- a/solution.py
+++ b/solution.py
@@ -72,7 +72,7 @@
     return ((me // 8 - w // 8 + 4) % 4) * 8 + ((me // 2 - w // 2 + 4) % 4) * 2 + (me + w) % 2
 
 
-def exchange(blocks):
+def exchange(blocks, across=None):
     def hop(array, dy, dx, dc):
         pairs = []
         for w in range(NB):
@@ -84,9 +84,10 @@
     blocks = jnp.stack([blocks[0], hop(blocks[1], 0, 0, 1)])
     along_x = [blocks[:, 0]] + [hop(blocks[:, d], 0, d, 0) for d in range(1, 4)]
     blocks = jnp.stack(along_x)
+    if across is not None:
+        blocks = across(blocks)
     along_y = [blocks[:, :, 0]] + [hop(blocks[:, :, d], d, 0, 0) for d in range(1, 4)]
-    blocks = jnp.stack(along_y)
-    return blocks.reshape((NB,) + blocks.shape[3:])
+    return [piece.reshape((8,) + piece.shape[2:]) for piece in along_y]
 
 
 def dot(x, y, cx=1, cy=0):
@@ -414,14 +415,17 @@
     )(scalars, x, obs)
 
 
-def unpack_kernel(sc_ref, up_ref, down_ref, o_ref):
+def unpack_kernel(sc_ref, *refs):
+    *pieces, o_ref, x_ref = refs
+    for i, piece in enumerate(pieces):
+        x_ref[i * 8 : (i + 1) * 8] = piece[...]
     perm = regroup(False, True)
     low, me = sc_ref[5], sc_ref[6]
     regrouped = ([], [])
     for gr in range(4):
         sides = []
-        for ref in (up_ref, down_ref):
-            rows = [ref[source_slot(me, gr * 8 + j)].astype(F32).reshape(32, LANES) for j in range(8)]
+        for side in range(2):
+            rows = [x_ref[source_slot(me, gr * 8 + j), side].astype(F32).reshape(32, LANES) for j in range(8)]
             sides.append(jnp.concatenate(rows, axis=0))
         regrouped[0].append(dot(perm, jnp.where(low == 1, sides[1], sides[0]).astype(BF16)))
         regrouped[1].append(dot(perm, jnp.where(low == 1, sides[0], sides[1]).astype(BF16)))
@@ -438,20 +442,21 @@
                     o_ref[s, ih * 8 + i, :, h * LANES : (h + 1) * LANES] = val
 
 
-def unpack_correl(scalars, up, down):
+def unpack_correl(scalars, pieces):
     block = lambda shape: pl.BlockSpec(shape, lambda i, sc: (0,) * len(shape))
     return pl.pallas_call(
         unpack_kernel,
         grid_spec=pltpu.PrefetchScalarGridSpec(
             num_scalar_prefetch=1,
             grid=(1,),
-            in_specs=[block((NB, KB, 8, LANES))] * 2,
+            in_specs=[block((8, 2, KB, 8, LANES))] * 4,
             out_specs=block((SLOTS, CB, CB, 2 * LANES)),
+            scratch_shapes=[pltpu.VMEM((NB, 2, KB, 8, LANES), BF16)],
         ),
         out_shape=jax.ShapeDtypeStruct((SLOTS, CB, CB, 2 * LANES), F32),
         compiler_params=pltpu.CompilerParams(vmem_limit_bytes=VMEM_LIMIT),
         name="unpack_correl",
-    )(scalars, up, down)
+    )(scalars, *pieces)
 
 
 def on_device(traces, pair_lists, observed):
@@ -463,15 +468,19 @@
     low = jnp.where(g < 4, 1, 0)
     scalars = jnp.concatenate([pair_lists[0], jnp.stack([2 * q + half, half, low, me]).astype(jnp.int32)])
     moved = lax.all_to_all(white.reshape(WINS, 8, CH), ("win", "grp"), 0, 0)
-    seen = exchange(pack_observed(scalars, observed[0]))
+    seen = jnp.concatenate(exchange(pack_observed(scalars, observed[0])))
     corr, grad = middle(scalars, moved.reshape(2048, CH), seen)
     returned = lax.all_to_all(grad.reshape(WINS, 8, CH), ("win", "grp"), 0, 0)
-    corr = exchange(corr)
-    up = lax.ppermute(corr[:, 0], "grp", [(i, (i + 1) % GRP) for i in range(GRP)])
-    down = lax.ppermute(corr[:, 1], "grp", [(i, (i - 3) % GRP) for i in range(GRP)])
+
+    def across(blocks):
+        up = lax.ppermute(blocks[..., 0, :, :, :], "grp", [(i, (i + 1) % GRP) for i in range(GRP)])
+        down = lax.ppermute(blocks[..., 1, :, :, :], "grp", [(i, (i - 3) % GRP) for i in range(GRP)])
+        return jnp.stack([up, down], axis=-4)
+
+    owned = exchange(corr, across)
     trace_grad = backward(returned.reshape(16, 2, GRP, 8, CH), white, inverse, consts)
-    up, down, trace_grad = lax.optimization_barrier((up, down, trace_grad))
-    correl = unpack_correl(scalars, up, down)
+    owned, trace_grad = lax.optimization_barrier((owned, trace_grad))
+    correl = unpack_correl(scalars, owned)
     return correl[None], trace_grad[None]
 
 

time: 158 us -> 170 us (1.076)
  waiting for transfers between devices: 79.6 us -> 92 us
    ppermute x2, waiting for transfers between devices: 3.85 us -> 43.1 us  [the longest x1 43.1 us: across(): lax.ppermute(blocks[..., 1, :, :, :], 'grp', [(i, (i - 3) % GRP) for i in...]
    all_to_all x1, waiting for transfers between devices: 15.5 us -> 0.01 us  [on_device(): returned = lax.all_to_all(grad.reshape(WINS, 8, CH), ('win', 'grp'), 0, 0)]
    ppermute x14, waiting for transfers between devices: 43.9 us -> 32.5 us  [hop(): return lax.ppermute(array, 'win', pairs)]
  transfers between devices with their start and end apart: 18 -> 18, of which waited for: 17 -> 13; matrix products, arithmetic and copies ran while one was open for 1% -> 0% of each run, Pallas kernels for 5% -> 4%
where the time goes in v7:
time: 170 us
  waiting for transfers between devices  92 us (54%)
  starting transfers between devices  49.3 us (29%)
  Pallas kernels  24.3 us (14%)
  local copies, waits for them, and re-layouts  3.06 us (2%)
    ppermute x1, waiting for transfers between devices, across(): lax.ppermute(blocks[..., 1, :, :, :], 'grp', [(i, (i - 3) % GRP) for i in...  43.1 us
    ppermute x14, waiting for transfers between devices, hop(): return lax.ppermute(array, 'win', pairs)  32.5 us
    ppermute x14, starting transfers between devices, hop(): return lax.ppermute(array, 'win', pairs)  20.7 us
    all_to_all x1, waiting for transfers between devices, on_device(): moved = lax.all_to_all(white.reshape(WINS, 8, CH), ('win', 'grp'), 0, 0)  16.4 us
    all_to_all x1, starting transfers between devices, on_device(): moved = lax.all_to_all(white.reshape(WINS, 8, CH), ('win', 'grp'), 0, 0)  14.2 us
    all_to_all x1, starting transfers between devices, on_device(): returned = lax.all_to_all(grad.reshape(WINS, 8, CH), ('win', 'grp'), 0, 0)  9.17 us
    pallas_call x1, Pallas kernels, middle(): pl.pallas_call(middle_kernel, in_specs=[IN_SMEM, IN_VMEM, IN_VMEM], out_s...  9.04 us
    pallas_call x1, Pallas kernels, backward(): pl.pallas_call(backward_kernel, in_specs=[IN_HBM] + [IN_VMEM] * 5, out_sp...  6.25 us
  transfers between devices with their start and end apart: 18, of which 13 were waited for; matrix products, arithmetic and copies ran while one was open for 0% of the time, Pallas kernels for 4%

profile of v7, /device:TPU:64, one launch (start us, length us, event | category | flops | bytes accessed | tf_op | source)
XLA Modules:
  0.0 169.8 jit_solution(4214099458511491716)
XLA Ops:
  0.6 5.6 %forward.1 = (bf16[16,2,8,8,512]{4,3,2,1,0:T(8,128)(2,1)}, f32[8,2,512]{2,1,0:T(2,128)S(1)}) custom-call(bf16[512,2048]{1,0:T(8,128)(2,1)} %bitcast.112, f32[64,1024]{1,0:T(8,128)} %constant.41.clone.a_hbm.a_ref, f32[24,1024]{1,0:T(8,128)} %constant.42.clone.c_hbm.c_ref, f32[24,1024]{1,0:T(8,128)} %constant.43.clone.s_hbm.s_ref), custom_call_target="tpu_custom_call" | custom-call | flops 2147483648 | bytes 8388608 | tf_op jit(solution)/shard_map/forward/pallas_call | solution.py:172
  6.2 0.0 copy-start.5
  6.3 14.2 %all-to-all-start = ((bf16[256,8,512]{2,1,0:T(8,128)(2,1)}), bf16[256,8,512]{2,1,0:T(8,128)(2,1)S(1)}, u32[]{:S(2)}, u32[]{:S(2)}) async-start(bf16[256,8,512]{2,1,0:T(8,128)(2,1)} %bitcast.86), calls=%async_computation | async-start | bytes 4194304 | tf_op jit(solution)/shard_map/all_to_all | solution.py:470
  20.5 0.0 copy-done.5
  20.5 0.1 concatenate.6.sc_ref
  20.6 2.8 %copy-done = f32[1,3,16,16,2048]{4,3,2,1,0:T(8,128)S(1)} copy-done((f32[1,3,16,16,2048]{4,3,2,1,0:T(8,128)S(1)}, f32[1,3,16,16,2048]{4,3,2,1,0:T(8,128)}, u32[]{:S(2)}) %copy-start) | copy-done | bytes 6291480
  23.4 1.2 pack_observed.1
  24.6 0.2 collective-permute-start
  24.9 1.4 collective-permute-done
  26.3 1.6 collective-permute-start.1
  27.9 1.8 %collective-permute-start.3 = (bf16[2,4,2,4,8,128]{5,4,3,2,0,1:T(8,128)(2,1)S(1)}, bf16[2,4,2,4,8,128]{5,4,3,2,0,1:T(8,128)(2,1)S(1)}, u32[]{:S(2)}, u32[]{:S(2)}) collective-permute-start(bf16[2,4,2,4,8,128]{5,4,3,2,0,1:T(8,128)(2,1)S(1)} %get-tuple-element.42), channel_id=1, source_target_pairs={{0,48},{8,56},{16,0},{24,8},{32,16},{40,24},{48,32},{56,40},{64,11... | collective-permute-start | bytes 393224 | tf_op jit(solution)/shard_map/ppermute | solution.py:81
  29.6 1.8 %collective-permute-start.2 = (bf16[2,4,2,4,8,128]{5,4,3,2,0,1:T(8,128)(2,1)S(1)}, bf16[2,4,2,4,8,128]{5,4,3,2,0,1:T(8,128)(2,1)S(1)}, u32[]{:S(2)}, u32[]{:S(2)}) collective-permute-start(bf16[2,4,2,4,8,128]{5,4,3,2,0,1:T(8,128)(2,1)S(1)} %get-tuple-element.43), channel_id=1, source_target_pairs={{0,32},{8,40},{16,48},{24,56},{32,0},{40,8},{48,16},{56,24},{64,96... | collective-permute-start | bytes 393224 | tf_op jit(solution)/shard_map/ppermute | solution.py:81
  31.4 4.2 %collective-permute-done.1 = bf16[2,4,2,4,8,128]{5,4,3,2,0,1:T(8,128)(2,1)S(1)} collective-permute-done((bf16[2,4,2,4,8,128]{5,4,3,2,0,1:T(8,128)(2,1)S(1)}, bf16[2,4,2,4,8,128]{5,4,3,2,0,1:T(8,128)(2,1)S(1)}, u32[]{:S(2)}, u32[]{:S(2)}) %collective-permute-start.1) | collective-permute-done | bytes 131104 | tf_op jit(solution)/shard_map/ppermute | solution.py:81
  35.6 3.7 %collective-permute-done.3 = bf16[2,4,2,4,8,128]{5,4,3,2,0,1:T(8,128)(2,1)S(1)} collective-permute-done((bf16[2,4,2,4,8,128]{5,4,3,2,0,1:T(8,128)(2,1)S(1)}, bf16[2,4,2,4,8,128]{5,4,3,2,0,1:T(8,128)(2,1)S(1)}, u32[]{:S(2)}, u32[]{:S(2)}) %collective-permute-start.3) | collective-permute-done | bytes 131104 | tf_op jit(solution)/shard_map/ppermute | solution.py:81
  39.3 2.0 %collective-permute-done.2 = bf16[2,4,2,4,8,128]{5,4,3,2,0,1:T(8,128)(2,1)S(1)} collective-permute-done((bf16[2,4,2,4,8,128]{5,4,3,2,0,1:T(8,128)(2,1)S(1)}, bf16[2,4,2,4,8,128]{5,4,3,2,0,1:T(8,128)(2,1)S(1)}, u32[]{:S(2)}, u32[]{:S(2)}) %collective-permute-start.2) | collective-permute-done | bytes 131104 | tf_op jit(solution)/shard_map/ppermute | solution.py:81
  41.3 0.1 pad_maximum_fusion
  41.4 2.9 %collective-permute-start.6 = (bf16[4,2,2,4,8,128]{5,4,3,2,1,0:T(8,128)(2,1)S(1)}, bf16[4,2,2,4,8,128]{5,4,3,2,1,0:T(8,128)(2,1)S(1)}, u32[]{:S(2)}, u32[]{:S(2)}) collective-permute-start(bf16[4,2,2,4,8,128]{5,4,3,2,1,0:T(8,128)(2,1)S(1)} %get-tuple-element.37), channel_id=1, source_target_pairs={{0,192},{8,200},{16,208},{24,216},{32,224},{40,232},{48,240},{56,2... | collective-permute-start | bytes 393224 | tf_op jit(solution)/shard_map/ppermute | solution.py:81
  44.3 0.8 collective-permute-start.5
  45.1 0.9 collective-permute-start.4
  46.0 6.8 %collective-permute-done.6 = bf16[4,2,2,4,8,128]{5,4,3,2,1,0:T(8,128)(2,1)S(1)} collective-permute-done((bf16[4,2,2,4,8,128]{5,4,3,2,1,0:T(8,128)(2,1)S(1)}, bf16[4,2,2,4,8,128]{5,4,3,2,1,0:T(8,128)(2,1)S(1)}, u32[]{:S(2)}, u32[]{:S(2)}) %collective-permute-start.6) | collective-permute-done | bytes 131104 | tf_op jit(solution)/shard_map/ppermute | solution.py:81
  52.8 1.7 %collective-permute-done.5 = bf16[4,2,2,4,8,128]{5,4,3,2,1,0:T(8,128)(2,1)S(1)} collective-permute-done((bf16[4,2,2,4,8,128]{5,4,3,2,1,0:T(8,128)(2,1)S(1)}, bf16[4,2,2,4,8,128]{5,4,3,2,1,0:T(8,128)(2,1)S(1)}, u32[]{:S(2)}, u32[]{:S(2)}) %collective-permute-start.5) | collective-permute-done | bytes 131104 | tf_op jit(solution)/shard_map/ppermute | solution.py:81
  54.5 2.1 %collective-permute-done.4 = bf16[4,2,2,4,8,128]{5,4,3,2,1,0:T(8,128)(2,1)S(1)} collective-permute-done((bf16[4,2,2,4,8,128]{5,4,3,2,1,0:T(8,128)(2,1)S(1)}, bf16[4,2,2,4,8,128]{5,4,3,2,1,0:T(8,128)(2,1)S(1)}, u32[]{:S(2)}, u32[]{:S(2)}) %collective-permute-start.4) | collective-permute-done | bytes 131104 | tf_op jit(solution)/shard_map/ppermute | solution.py:81
  56.6 0.1 pad_maximum_fusion.1.obs_ref
  56.7 16.4 %all-to-all-done = bf16[256,8,512]{2,1,0:T(8,128)(2,1)S(1)} async-done(((bf16[256,8,512]{2,1,0:T(8,128)(2,1)}), bf16[256,8,512]{2,1,0:T(8,128)(2,1)S(1)}, u32[]{:S(2)}, u32[]{:S(2)}) %all-to-all-start) | async-done | bytes 2097184 | tf_op jit(solution)/shard_map/all_to_all | solution.py:470
  73.1 9.0 %middle.1 = (bf16[32,2,4,8,128]{4,3,2,1,0:T(8,128)(2,1)S(1)}, bf16[2048,512]{1,0:T(8,128)(2,1)}) custom-call(s32[7]{0:T(128)S(1)} %concatenate.6.sc_ref, bf16[2048,512]{1,0:T(8,128)(2,1)S(1)} %bitcast.85, bf16[32,2,4,8,128]{4,3,2,1,0:T(8,128)(2,1)S(1)} %pad_maximum_fusion.1.obs_ref), custom_call_target="tpu_custom_call" | custom-call | tf_op jit(solution)/shard_map/middle/pallas_call | solution.py:399
  82.2 9.2 %all-to-all-start.1 = ((bf16[256,8,512]{2,1,0:T(8,128)(2,1)}), bf16[256,8,512]{2,1,0:T(8,128)(2,1)}, u32[]{:S(2)}, u32[]{:S(2)}) async-start(bf16[256,8,512]{2,1,0:T(8,128)(2,1)} %bitcast.91), calls=%async_computation.1 | async-start | bytes 4194304 | tf_op jit(solution)/shard_map/all_to_all | solution.py:473
  91.4 0.2 collective-permute-start.7
  91.6 1.4 collective-permute-done.7
  93.1 1.6 collective-permute-start.8
  94.6 1.8 %collective-permute-start.10 = (bf16[2,4,2,4,8,128]{5,4,3,0,1,2:T(8,128)(2,1)S(1)}, bf16[2,4,2,4,8,128]{5,4,3,0,1,2:T(8,128)(2,1)S(1)}, u32[]{:S(2)}, u32[]{:S(2)}) collective-permute-start(bf16[2,4,2,4,8,128]{5,4,3,0,1,2:T(8,128)(2,1)S(1)} %get-tuple-element.32), channel_id=1, source_target_pairs={{0,48},{8,56},{16,0},{24,8},{32,16},{40,24},{48,32},{56,40},{64,11... | collective-permute-start | bytes 393224 | tf_op jit(solution)/shard_map/ppermute | solution.py:81
  96.4 1.8 %collective-permute-start.9 = (bf16[2,4,2,4,8,128]{5,4,3,0,1,2:T(8,128)(2,1)S(1)}, bf16[2,4,2,4,8,128]{5,4,3,0,1,2:T(8,128)(2,1)S(1)}, u32[]{:S(2)}, u32[]{:S(2)}) collective-permute-start(bf16[2,4,2,4,8,128]{5,4,3,0,1,2:T(8,128)(2,1)S(1)} %get-tuple-element.33), channel_id=1, source_target_pairs={{0,32},{8,40},{16,48},{24,56},{32,0},{40,8},{48,16},{56,24},{64,96... | collective-permute-start | bytes 393224 | tf_op jit(solution)/shard_map/ppermute | solution.py:81
  98.2 4.3 %collective-permute-done.8 = bf16[2,4,2,4,8,128]{5,4,3,0,1,2:T(8,128)(2,1)S(1)} collective-permute-done((bf16[2,4,2,4,8,128]{5,4,3,0,1,2:T(8,128)(2,1)S(1)}, bf16[2,4,2,4,8,128]{5,4,3,0,1,2:T(8,128)(2,1)S(1)}, u32[]{:S(2)}, u32[]{:S(2)}) %collective-permute-start.8) | collective-permute-done | bytes 131104 | tf_op jit(solution)/shard_map/ppermute | solution.py:81
  102.5 0.3 collective-permute-done.10
  102.8 4.6 %collective-permute-done.9 = bf16[2,4,2,4,8,128]{5,4,3,0,1,2:T(8,128)(2,1)S(1)} collective-permute-done((bf16[2,4,2,4,8,128]{5,4,3,0,1,2:T(8,128)(2,1)S(1)}, bf16[2,4,2,4,8,128]{5,4,3,0,1,2:T(8,128)(2,1)S(1)}, u32[]{:S(2)}, u32[]{:S(2)}) %collective-permute-start.9) | collective-permute-done | bytes 131104 | tf_op jit(solution)/shard_map/ppermute | solution.py:81
  107.4 0.1 pad_maximum_fusion.2
  107.5 5.2 %collective-permute-start.12 = (bf16[4,2,4,4,8,128]{5,4,3,1,0,2:T(8,128)(2,1)S(1)}, bf16[4,2,4,4,8,128]{5,4,3,1,0,2:T(8,128)(2,1)S(1)}, u32[]{:S(2)}, u32[]{:S(2)}) collective-permute-start(bf16[4,2,4,4,8,128]{5,4,3,1,0,2:T(8,128)(2,1)S(1)} %get-tuple-element.28), channel_id=1, source_target_pairs={{0,5},{1,6},{2,7},{3,0},{4,1},{5,2},{6,3},{7,4},{8,13},{9,14},{10,... | collective-permute-start | bytes 786440 | tf_op jit(solution)/shard_map/ppermute | solution.py:477
  112.7 0.0 collective-permute-start.11
  112.7 43.1 %collective-permute-done.12 = bf16[4,2,4,4,8,128]{5,4,3,1,0,2:T(8,128)(2,1)S(1)} collective-permute-done((bf16[4,2,4,4,8,128]{5,4,3,1,0,2:T(8,128)(2,1)S(1)}, bf16[4,2,4,4,8,128]{5,4,3,1,0,2:T(8,128)(2,1)S(1)}, u32[]{:S(2)}, u32[]{:S(2)}) %collective-permute-start.12) | collective-permute-done | bytes 262176 | tf_op jit(solution)/shard_map/ppermute | solution.py:477
  155.8 0.0 collective-permute-done.11
  155.9 3.2 %collective-permute-start.15 = (bf16[4,2,2,4,8,128]{5,4,3,2,1,0:T(8,128)(2,1)S(1)}, bf16[4,2,2,4,8,128]{5,4,3,2,1,0:T(8,128)(2,1)S(1)}, u32[]{:S(2)}, u32[]{:S(2)}) collective-permute-start(bf16[4,2,2,4,8,128]{5,4,3,2,1,0:T(8,128)(2,1)S(1)} %get-tuple-element.24), channel_id=1, source_target_pairs={{0,192},{8,200},{16,208},{24,216},{32,224},{40,232},{48,240},{56,2... | collective-permute-start | bytes 393224 | tf_op jit(solution)/shard_map/ppermute | solution.py:81
  159.1 0.0 collective-permute-start.13
  159.1 2.2 %collective-permute-start.14 = (bf16[4,2,2,4,8,128]{5,4,3,2,1,0:T(8,128)(2,1)S(1)}, bf16[4,2,2,4,8,128]{5,4,3,2,1,0:T(8,128)(2,1)S(1)}, u32[]{:S(2)}, u32[]{:S(2)}) collective-permute-start(bf16[4,2,2,4,8,128]{5,4,3,2,1,0:T(8,128)(2,1)S(1)} %get-tuple-element.27), channel_id=1, source_target_pairs={{0,128},{8,136},{16,144},{24,152},{32,160},{40,168},{48,176},{56,1... | collective-permute-start | bytes 393224 | tf_op jit(solution)/shard_map/ppermute | solution.py:81
  161.3 0.0 all-to-all-done.1
  161.3 6.3 %backward.1 = bf16[512,2048]{1,0:T(8,128)(2,1)} custom-call(bf16[16,2,8,8,512]{4,3,2,1,0:T(8,128)(2,1)} %bitcast.56.g_hbm, bf16[16,2,8,8,512]{4,3,2,1,0:T(8,128)(2,1)S(1)} %copy-done.1, f32[8,2,512]{2,1,0:T(2,128)S(1)} %get-tuple-element.18.r_ref, f32[64,1024]{1,0:T(8,128)S(1)} %copy-done.2, f32[24,1024]{1,0:T(8,128)S(1)} %copy-done.4, f32[24,1024]{1,0:T(8,128)S(1)} %copy-done.3), custom_call_target="tpu_custom_call" | custom-call | flops 2147483648 | bytes 10485760 | tf_op jit(solution)/shard_map/backward/pallas_call | solution.py:245
  167.6 0.0 collective-permute-done.15
  167.6 0.0 collective-permute-done.13
  167.6 0.0 collective-permute-done.14
  167.6 2.2 %unpack_correl.1 = f32[3,16,16,256]{3,2,1,0:T(8,128)} custom-call(s32[7]{0:T(128)S(1)} %concatenate.6.sc_ref, bf16[8,2,4,8,128]{4,3,2,1,0:T(8,128)(2,1)S(1)} %bitcast.87, bf16[8,2,4,8,128]{4,3,2,1,0:T(8,128)(2,1)S(1)} %bitcast.89, bf16[8,2,4,8,128]{4,3,2,1,0:T(8,128)(2,1)S(1)} %bitcast.90, bf16[8,2,4,8,128]{4,3,2,1,0:T(8,128)(2,1)S(1)} %bitcast.88), custom_call_target="tpu_custom_call" | custom-call | tf_op jit(solution)/shard_map/unpack_correl/pallas_call | solution.py:447
  (17 shorter events, 0.3 us)
Async XLA Ops:
  6.2 14.3 %copy-start.5 = (s32[1,3]{1,0:T(1,128)S(1)}, s32[1,3]{1,0:T(1,128)}, u32[]{:S(2)}) copy-start(s32[1,3]{1,0:T(1,128)} %param.7) | copy-start | bytes 40
  6.3 66.8 %all-to-all-start = ((bf16[256,8,512]{2,1,0:T(8,128)(2,1)}), bf16[256,8,512]{2,1,0:T(8,128)(2,1)S(1)}, u32[]{:S(2)}, u32[]{:S(2)}) async-start(bf16[256,8,512]{2,1,0:T(8,128)(2,1)} %bitcast.86), calls=%async_computation | async-start | bytes 4194304 | tf_op jit(solution)/shard_map/all_to_all | solution.py:470
  20.6 2.8 %copy-start = (f32[1,3,16,16,2048]{4,3,2,1,0:T(8,128)S(1)}, f32[1,3,16,16,2048]{4,3,2,1,0:T(8,128)}, u32[]{:S(2)}) copy-start(f32[1,3,16,16,2048]{4,3,2,1,0:T(8,128)} %param.8) | copy-start | bytes 18874372
  24.6 1.6 collective-permute-start
  26.3 9.3 %collective-permute-start.1 = (bf16[2,4,2,4,8,128]{5,4,3,2,0,1:T(8,128)(2,1)S(1)}, bf16[2,4,2,4,8,128]{5,4,3,2,0,1:T(8,128)(2,1)S(1)}, u32[]{:S(2)}, u32[]{:S(2)}) collective-permute-start(bf16[2,4,2,4,8,128]{5,4,3,2,0,1:T(8,128)(2,1)S(1)} %get-tuple-element.41), channel_id=1, source_target_pairs={{0,16},{8,24},{16,32},{24,40},{32,48},{40,56},{48,0},{56,8},{64,80... | collective-permute-start | bytes 393224 | tf_op jit(solution)/shard_map/ppermute | solution.py:81
  27.9 11.4 %collective-permute-start.3 = (bf16[2,4,2,4,8,128]{5,4,3,2,0,1:T(8,128)(2,1)S(1)}, bf16[2,4,2,4,8,128]{5,4,3,2,0,1:T(8,128)(2,1)S(1)}, u32[]{:S(2)}, u32[]{:S(2)}) collective-permute-start(bf16[2,4,2,4,8,128]{5,4,3,2,0,1:T(8,128)(2,1)S(1)} %get-tuple-element.42), channel_id=1, source_target_pairs={{0,48},{8,56},{16,0},{24,8},{32,16},{40,24},{48,32},{56,40},{64,11... | collective-permute-start | bytes 393224 | tf_op jit(solution)/shard_map/ppermute | solution.py:81
  29.6 11.7 %collective-permute-start.2 = (bf16[2,4,2,4,8,128]{5,4,3,2,0,1:T(8,128)(2,1)S(1)}, bf16[2,4,2,4,8,128]{5,4,3,2,0,1:T(8,128)(2,1)S(1)}, u32[]{:S(2)}, u32[]{:S(2)}) collective-permute-start(bf16[2,4,2,4,8,128]{5,4,3,2,0,1:T(8,128)(2,1)S(1)} %get-tuple-element.43), channel_id=1, source_target_pairs={{0,32},{8,40},{16,48},{24,56},{32,0},{40,8},{48,16},{56,24},{64,96... | collective-permute-start | bytes 393224 | tf_op jit(solution)/shard_map/ppermute | solution.py:81
  41.4 11.4 %collective-permute-start.6 = (bf16[4,2,2,4,8,128]{5,4,3,2,1,0:T(8,128)(2,1)S(1)}, bf16[4,2,2,4,8,128]{5,4,3,2,1,0:T(8,128)(2,1)S(1)}, u32[]{:S(2)}, u32[]{:S(2)}) collective-permute-start(bf16[4,2,2,4,8,128]{5,4,3,2,1,0:T(8,128)(2,1)S(1)} %get-tuple-element.37), channel_id=1, source_target_pairs={{0,192},{8,200},{16,208},{24,216},{32,224},{40,232},{48,240},{56,2... | collective-permute-start | bytes 393224 | tf_op jit(solution)/shard_map/ppermute | solution.py:81
  44.3 10.1 %collective-permute-start.5 = (bf16[4,2,2,4,8,128]{5,4,3,2,1,0:T(8,128)(2,1)S(1)}, bf16[4,2,2,4,8,128]{5,4,3,2,1,0:T(8,128)(2,1)S(1)}, u32[]{:S(2)}, u32[]{:S(2)}) collective-permute-start(bf16[4,2,2,4,8,128]{5,4,3,2,1,0:T(8,128)(2,1)S(1)} %get-tuple-element.38), channel_id=1, source_target_pairs={{0,128},{8,136},{16,144},{24,152},{32,160},{40,168},{48,176},{56,1... | collective-permute-start | bytes 393224 | tf_op jit(solution)/shard_map/ppermute | solution.py:81
  45.1 11.5 %collective-permute-start.4 = (bf16[4,2,2,4,8,128]{5,4,3,2,1,0:T(8,128)(2,1)S(1)}, bf16[4,2,2,4,8,128]{5,4,3,2,1,0:T(8,128)(2,1)S(1)}, u32[]{:S(2)}, u32[]{:S(2)}) collective-permute-start(bf16[4,2,2,4,8,128]{5,4,3,2,1,0:T(8,128)(2,1)S(1)} %get-tuple-element.39), channel_id=1, source_target_pairs={{0,64},{8,72},{16,80},{24,88},{32,96},{40,104},{48,112},{56,120},{... | collective-permute-start | bytes 393224 | tf_op jit(solution)/shard_map/ppermute | solution.py:81
  82.2 79.2 %all-to-all-start.1 = ((bf16[256,8,512]{2,1,0:T(8,128)(2,1)}), bf16[256,8,512]{2,1,0:T(8,128)(2,1)}, u32[]{:S(2)}, u32[]{:S(2)}) async-start(bf16[256,8,512]{2,1,0:T(8,128)(2,1)} %bitcast.91), calls=%async_computation.1 | async-start | bytes 4194304 | tf_op jit(solution)/shard_map/all_to_all | solution.py:473
  91.4 1.6 collective-permute-start.7
  93.0 68.3 %copy-start.1 = (bf16[16,2,8,8,512]{4,3,2,1,0:T(8,128)(2,1)S(1)}, bf16[16,2,8,8,512]{4,3,2,1,0:T(8,128)(2,1)}, u32[]{:S(2)}) copy-start(bf16[16,2,8,8,512]{4,3,2,1,0:T(8,128)(2,1)} %get-tuple-element.15.y_ref) | copy-start | bytes 6291460
  93.0 68.3 %copy-start.2 = (f32[64,1024]{1,0:T(8,128)S(1)}, f32[64,1024]{1,0:T(8,128)}, u32[]{:S(2)}) copy-start(f32[64,1024]{1,0:T(8,128)} %constant.41.clone.a_hbm.a_ref) | copy-start | bytes 786436
  93.0 68.3 %copy-start.3 = (f32[24,1024]{1,0:T(8,128)S(1)}, f32[24,1024]{1,0:T(8,128)}, u32[]{:S(2)}) copy-start(f32[24,1024]{1,0:T(8,128)} %constant.43.clone.s_hbm.s_ref) | copy-start | bytes 294916
  93.0 68.3 %copy-start.4 = (f32[24,1024]{1,0:T(8,128)S(1)}, f32[24,1024]{1,0:T(8,128)}, u32[]{:S(2)}) copy-start(f32[24,1024]{1,0:T(8,128)} %constant.42.clone.c_hbm.c_ref) | copy-start | bytes 294916
  93.1 9.4 %collective-permute-start.8 = (bf16[2,4,2,4,8,128]{5,4,3,0,1,2:T(8,128)(2,1)S(1)}, bf16[2,4,2,4,8,128]{5,4,3,0,1,2:T(8,128)(2,1)S(1)}, u32[]{:S(2)}, u32[]{:S(2)}) collective-permute-start(bf16[2,4,2,4,8,128]{5,4,3,0,1,2:T(8,128)(2,1)S(1)} %get-tuple-element.31), channel_id=1, source_target_pairs={{0,16},{8,24},{16,32},{24,40},{32,48},{40,56},{48,0},{56,8},{64,80... | collective-permute-start | bytes 393224 | tf_op jit(solution)/shard_map/ppermute | solution.py:81
  94.6 8.2 %collective-permute-start.10 = (bf16[2,4,2,4,8,128]{5,4,3,0,1,2:T(8,128)(2,1)S(1)}, bf16[2,4,2,4,8,128]{5,4,3,0,1,2:T(8,128)(2,1)S(1)}, u32[]{:S(2)}, u32[]{:S(2)}) collective-permute-start(bf16[2,4,2,4,8,128]{5,4,3,0,1,2:T(8,128)(2,1)S(1)} %get-tuple-element.32), channel_id=1, source_target_pairs={{0,48},{8,56},{16,0},{24,8},{32,16},{40,24},{48,32},{56,40},{64,11... | collective-permute-start | bytes 393224 | tf_op jit(solution)/shard_map/ppermute | solution.py:81
  96.4 11.0 %collective-permute-start.9 = (bf16[2,4,2,4,8,128]{5,4,3,0,1,2:T(8,128)(2,1)S(1)}, bf16[2,4,2,4,8,128]{5,4,3,0,1,2:T(8,128)(2,1)S(1)}, u32[]{:S(2)}, u32[]{:S(2)}) collective-permute-start(bf16[2,4,2,4,8,128]{5,4,3,0,1,2:T(8,128)(2,1)S(1)} %get-tuple-element.33), channel_id=1, source_target_pairs={{0,32},{8,40},{16,48},{24,56},{32,0},{40,8},{48,16},{56,24},{64,96... | collective-permute-start | bytes 393224 | tf_op jit(solution)/shard_map/ppermute | solution.py:81
  107.5 48.3 %collective-permute-start.12 = (bf16[4,2,4,4,8,128]{5,4,3,1,0,2:T(8,128)(2,1)S(1)}, bf16[4,2,4,4,8,128]{5,4,3,1,0,2:T(8,128)(2,1)S(1)}, u32[]{:S(2)}, u32[]{:S(2)}) collective-permute-start(bf16[4,2,4,4,8,128]{5,4,3,1,0,2:T(8,128)(2,1)S(1)} %get-tuple-element.28), channel_id=1, source_target_pairs={{0,5},{1,6},{2,7},{3,0},{4,1},{5,2},{6,3},{7,4},{8,13},{9,14},{10,... | collective-permute-start | bytes 786440 | tf_op jit(solution)/shard_map/ppermute | solution.py:477
  112.7 43.1 %collective-permute-start.11 = (bf16[4,2,4,4,8,128]{5,4,3,1,0,2:T(8,128)(2,1)S(1)}, bf16[4,2,4,4,8,128]{5,4,3,1,0,2:T(8,128)(2,1)S(1)}, u32[]{:S(2)}, u32[]{:S(2)}) collective-permute-start(bf16[4,2,4,4,8,128]{5,4,3,1,0,2:T(8,128)(2,1)S(1)} %get-tuple-element.29), channel_id=1, source_target_pairs={{0,1},{1,2},{2,3},{3,4},{4,5},{5,6},{6,7},{7,0},{8,9},{9,10},{10,1... | collective-permute-start | bytes 786440 | tf_op jit(solution)/shard_map/ppermute | solution.py:476
  155.9 11.7 %collective-permute-start.15 = (bf16[4,2,2,4,8,128]{5,4,3,2,1,0:T(8,128)(2,1)S(1)}, bf16[4,2,2,4,8,128]{5,4,3,2,1,0:T(8,128)(2,1)S(1)}, u32[]{:S(2)}, u32[]{:S(2)}) collective-permute-start(bf16[4,2,2,4,8,128]{5,4,3,2,1,0:T(8,128)(2,1)S(1)} %get-tuple-element.24), channel_id=1, source_target_pairs={{0,192},{8,200},{16,208},{24,216},{32,224},{40,232},{48,240},{56,2... | collective-permute-start | bytes 393224 | tf_op jit(solution)/shard_map/ppermute | solution.py:81
  159.1 8.6 %collective-permute-start.13 = (bf16[4,2,2,4,8,128]{5,4,3,2,1,0:T(8,128)(2,1)S(1)}, bf16[4,2,2,4,8,128]{5,4,3,2,1,0:T(8,128)(2,1)S(1)}, u32[]{:S(2)}, u32[]{:S(2)}) collective-permute-start(bf16[4,2,2,4,8,128]{5,4,3,2,1,0:T(8,128)(2,1)S(1)} %get-tuple-element.26), channel_id=1, source_target_pairs={{0,64},{8,72},{16,80},{24,88},{32,96},{40,104},{48,112},{56,120},{... | collective-permute-start | bytes 393224 | tf_op jit(solution)/shard_map/ppermute | solution.py:81
  159.1 8.6 %collective-permute-start.14 = (bf16[4,2,2,4,8,128]{5,4,3,2,1,0:T(8,128)(2,1)S(1)}, bf16[4,2,2,4,8,128]{5,4,3,2,1,0:T(8,128)(2,1)S(1)}, u32[]{:S(2)}, u32[]{:S(2)}) collective-permute-start(bf16[4,2,2,4,8,128]{5,4,3,2,1,0:T(8,128)(2,1)S(1)} %get-tuple-element.27), channel_id=1, source_target_pairs={{0,128},{8,136},{16,144},{24,152},{32,160},{40,168},{48,176},{56,1... | collective-permute-start | bytes 393224 | tf_op jit(solution)/shard_map/ppermute | solution.py:81

commit v8 on v6

--- a/solution.py
+++ b/solution.py
@@ -30,11 +30,11 @@
 
 
 def half_of(g):
-    return jnp.where(jnp.logical_and(g >= 3, g <= 6), 0, 1)
+    return jnp.where(jnp.logical_and(g >= 1, g <= 4), 1, 0)
 
 
 def quarter_of(g):
-    return jnp.where(half_of(g) == 0, g - 3, (g + 1) % GRP)
+    return jnp.where(half_of(g) == 1, g - 1, (g + 3) % GRP)
 
 
 def table_parts():
@@ -108,8 +108,8 @@
 
 
 def plane_bands(g):
-    h = 0 if 3 <= g <= 6 else 1
-    q = g - 3 if h == 0 else (g + 1) % GRP
+    h = 1 if 1 <= g <= 4 else 0
+    q = g - 1 if h == 1 else (g + 3) % GRP
     return (q * 4 + h * 2, q * 4 + h * 2 + 1)
 
 
@@ -467,8 +467,8 @@
     corr, grad = middle(scalars, moved.reshape(2048, CH), seen)
     returned = lax.all_to_all(grad.reshape(WINS, 8, CH), ("win", "grp"), 0, 0)
     corr = exchange(corr)
-    up = lax.ppermute(corr[:, 0], "grp", [(i, (i + 1) % GRP) for i in range(GRP)])
-    down = lax.ppermute(corr[:, 1], "grp", [(i, (i - 3) % GRP) for i in range(GRP)])
+    up = lax.ppermute(corr[:, 0], "grp", [(i, (i - 1) % GRP) for i in range(GRP)])
+    down = lax.ppermute(corr[:, 1], "grp", [(i, (i + 3) % GRP) for i in range(GRP)])
     trace_grad = backward(returned.reshape(16, 2, GRP, 8, CH), white, inverse, consts)
     up, down, trace_grad = lax.optimization_barrier((up, down, trace_grad))
     correl = unpack_correl(scalars, up, down)

time: 158 us -> 160 us (1.013); the launches traced: 158 us -> 157 us
  waiting for transfers between devices: 79.6 us -> 75.5 us
  starting transfers between devices: 49.1 us -> 52.1 us
    all_to_all x1, waiting for transfers between devices: 15.5 us -> 10.6 us  [on_device(): returned = lax.all_to_all(grad.reshape(WINS, 8, CH), ('win', 'grp'), 0, 0)]
    ppermute x2, starting transfers between devices: 5.89 us -> 8.91 us  [the longest x1 5.06 us: on_device(): lax.ppermute(corr[:, 1], 'grp', [(i, (i + 3) % GRP) for i in range(GRP)])]
where the time goes in v8:
time: 160 us; the launch traced here: 157 us
  waiting for transfers between devices  75.5 us (47%)
  starting transfers between devices  52.1 us (33%)
  Pallas kernels  24.3 us (15%)
  local copies, waits for them, and re-layouts  3.78 us (2%)
    ppermute x14, waiting for transfers between devices, hop(): return lax.ppermute(array, 'win', pairs)  43.9 us
    ppermute x14, starting transfers between devices, hop(): return lax.ppermute(array, 'win', pairs)  19.9 us
    all_to_all x1, waiting for transfers between devices, on_device(): moved = lax.all_to_all(white.reshape(WINS, 8, CH), ('win', 'grp'), 0, 0)  16.4 us
    all_to_all x1, starting transfers between devices, on_device(): moved = lax.all_to_all(white.reshape(WINS, 8, CH), ('win', 'grp'), 0, 0)  14.2 us
    all_to_all x1, waiting for transfers between devices, on_device(): returned = lax.all_to_all(grad.reshape(WINS, 8, CH), ('win', 'grp'), 0, 0)  10.6 us
    all_to_all x1, starting transfers between devices, on_device(): returned = lax.all_to_all(grad.reshape(WINS, 8, CH), ('win', 'grp'), 0, 0)  9.17 us
    pallas_call x1, Pallas kernels, middle(): pl.pallas_call(middle_kernel, in_specs=[IN_SMEM, IN_VMEM, IN_VMEM], out_s...  9.04 us
    pallas_call x1, Pallas kernels, backward(): pl.pallas_call(backward_kernel, in_specs=[IN_HBM] + [IN_VMEM] * 5, out_sp...  6.26 us
  transfers between devices with their start and end apart: 18, of which 17 were waited for; matrix products, arithmetic and copies ran while one was open for 1% of the time, Pallas kernels for 5%

profile of v8, /device:TPU:64, one launch (start us, length us, event | category | flops | bytes accessed | tf_op | source)
XLA Modules:
  0.0 156.9 jit_solution(13482026979241090452)
XLA Ops:
  0.6 5.6 %forward.1 = (bf16[16,2,8,8,512]{4,3,2,1,0:T(8,128)(2,1)}, f32[8,2,512]{2,1,0:T(2,128)S(1)}) custom-call(bf16[512,2048]{1,0:T(8,128)(2,1)} %bitcast.118, f32[64,1024]{1,0:T(8,128)} %constant.39.clone.a_hbm.a_ref, f32[24,1024]{1,0:T(8,128)} %constant.40.clone.c_hbm.c_ref, f32[24,1024]{1,0:T(8,128)} %constant.41.clone.s_hbm.s_ref), custom_call_target="tpu_custom_call" | custom-call | flops 2147483648 | bytes 8388608 | tf_op jit(solution)/shard_map/forward/pallas_call | solution.py:171
  6.2 0.0 copy-start.5
  6.3 14.2 %all-to-all-start = ((bf16[256,8,512]{2,1,0:T(8,128)(2,1)}), bf16[256,8,512]{2,1,0:T(8,128)(2,1)S(1)}, u32[]{:S(2)}, u32[]{:S(2)}) async-start(bf16[256,8,512]{2,1,0:T(8,128)(2,1)} %bitcast.94), calls=%async_computation | async-start | bytes 4194304 | tf_op jit(solution)/shard_map/all_to_all | solution.py:465
  20.5 0.1 concatenate.3.sc_ref
  20.6 2.8 %copy-done = f32[1,3,16,16,2048]{4,3,2,1,0:T(8,128)S(1)} copy-done((f32[1,3,16,16,2048]{4,3,2,1,0:T(8,128)S(1)}, f32[1,3,16,16,2048]{4,3,2,1,0:T(8,128)}, u32[]{:S(2)}) %copy-start) | copy-done | bytes 6291480
  23.4 1.2 pack_observed.1
  24.6 0.2 collective-permute-start
  24.9 1.4 collective-permute-done
  26.3 1.6 collective-permute-start.1
  27.9 1.8 %collective-permute-start.3 = (bf16[2,4,2,4,8,128]{5,4,3,2,0,1:T(8,128)(2,1)S(1)}, bf16[2,4,2,4,8,128]{5,4,3,2,0,1:T(8,128)(2,1)S(1)}, u32[]{:S(2)}, u32[]{:S(2)}) collective-permute-start(bf16[2,4,2,4,8,128]{5,4,3,2,0,1:T(8,128)(2,1)S(1)} %get-tuple-element.38), channel_id=1, source_target_pairs={{0,48},{8,56},{16,0},{24,8},{32,16},{40,24},{48,32},{56,40},{64,11... | collective-permute-start | bytes 393224 | tf_op jit(solution)/shard_map/ppermute | solution.py:81
  29.6 1.8 %collective-permute-start.2 = (bf16[2,4,2,4,8,128]{5,4,3,2,0,1:T(8,128)(2,1)S(1)}, bf16[2,4,2,4,8,128]{5,4,3,2,0,1:T(8,128)(2,1)S(1)}, u32[]{:S(2)}, u32[]{:S(2)}) collective-permute-start(bf16[2,4,2,4,8,128]{5,4,3,2,0,1:T(8,128)(2,1)S(1)} %get-tuple-element.39), channel_id=1, source_target_pairs={{0,32},{8,40},{16,48},{24,56},{32,0},{40,8},{48,16},{56,24},{64,96... | collective-permute-start | bytes 393224 | tf_op jit(solution)/shard_map/ppermute | solution.py:81
  31.4 4.2 %collective-permute-done.1 = bf16[2,4,2,4,8,128]{5,4,3,2,0,1:T(8,128)(2,1)S(1)} collective-permute-done((bf16[2,4,2,4,8,128]{5,4,3,2,0,1:T(8,128)(2,1)S(1)}, bf16[2,4,2,4,8,128]{5,4,3,2,0,1:T(8,128)(2,1)S(1)}, u32[]{:S(2)}, u32[]{:S(2)}) %collective-permute-start.1) | collective-permute-done | bytes 131104 | tf_op jit(solution)/shard_map/ppermute | solution.py:81
  35.6 3.7 %collective-permute-done.3 = bf16[2,4,2,4,8,128]{5,4,3,2,0,1:T(8,128)(2,1)S(1)} collective-permute-done((bf16[2,4,2,4,8,128]{5,4,3,2,0,1:T(8,128)(2,1)S(1)}, bf16[2,4,2,4,8,128]{5,4,3,2,0,1:T(8,128)(2,1)S(1)}, u32[]{:S(2)}, u32[]{:S(2)}) %collective-permute-start.3) | collective-permute-done | bytes 131104 | tf_op jit(solution)/shard_map/ppermute | solution.py:81
  39.3 2.0 %collective-permute-done.2 = bf16[2,4,2,4,8,128]{5,4,3,2,0,1:T(8,128)(2,1)S(1)} collective-permute-done((bf16[2,4,2,4,8,128]{5,4,3,2,0,1:T(8,128)(2,1)S(1)}, bf16[2,4,2,4,8,128]{5,4,3,2,0,1:T(8,128)(2,1)S(1)}, u32[]{:S(2)}, u32[]{:S(2)}) %collective-permute-start.2) | collective-permute-done | bytes 131104 | tf_op jit(solution)/shard_map/ppermute | solution.py:81
  41.3 0.1 pad_maximum_fusion
  41.4 2.9 %collective-permute-start.6 = (bf16[4,2,2,4,8,128]{5,4,3,2,1,0:T(8,128)(2,1)S(1)}, bf16[4,2,2,4,8,128]{5,4,3,2,1,0:T(8,128)(2,1)S(1)}, u32[]{:S(2)}, u32[]{:S(2)}) collective-permute-start(bf16[4,2,2,4,8,128]{5,4,3,2,1,0:T(8,128)(2,1)S(1)} %get-tuple-element.33), channel_id=1, source_target_pairs={{0,192},{8,200},{16,208},{24,216},{32,224},{40,232},{48,240},{56,2... | collective-permute-start | bytes 393224 | tf_op jit(solution)/shard_map/ppermute | solution.py:81
  44.3 0.8 collective-permute-start.5
  45.1 0.9 collective-permute-start.4
  46.0 6.8 %collective-permute-done.6 = bf16[4,2,2,4,8,128]{5,4,3,2,1,0:T(8,128)(2,1)S(1)} collective-permute-done((bf16[4,2,2,4,8,128]{5,4,3,2,1,0:T(8,128)(2,1)S(1)}, bf16[4,2,2,4,8,128]{5,4,3,2,1,0:T(8,128)(2,1)S(1)}, u32[]{:S(2)}, u32[]{:S(2)}) %collective-permute-start.6) | collective-permute-done | bytes 131104 | tf_op jit(solution)/shard_map/ppermute | solution.py:81
  52.8 1.7 %collective-permute-done.5 = bf16[4,2,2,4,8,128]{5,4,3,2,1,0:T(8,128)(2,1)S(1)} collective-permute-done((bf16[4,2,2,4,8,128]{5,4,3,2,1,0:T(8,128)(2,1)S(1)}, bf16[4,2,2,4,8,128]{5,4,3,2,1,0:T(8,128)(2,1)S(1)}, u32[]{:S(2)}, u32[]{:S(2)}) %collective-permute-start.5) | collective-permute-done | bytes 131104 | tf_op jit(solution)/shard_map/ppermute | solution.py:81
  54.5 2.1 %collective-permute-done.4 = bf16[4,2,2,4,8,128]{5,4,3,2,1,0:T(8,128)(2,1)S(1)} collective-permute-done((bf16[4,2,2,4,8,128]{5,4,3,2,1,0:T(8,128)(2,1)S(1)}, bf16[4,2,2,4,8,128]{5,4,3,2,1,0:T(8,128)(2,1)S(1)}, u32[]{:S(2)}, u32[]{:S(2)}) %collective-permute-start.4) | collective-permute-done | bytes 131104 | tf_op jit(solution)/shard_map/ppermute | solution.py:81
  56.6 0.1 pad_maximum_fusion.1
  56.7 16.4 %all-to-all-done = bf16[256,8,512]{2,1,0:T(8,128)(2,1)S(1)} async-done(((bf16[256,8,512]{2,1,0:T(8,128)(2,1)}), bf16[256,8,512]{2,1,0:T(8,128)(2,1)S(1)}, u32[]{:S(2)}, u32[]{:S(2)}) %all-to-all-start) | async-done | bytes 2097184 | tf_op jit(solution)/shard_map/all_to_all | solution.py:465
  73.1 9.0 %middle.1 = (bf16[32,2,4,8,128]{4,3,2,1,0:T(8,128)(2,1)S(1)}, bf16[2048,512]{1,0:T(8,128)(2,1)}) custom-call(s32[7]{0:T(128)S(1)} %concatenate.3.sc_ref, bf16[2048,512]{1,0:T(8,128)(2,1)S(1)} %bitcast.93, bf16[32,2,4,8,128]{4,3,2,1,0:T(8,128)(2,1)S(1)} %bitcast.95), custom_call_target="tpu_custom_call" | custom-call | tf_op jit(solution)/shard_map/middle/pallas_call | solution.py:398
  82.2 9.2 %all-to-all-start.1 = ((bf16[256,8,512]{2,1,0:T(8,128)(2,1)}), bf16[256,8,512]{2,1,0:T(8,128)(2,1)}, u32[]{:S(2)}, u32[]{:S(2)}) async-start(bf16[256,8,512]{2,1,0:T(8,128)(2,1)} %bitcast.96), calls=%async_computation.1 | async-start | bytes 4194304 | tf_op jit(solution)/shard_map/all_to_all | solution.py:468
  91.4 0.2 collective-permute-start.7
  91.6 1.4 collective-permute-done.7
  93.0 1.6 collective-permute-start.8
  94.6 1.8 %collective-permute-start.10 = (bf16[2,4,2,4,8,128]{5,4,3,0,2,1:T(8,128)(2,1)S(1)}, bf16[2,4,2,4,8,128]{5,4,3,0,2,1:T(8,128)(2,1)S(1)}, u32[]{:S(2)}, u32[]{:S(2)}) collective-permute-start(bf16[2,4,2,4,8,128]{5,4,3,0,2,1:T(8,128)(2,1)S(1)} %get-tuple-element.28), channel_id=1, source_target_pairs={{0,48},{8,56},{16,0},{24,8},{32,16},{40,24},{48,32},{56,40},{64,11... | collective-permute-start | bytes 393224 | tf_op jit(solution)/shard_map/ppermute | solution.py:81
  96.4 1.8 %collective-permute-start.9 = (bf16[2,4,2,4,8,128]{5,4,3,0,2,1:T(8,128)(2,1)S(1)}, bf16[2,4,2,4,8,128]{5,4,3,0,2,1:T(8,128)(2,1)S(1)}, u32[]{:S(2)}, u32[]{:S(2)}) collective-permute-start(bf16[2,4,2,4,8,128]{5,4,3,0,2,1:T(8,128)(2,1)S(1)} %get-tuple-element.29), channel_id=1, source_target_pairs={{0,32},{8,40},{16,48},{24,56},{32,0},{40,8},{48,16},{56,24},{64,96... | collective-permute-start | bytes 393224 | tf_op jit(solution)/shard_map/ppermute | solution.py:81
  98.2 4.3 %collective-permute-done.8 = bf16[2,4,2,4,8,128]{5,4,3,0,2,1:T(8,128)(2,1)S(1)} collective-permute-done((bf16[2,4,2,4,8,128]{5,4,3,0,2,1:T(8,128)(2,1)S(1)}, bf16[2,4,2,4,8,128]{5,4,3,0,2,1:T(8,128)(2,1)S(1)}, u32[]{:S(2)}, u32[]{:S(2)}) %collective-permute-start.8) | collective-permute-done | bytes 131104 | tf_op jit(solution)/shard_map/ppermute | solution.py:81
  102.5 0.3 collective-permute-done.10
  102.8 4.6 %collective-permute-done.9 = bf16[2,4,2,4,8,128]{5,4,3,0,2,1:T(8,128)(2,1)S(1)} collective-permute-done((bf16[2,4,2,4,8,128]{5,4,3,0,2,1:T(8,128)(2,1)S(1)}, bf16[2,4,2,4,8,128]{5,4,3,0,2,1:T(8,128)(2,1)S(1)}, u32[]{:S(2)}, u32[]{:S(2)}) %collective-permute-start.9) | collective-permute-done | bytes 131104 | tf_op jit(solution)/shard_map/ppermute | solution.py:81
  107.3 0.1 pad_maximum_fusion.2
  107.4 3.0 %collective-permute-start.13 = (bf16[4,2,2,4,8,128]{5,4,3,1,0,2:T(8,128)(2,1)S(1)}, bf16[4,2,2,4,8,128]{5,4,3,1,0,2:T(8,128)(2,1)S(1)}, u32[]{:S(2)}, u32[]{:S(2)}) collective-permute-start(bf16[4,2,2,4,8,128]{5,4,3,1,0,2:T(8,128)(2,1)S(1)} %get-tuple-element.23), channel_id=1, source_target_pairs={{0,192},{8,200},{16,208},{24,216},{32,224},{40,232},{48,240},{56,2... | collective-permute-start | bytes 393224 | tf_op jit(solution)/shard_map/ppermute | solution.py:81
  110.4 0.7 collective-permute-start.12
  111.1 0.9 collective-permute-start.11
  112.0 7.1 %collective-permute-done.13 = bf16[4,2,2,4,8,128]{5,4,3,1,0,2:T(8,128)(2,1)S(1)} collective-permute-done((bf16[4,2,2,4,8,128]{5,4,3,1,0,2:T(8,128)(2,1)S(1)}, bf16[4,2,2,4,8,128]{5,4,3,1,0,2:T(8,128)(2,1)S(1)}, u32[]{:S(2)}, u32[]{:S(2)}) %collective-permute-start.13) | collective-permute-done | bytes 131104 | tf_op jit(solution)/shard_map/ppermute | solution.py:81
  119.2 0.9 collective-permute-done.12
  120.1 3.4 %collective-permute-done.11 = bf16[4,2,2,4,8,128]{5,4,3,1,0,2:T(8,128)(2,1)S(1)} collective-permute-done((bf16[4,2,2,4,8,128]{5,4,3,1,0,2:T(8,128)(2,1)S(1)}, bf16[4,2,2,4,8,128]{5,4,3,1,0,2:T(8,128)(2,1)S(1)}, u32[]{:S(2)}, u32[]{:S(2)}) %collective-permute-start.11) | collective-permute-done | bytes 131104 | tf_op jit(solution)/shard_map/ppermute | solution.py:81
  123.5 0.1 pad_maximum_fusion.3
  123.6 0.7 slice_bitcast_fusion
  124.3 5.1 %collective-permute-start.15 = (bf16[32,4,8,128]{3,2,1,0:T(8,128)(2,1)}, bf16[32,4,8,128]{3,2,1,0:T(8,128)(2,1)S(1)}, u32[]{:S(2)}, u32[]{:S(2)}) collective-permute-start(bf16[32,4,8,128]{3,2,1,0:T(8,128)(2,1)} %get-tuple-element.20), channel_id=1, source_target_pairs={{0,3},{1,4},{2,5},{3,6},{4,7},{5,0},{6,1},{7,2},{8,11},{9,12},{10,... | collective-permute-start | bytes 786440 | tf_op jit(solution)/shard_map/ppermute | solution.py:471
  129.4 3.9 %collective-permute-start.14 = (bf16[32,4,8,128]{3,2,1,0:T(8,128)(2,1)S(1)}, bf16[32,4,8,128]{3,2,1,0:T(8,128)(2,1)S(1)}, u32[]{:S(2)}, u32[]{:S(2)}) collective-permute-start(bf16[32,4,8,128]{3,2,1,0:T(8,128)(2,1)S(1)} %get-tuple-element.21), channel_id=1, source_target_pairs={{0,7},{1,0},{2,1},{3,2},{4,3},{5,4},{6,5},{7,6},{8,15},{9,8},{10,9... | collective-permute-start | bytes 786440 | tf_op jit(solution)/shard_map/ppermute | solution.py:470
  133.2 10.6 %all-to-all-done.1 = bf16[256,8,512]{2,1,0:T(8,128)(2,1)} async-done(((bf16[256,8,512]{2,1,0:T(8,128)(2,1)}), bf16[256,8,512]{2,1,0:T(8,128)(2,1)}, u32[]{:S(2)}, u32[]{:S(2)}) %all-to-all-start.1) | async-done | bytes 2097184 | tf_op jit(solution)/shard_map/all_to_all | solution.py:468
  143.8 6.3 %backward.1 = bf16[512,2048]{1,0:T(8,128)(2,1)} custom-call(bf16[16,2,8,8,512]{4,3,2,1,0:T(8,128)(2,1)} %bitcast.59.g_hbm, bf16[16,2,8,8,512]{4,3,2,1,0:T(8,128)(2,1)S(1)} %copy-done.1, f32[8,2,512]{2,1,0:T(2,128)S(1)} %get-tuple-element.16.r_ref, f32[64,1024]{1,0:T(8,128)S(1)} %copy-done.2, f32[24,1024]{1,0:T(8,128)S(1)} %copy-done.4, f32[24,1024]{1,0:T(8,128)S(1)} %copy-done.3), custom_call_target="tpu_custom_call" | custom-call | flops 2147483648 | bytes 10485760 | tf_op jit(solution)/shard_map/backward/pallas_call | solution.py:244
  150.1 4.6 %collective-permute-done.15.down_ref = bf16[32,4,8,128]{3,2,1,0:T(8,128)(2,1)S(1)} collective-permute-done((bf16[32,4,8,128]{3,2,1,0:T(8,128)(2,1)}, bf16[32,4,8,128]{3,2,1,0:T(8,128)(2,1)S(1)}, u32[]{:S(2)}, u32[]{:S(2)}) %collective-permute-start.15) | collective-permute-done | bytes 262176 | tf_op jit(solution)/shard_map/ppermute | solution.py:471
  154.7 2.2 %unpack_correl.1 = f32[3,16,16,256]{3,2,1,0:T(8,128)} custom-call(s32[7]{0:T(128)S(1)} %concatenate.3.sc_ref, bf16[32,4,8,128]{3,2,1,0:T(8,128)(2,1)S(1)} %collective-permute-done.14.up_ref, bf16[32,4,8,128]{3,2,1,0:T(8,128)(2,1)S(1)} %collective-permute-done.15.down_ref), custom_call_target="tpu_custom_call" | custom-call | tf_op jit(solution)/shard_map/unpack_correl/pallas_call | solution.py:443
  (17 shorter events, 0.3 us)
Async XLA Ops:
  6.2 14.3 %copy-start.5 = (s32[1,3]{1,0:T(1,128)S(1)}, s32[1,3]{1,0:T(1,128)}, u32[]{:S(2)}) copy-start(s32[1,3]{1,0:T(1,128)} %param.7) | copy-start | bytes 40
  6.3 66.8 %all-to-all-start = ((bf16[256,8,512]{2,1,0:T(8,128)(2,1)}), bf16[256,8,512]{2,1,0:T(8,128)(2,1)S(1)}, u32[]{:S(2)}, u32[]{:S(2)}) async-start(bf16[256,8,512]{2,1,0:T(8,128)(2,1)} %bitcast.94), calls=%async_computation | async-start | bytes 4194304 | tf_op jit(solution)/shard_map/all_to_all | solution.py:465
  20.6 2.8 %copy-start = (f32[1,3,16,16,2048]{4,3,2,1,0:T(8,128)S(1)}, f32[1,3,16,16,2048]{4,3,2,1,0:T(8,128)}, u32[]{:S(2)}) copy-start(f32[1,3,16,16,2048]{4,3,2,1,0:T(8,128)} %param.8) | copy-start | bytes 18874372
  24.6 1.6 %collective-permute-start = (bf16[4,4,2,4,8,128]{5,4,3,2,1,0:T(8,128)(2,1)S(1)}, bf16[4,4,2,4,8,128]{5,4,3,2,1,0:T(8,128)(2,1)S(1)}, u32[]{:S(2)}, u32[]{:S(2)}) collective-permute-start(bf16[4,4,2,4,8,128]{5,4,3,2,1,0:T(8,128)(2,1)S(1)} %bitcast.103), channel_id=1, source_target_pairs={{0,8},{8,0},{16,24},{24,16},{32,40},{40,32},{48,56},{56,48},{64,72... | collective-permute-start | bytes 786440 | tf_op jit(solution)/shard_map/ppermute | solution.py:81
  26.3 9.3 %collective-permute-start.1 = (bf16[2,4,2,4,8,128]{5,4,3,2,0,1:T(8,128)(2,1)S(1)}, bf16[2,4,2,4,8,128]{5,4,3,2,0,1:T(8,128)(2,1)S(1)}, u32[]{:S(2)}, u32[]{:S(2)}) collective-permute-start(bf16[2,4,2,4,8,128]{5,4,3,2,0,1:T(8,128)(2,1)S(1)} %get-tuple-element.37), channel_id=1, source_target_pairs={{0,16},{8,24},{16,32},{24,40},{32,48},{40,56},{48,0},{56,8},{64,80... | collective-permute-start | bytes 393224 | tf_op jit(solution)/shard_map/ppermute | solution.py:81
  27.9 11.4 %collective-permute-start.3 = (bf16[2,4,2,4,8,128]{5,4,3,2,0,1:T(8,128)(2,1)S(1)}, bf16[2,4,2,4,8,128]{5,4,3,2,0,1:T(8,128)(2,1)S(1)}, u32[]{:S(2)}, u32[]{:S(2)}) collective-permute-start(bf16[2,4,2,4,8,128]{5,4,3,2,0,1:T(8,128)(2,1)S(1)} %get-tuple-element.38), channel_id=1, source_target_pairs={{0,48},{8,56},{16,0},{24,8},{32,16},{40,24},{48,32},{56,40},{64,11... | collective-permute-start | bytes 393224 | tf_op jit(solution)/shard_map/ppermute | solution.py:81
  29.6 11.7 %collective-permute-start.2 = (bf16[2,4,2,4,8,128]{5,4,3,2,0,1:T(8,128)(2,1)S(1)}, bf16[2,4,2,4,8,128]{5,4,3,2,0,1:T(8,128)(2,1)S(1)}, u32[]{:S(2)}, u32[]{:S(2)}) collective-permute-start(bf16[2,4,2,4,8,128]{5,4,3,2,0,1:T(8,128)(2,1)S(1)} %get-tuple-element.39), channel_id=1, source_target_pairs={{0,32},{8,40},{16,48},{24,56},{32,0},{40,8},{48,16},{56,24},{64,96... | collective-permute-start | bytes 393224 | tf_op jit(solution)/shard_map/ppermute | solution.py:81
  41.4 11.4 %collective-permute-start.6 = (bf16[4,2,2,4,8,128]{5,4,3,2,1,0:T(8,128)(2,1)S(1)}, bf16[4,2,2,4,8,128]{5,4,3,2,1,0:T(8,128)(2,1)S(1)}, u32[]{:S(2)}, u32[]{:S(2)}) collective-permute-start(bf16[4,2,2,4,8,128]{5,4,3,2,1,0:T(8,128)(2,1)S(1)} %get-tuple-element.33), channel_id=1, source_target_pairs={{0,192},{8,200},{16,208},{24,216},{32,224},{40,232},{48,240},{56,2... | collective-permute-start | bytes 393224 | tf_op jit(solution)/shard_map/ppermute | solution.py:81
  44.3 10.1 %collective-permute-start.5 = (bf16[4,2,2,4,8,128]{5,4,3,2,1,0:T(8,128)(2,1)S(1)}, bf16[4,2,2,4,8,128]{5,4,3,2,1,0:T(8,128)(2,1)S(1)}, u32[]{:S(2)}, u32[]{:S(2)}) collective-permute-start(bf16[4,2,2,4,8,128]{5,4,3,2,1,0:T(8,128)(2,1)S(1)} %get-tuple-element.34), channel_id=1, source_target_pairs={{0,128},{8,136},{16,144},{24,152},{32,160},{40,168},{48,176},{56,1... | collective-permute-start | bytes 393224 | tf_op jit(solution)/shard_map/ppermute | solution.py:81
  45.1 11.5 %collective-permute-start.4 = (bf16[4,2,2,4,8,128]{5,4,3,2,1,0:T(8,128)(2,1)S(1)}, bf16[4,2,2,4,8,128]{5,4,3,2,1,0:T(8,128)(2,1)S(1)}, u32[]{:S(2)}, u32[]{:S(2)}) collective-permute-start(bf16[4,2,2,4,8,128]{5,4,3,2,1,0:T(8,128)(2,1)S(1)} %get-tuple-element.35), channel_id=1, source_target_pairs={{0,64},{8,72},{16,80},{24,88},{32,96},{40,104},{48,112},{56,120},{... | collective-permute-start | bytes 393224 | tf_op jit(solution)/shard_map/ppermute | solution.py:81
  82.2 61.6 %all-to-all-start.1 = ((bf16[256,8,512]{2,1,0:T(8,128)(2,1)}), bf16[256,8,512]{2,1,0:T(8,128)(2,1)}, u32[]{:S(2)}, u32[]{:S(2)}) async-start(bf16[256,8,512]{2,1,0:T(8,128)(2,1)} %bitcast.96), calls=%async_computation.1 | async-start | bytes 4194304 | tf_op jit(solution)/shard_map/all_to_all | solution.py:468
  91.4 1.6 %collective-permute-start.7 = (bf16[4,4,2,4,8,128]{5,4,3,2,1,0:T(8,128)(2,1)S(1)}, bf16[4,4,2,4,8,128]{5,4,3,2,1,0:T(8,128)(2,1)S(1)}, u32[]{:S(2)}, u32[]{:S(2)}) collective-permute-start(bf16[4,4,2,4,8,128]{5,4,3,2,1,0:T(8,128)(2,1)S(1)} %bitcast.104), channel_id=1, source_target_pairs={{0,8},{8,0},{16,24},{24,16},{32,40},{40,32},{48,56},{56,48},{64,72... | collective-permute-start | bytes 786440 | tf_op jit(solution)/shard_map/ppermute | solution.py:81
  93.0 9.5 %collective-permute-start.8 = (bf16[2,4,2,4,8,128]{5,4,3,0,2,1:T(8,128)(2,1)S(1)}, bf16[2,4,2,4,8,128]{5,4,3,0,2,1:T(8,128)(2,1)S(1)}, u32[]{:S(2)}, u32[]{:S(2)}) collective-permute-start(bf16[2,4,2,4,8,128]{5,4,3,0,2,1:T(8,128)(2,1)S(1)} %get-tuple-element.27), channel_id=1, source_target_pairs={{0,16},{8,24},{16,32},{24,40},{32,48},{40,56},{48,0},{56,8},{64,80... | collective-permute-start | bytes 393224 | tf_op jit(solution)/shard_map/ppermute | solution.py:81
  94.6 8.1 %collective-permute-start.10 = (bf16[2,4,2,4,8,128]{5,4,3,0,2,1:T(8,128)(2,1)S(1)}, bf16[2,4,2,4,8,128]{5,4,3,0,2,1:T(8,128)(2,1)S(1)}, u32[]{:S(2)}, u32[]{:S(2)}) collective-permute-start(bf16[2,4,2,4,8,128]{5,4,3,0,2,1:T(8,128)(2,1)S(1)} %get-tuple-element.28), channel_id=1, source_target_pairs={{0,48},{8,56},{16,0},{24,8},{32,16},{40,24},{48,32},{56,40},{64,11... | collective-permute-start | bytes 393224 | tf_op jit(solution)/shard_map/ppermute | solution.py:81
  96.4 10.9 %collective-permute-start.9 = (bf16[2,4,2,4,8,128]{5,4,3,0,2,1:T(8,128)(2,1)S(1)}, bf16[2,4,2,4,8,128]{5,4,3,0,2,1:T(8,128)(2,1)S(1)}, u32[]{:S(2)}, u32[]{:S(2)}) collective-permute-start(bf16[2,4,2,4,8,128]{5,4,3,0,2,1:T(8,128)(2,1)S(1)} %get-tuple-element.29), channel_id=1, source_target_pairs={{0,32},{8,40},{16,48},{24,56},{32,0},{40,8},{48,16},{56,24},{64,96... | collective-permute-start | bytes 393224 | tf_op jit(solution)/shard_map/ppermute | solution.py:81
  107.3 36.5 %copy-start.1 = (bf16[16,2,8,8,512]{4,3,2,1,0:T(8,128)(2,1)S(1)}, bf16[16,2,8,8,512]{4,3,2,1,0:T(8,128)(2,1)}, u32[]{:S(2)}) copy-start(bf16[16,2,8,8,512]{4,3,2,1,0:T(8,128)(2,1)} %get-tuple-element.13.y_ref) | copy-start | bytes 6291460
  107.3 36.5 %copy-start.2 = (f32[64,1024]{1,0:T(8,128)S(1)}, f32[64,1024]{1,0:T(8,128)}, u32[]{:S(2)}) copy-start(f32[64,1024]{1,0:T(8,128)} %constant.39.clone.a_hbm.a_ref) | copy-start | bytes 786436
  107.3 36.5 %copy-start.3 = (f32[24,1024]{1,0:T(8,128)S(1)}, f32[24,1024]{1,0:T(8,128)}, u32[]{:S(2)}) copy-start(f32[24,1024]{1,0:T(8,128)} %constant.41.clone.s_hbm.s_ref) | copy-start | bytes 294916
  107.3 36.5 %copy-start.4 = (f32[24,1024]{1,0:T(8,128)S(1)}, f32[24,1024]{1,0:T(8,128)}, u32[]{:S(2)}) copy-start(f32[24,1024]{1,0:T(8,128)} %constant.40.clone.c_hbm.c_ref) | copy-start | bytes 294916
  107.4 11.7 %collective-permute-start.13 = (bf16[4,2,2,4,8,128]{5,4,3,1,0,2:T(8,128)(2,1)S(1)}, bf16[4,2,2,4,8,128]{5,4,3,1,0,2:T(8,128)(2,1)S(1)}, u32[]{:S(2)}, u32[]{:S(2)}) collective-permute-start(bf16[4,2,2,4,8,128]{5,4,3,1,0,2:T(8,128)(2,1)S(1)} %get-tuple-element.23), channel_id=1, source_target_pairs={{0,192},{8,200},{16,208},{24,216},{32,224},{40,232},{48,240},{56,2... | collective-permute-start | bytes 393224 | tf_op jit(solution)/shard_map/ppermute | solution.py:81
  110.4 9.7 %collective-permute-start.12 = (bf16[4,2,2,4,8,128]{5,4,3,1,0,2:T(8,128)(2,1)S(1)}, bf16[4,2,2,4,8,128]{5,4,3,1,0,2:T(8,128)(2,1)S(1)}, u32[]{:S(2)}, u32[]{:S(2)}) collective-permute-start(bf16[4,2,2,4,8,128]{5,4,3,1,0,2:T(8,128)(2,1)S(1)} %get-tuple-element.24), channel_id=1, source_target_pairs={{0,128},{8,136},{16,144},{24,152},{32,160},{40,168},{48,176},{56,1... | collective-permute-start | bytes 393224 | tf_op jit(solution)/shard_map/ppermute | solution.py:81
  111.1 12.4 %collective-permute-start.11 = (bf16[4,2,2,4,8,128]{5,4,3,1,0,2:T(8,128)(2,1)S(1)}, bf16[4,2,2,4,8,128]{5,4,3,1,0,2:T(8,128)(2,1)S(1)}, u32[]{:S(2)}, u32[]{:S(2)}) collective-permute-start(bf16[4,2,2,4,8,128]{5,4,3,1,0,2:T(8,128)(2,1)S(1)} %get-tuple-element.25), channel_id=1, source_target_pairs={{0,64},{8,72},{16,80},{24,88},{32,96},{40,104},{48,112},{56,120},{... | collective-permute-start | bytes 393224 | tf_op jit(solution)/shard_map/ppermute | solution.py:81
  124.3 30.4 %collective-permute-start.15 = (bf16[32,4,8,128]{3,2,1,0:T(8,128)(2,1)}, bf16[32,4,8,128]{3,2,1,0:T(8,128)(2,1)S(1)}, u32[]{:S(2)}, u32[]{:S(2)}) collective-permute-start(bf16[32,4,8,128]{3,2,1,0:T(8,128)(2,1)} %get-tuple-element.20), channel_id=1, source_target_pairs={{0,3},{1,4},{2,5},{3,6},{4,7},{5,0},{6,1},{7,2},{8,11},{9,12},{10,... | collective-permute-start | bytes 786440 | tf_op jit(solution)/shard_map/ppermute | solution.py:471
  129.4 25.3 %collective-permute-start.14 = (bf16[32,4,8,128]{3,2,1,0:T(8,128)(2,1)S(1)}, bf16[32,4,8,128]{3,2,1,0:T(8,128)(2,1)S(1)}, u32[]{:S(2)}, u32[]{:S(2)}) collective-permute-start(bf16[32,4,8,128]{3,2,1,0:T(8,128)(2,1)S(1)} %get-tuple-element.21), channel_id=1, source_target_pairs={{0,7},{1,0},{2,1},{3,2},{4,3},{5,4},{6,5},{7,6},{8,15},{9,8},{10,9... | collective-permute-start | bytes 786440 | tf_op jit(solution)/shard_map/ppermute | solution.py:470

commit v9 on v8

--- a/solution.py
+++ b/solution.py
@@ -30,11 +30,11 @@
 
 
 def half_of(g):
-    return jnp.where(jnp.logical_and(g >= 1, g <= 4), 1, 0)
+    return jnp.where(jnp.logical_and(g >= 2, g <= 5), 0, 1)
 
 
 def quarter_of(g):
-    return jnp.where(half_of(g) == 1, g - 1, (g + 3) % GRP)
+    return jnp.where(half_of(g) == 0, g - 2, (g + 2) % GRP)
 
 
 def table_parts():
@@ -108,8 +108,8 @@
 
 
 def plane_bands(g):
-    h = 1 if 1 <= g <= 4 else 0
-    q = g - 1 if h == 1 else (g + 3) % GRP
+    h = 0 if 2 <= g <= 5 else 1
+    q = g - 2 if h == 0 else (g + 2) % GRP
     return (q * 4 + h * 2, q * 4 + h * 2 + 1)
 
 
@@ -467,8 +467,8 @@
     corr, grad = middle(scalars, moved.reshape(2048, CH), seen)
     returned = lax.all_to_all(grad.reshape(WINS, 8, CH), ("win", "grp"), 0, 0)
     corr = exchange(corr)
-    up = lax.ppermute(corr[:, 0], "grp", [(i, (i - 1) % GRP) for i in range(GRP)])
-    down = lax.ppermute(corr[:, 1], "grp", [(i, (i + 3) % GRP) for i in range(GRP)])
+    up = lax.ppermute(corr[:, 0], "grp", [(i, (i + 2) % GRP) for i in range(GRP)])
+    down = lax.ppermute(corr[:, 1], "grp", [(i, (i - 2) % GRP) for i in range(GRP)])
     trace_grad = backward(returned.reshape(16, 2, GRP, 8, CH), white, inverse, consts)
     up, down, trace_grad = lax.optimization_barrier((up, down, trace_grad))
     correl = unpack_correl(scalars, up, down)

time: 160 us -> 154 us (0.963)
  waiting for transfers between devices: 75.5 us -> 71.9 us
    ppermute x2, waiting for transfers between devices: 4.62 us -> 0.01 us  [the longest x1 0.01 us: on_device(): lax.ppermute(corr[:, 1], 'grp', [(i, (i - 2) % GRP) for i in range(GRP)])]
  transfers between devices with their start and end apart: 18 -> 18, of which waited for: 17 -> 16; matrix products, arithmetic and copies ran while one was open for 1% -> 1% of each run, Pallas kernels for 5% -> 5%
where the time goes in v9:
time: 154 us; the launch traced here: 152 us
  waiting for transfers between devices  71.9 us (47%)
  starting transfers between devices  50.7 us (33%)
  Pallas kernels  24.3 us (16%)
  local copies, waits for them, and re-layouts  3.78 us (2%)
    ppermute x14, waiting for transfers between devices, hop(): return lax.ppermute(array, 'win', pairs)  43.9 us
    ppermute x14, starting transfers between devices, hop(): return lax.ppermute(array, 'win', pairs)  19.9 us
    all_to_all x1, waiting for transfers between devices, on_device(): moved = lax.all_to_all(white.reshape(WINS, 8, CH), ('win', 'grp'), 0, 0)  16.4 us
    all_to_all x1, starting transfers between devices, on_device(): moved = lax.all_to_all(white.reshape(WINS, 8, CH), ('win', 'grp'), 0, 0)  14.2 us
    all_to_all x1, waiting for transfers between devices, on_device(): returned = lax.all_to_all(grad.reshape(WINS, 8, CH), ('win', 'grp'), 0, 0)  11.6 us
    all_to_all x1, starting transfers between devices, on_device(): returned = lax.all_to_all(grad.reshape(WINS, 8, CH), ('win', 'grp'), 0, 0)  9.17 us
    pallas_call x1, Pallas kernels, middle(): pl.pallas_call(middle_kernel, in_specs=[IN_SMEM, IN_VMEM, IN_VMEM], out_s...  9.04 us
    pallas_call x1, Pallas kernels, backward(): pl.pallas_call(backward_kernel, in_specs=[IN_HBM] + [IN_VMEM] * 5, out_sp...  6.25 us
  transfers between devices with their start and end apart: 18, of which 16 were waited for; matrix products, arithmetic and copies ran while one was open for 1% of the time, Pallas kernels for 5%

profile of v9, /device:TPU:64, one launch (start us, length us, event | category | flops | bytes accessed | tf_op | source)
XLA Modules:
  0.0 151.8 jit_solution(12410975899000244739)
XLA Ops:
  0.6 5.6 %forward.1 = (bf16[16,2,8,8,512]{4,3,2,1,0:T(8,128)(2,1)}, f32[8,2,512]{2,1,0:T(2,128)S(1)}) custom-call(bf16[512,2048]{1,0:T(8,128)(2,1)} %bitcast.118, f32[64,1024]{1,0:T(8,128)} %constant.39.clone.a_hbm.a_ref, f32[24,1024]{1,0:T(8,128)} %constant.40.clone.c_hbm.c_ref, f32[24,1024]{1,0:T(8,128)} %constant.41.clone.s_hbm.s_ref), custom_call_target="tpu_custom_call" | custom-call | flops 2147483648 | bytes 8388608 | tf_op jit(solution)/shard_map/forward/pallas_call | solution.py:171
  6.2 0.0 copy-start.5
  6.3 14.2 %all-to-all-start = ((bf16[256,8,512]{2,1,0:T(8,128)(2,1)}), bf16[256,8,512]{2,1,0:T(8,128)(2,1)S(1)}, u32[]{:S(2)}, u32[]{:S(2)}) async-start(bf16[256,8,512]{2,1,0:T(8,128)(2,1)} %bitcast.94), calls=%async_computation | async-start | bytes 4194304 | tf_op jit(solution)/shard_map/all_to_all | solution.py:465
  20.5 0.1 concatenate.3.sc_ref
  20.6 2.8 %copy-done = f32[1,3,16,16,2048]{4,3,2,1,0:T(8,128)S(1)} copy-done((f32[1,3,16,16,2048]{4,3,2,1,0:T(8,128)S(1)}, f32[1,3,16,16,2048]{4,3,2,1,0:T(8,128)}, u32[]{:S(2)}) %copy-start) | copy-done | bytes 6291480
  23.4 1.2 pack_observed.1
  24.6 0.2 collective-permute-start
  24.9 1.4 collective-permute-done
  26.3 1.6 %collective-permute-start.1 = (bf16[2,4,2,4,8,128]{5,4,3,2,0,1:T(8,128)(2,1)S(1)}, bf16[2,4,2,4,8,128]{5,4,3,2,0,1:T(8,128)(2,1)S(1)}, u32[]{:S(2)}, u32[]{:S(2)}) collective-permute-start(bf16[2,4,2,4,8,128]{5,4,3,2,0,1:T(8,128)(2,1)S(1)} %get-tuple-element.37), channel_id=1, source_target_pairs={{0,16},{8,24},{16,32},{24,40},{32,48},{40,56},{48,0},{56,8},{64,80... | collective-permute-start | bytes 393224 | tf_op jit(solution)/shard_map/ppermute | solution.py:81
  27.9 1.8 %collective-permute-start.3 = (bf16[2,4,2,4,8,128]{5,4,3,2,0,1:T(8,128)(2,1)S(1)}, bf16[2,4,2,4,8,128]{5,4,3,2,0,1:T(8,128)(2,1)S(1)}, u32[]{:S(2)}, u32[]{:S(2)}) collective-permute-start(bf16[2,4,2,4,8,128]{5,4,3,2,0,1:T(8,128)(2,1)S(1)} %get-tuple-element.38), channel_id=1, source_target_pairs={{0,48},{8,56},{16,0},{24,8},{32,16},{40,24},{48,32},{56,40},{64,11... | collective-permute-start | bytes 393224 | tf_op jit(solution)/shard_map/ppermute | solution.py:81
  29.6 1.8 %collective-permute-start.2 = (bf16[2,4,2,4,8,128]{5,4,3,2,0,1:T(8,128)(2,1)S(1)}, bf16[2,4,2,4,8,128]{5,4,3,2,0,1:T(8,128)(2,1)S(1)}, u32[]{:S(2)}, u32[]{:S(2)}) collective-permute-start(bf16[2,4,2,4,8,128]{5,4,3,2,0,1:T(8,128)(2,1)S(1)} %get-tuple-element.39), channel_id=1, source_target_pairs={{0,32},{8,40},{16,48},{24,56},{32,0},{40,8},{48,16},{56,24},{64,96... | collective-permute-start | bytes 393224 | tf_op jit(solution)/shard_map/ppermute | solution.py:81
  31.4 4.2 %collective-permute-done.1 = bf16[2,4,2,4,8,128]{5,4,3,2,0,1:T(8,128)(2,1)S(1)} collective-permute-done((bf16[2,4,2,4,8,128]{5,4,3,2,0,1:T(8,128)(2,1)S(1)}, bf16[2,4,2,4,8,128]{5,4,3,2,0,1:T(8,128)(2,1)S(1)}, u32[]{:S(2)}, u32[]{:S(2)}) %collective-permute-start.1) | collective-permute-done | bytes 131104 | tf_op jit(solution)/shard_map/ppermute | solution.py:81
  35.6 3.7 %collective-permute-done.3 = bf16[2,4,2,4,8,128]{5,4,3,2,0,1:T(8,128)(2,1)S(1)} collective-permute-done((bf16[2,4,2,4,8,128]{5,4,3,2,0,1:T(8,128)(2,1)S(1)}, bf16[2,4,2,4,8,128]{5,4,3,2,0,1:T(8,128)(2,1)S(1)}, u32[]{:S(2)}, u32[]{:S(2)}) %collective-permute-start.3) | collective-permute-done | bytes 131104 | tf_op jit(solution)/shard_map/ppermute | solution.py:81
  39.3 2.0 %collective-permute-done.2 = bf16[2,4,2,4,8,128]{5,4,3,2,0,1:T(8,128)(2,1)S(1)} collective-permute-done((bf16[2,4,2,4,8,128]{5,4,3,2,0,1:T(8,128)(2,1)S(1)}, bf16[2,4,2,4,8,128]{5,4,3,2,0,1:T(8,128)(2,1)S(1)}, u32[]{:S(2)}, u32[]{:S(2)}) %collective-permute-start.2) | collective-permute-done | bytes 131104 | tf_op jit(solution)/shard_map/ppermute | solution.py:81
  41.3 0.1 pad_maximum_fusion
  41.4 2.9 %collective-permute-start.6 = (bf16[4,2,2,4,8,128]{5,4,3,2,1,0:T(8,128)(2,1)S(1)}, bf16[4,2,2,4,8,128]{5,4,3,2,1,0:T(8,128)(2,1)S(1)}, u32[]{:S(2)}, u32[]{:S(2)}) collective-permute-start(bf16[4,2,2,4,8,128]{5,4,3,2,1,0:T(8,128)(2,1)S(1)} %get-tuple-element.33), channel_id=1, source_target_pairs={{0,192},{8,200},{16,208},{24,216},{32,224},{40,232},{48,240},{56,2... | collective-permute-start | bytes 393224 | tf_op jit(solution)/shard_map/ppermute | solution.py:81
  44.3 0.8 collective-permute-start.5
  45.1 0.9 collective-permute-start.4
  46.0 6.8 %collective-permute-done.6 = bf16[4,2,2,4,8,128]{5,4,3,2,1,0:T(8,128)(2,1)S(1)} collective-permute-done((bf16[4,2,2,4,8,128]{5,4,3,2,1,0:T(8,128)(2,1)S(1)}, bf16[4,2,2,4,8,128]{5,4,3,2,1,0:T(8,128)(2,1)S(1)}, u32[]{:S(2)}, u32[]{:S(2)}) %collective-permute-start.6) | collective-permute-done | bytes 131104 | tf_op jit(solution)/shard_map/ppermute | solution.py:81
  52.8 1.7 %collective-permute-done.5 = bf16[4,2,2,4,8,128]{5,4,3,2,1,0:T(8,128)(2,1)S(1)} collective-permute-done((bf16[4,2,2,4,8,128]{5,4,3,2,1,0:T(8,128)(2,1)S(1)}, bf16[4,2,2,4,8,128]{5,4,3,2,1,0:T(8,128)(2,1)S(1)}, u32[]{:S(2)}, u32[]{:S(2)}) %collective-permute-start.5) | collective-permute-done | bytes 131104 | tf_op jit(solution)/shard_map/ppermute | solution.py:81
  54.5 2.1 %collective-permute-done.4 = bf16[4,2,2,4,8,128]{5,4,3,2,1,0:T(8,128)(2,1)S(1)} collective-permute-done((bf16[4,2,2,4,8,128]{5,4,3,2,1,0:T(8,128)(2,1)S(1)}, bf16[4,2,2,4,8,128]{5,4,3,2,1,0:T(8,128)(2,1)S(1)}, u32[]{:S(2)}, u32[]{:S(2)}) %collective-permute-start.4) | collective-permute-done | bytes 131104 | tf_op jit(solution)/shard_map/ppermute | solution.py:81
  56.6 0.1 pad_maximum_fusion.1
  56.7 16.4 %all-to-all-done = bf16[256,8,512]{2,1,0:T(8,128)(2,1)S(1)} async-done(((bf16[256,8,512]{2,1,0:T(8,128)(2,1)}), bf16[256,8,512]{2,1,0:T(8,128)(2,1)S(1)}, u32[]{:S(2)}, u32[]{:S(2)}) %all-to-all-start) | async-done | bytes 2097184 | tf_op jit(solution)/shard_map/all_to_all | solution.py:465
  73.1 9.0 %middle.1 = (bf16[32,2,4,8,128]{4,3,2,1,0:T(8,128)(2,1)S(1)}, bf16[2048,512]{1,0:T(8,128)(2,1)}) custom-call(s32[7]{0:T(128)S(1)} %concatenate.3.sc_ref, bf16[2048,512]{1,0:T(8,128)(2,1)S(1)} %bitcast.93, bf16[32,2,4,8,128]{4,3,2,1,0:T(8,128)(2,1)S(1)} %bitcast.95), custom_call_target="tpu_custom_call" | custom-call | tf_op jit(solution)/shard_map/middle/pallas_call | solution.py:398
  82.2 9.2 %all-to-all-start.1 = ((bf16[256,8,512]{2,1,0:T(8,128)(2,1)}), bf16[256,8,512]{2,1,0:T(8,128)(2,1)}, u32[]{:S(2)}, u32[]{:S(2)}) async-start(bf16[256,8,512]{2,1,0:T(8,128)(2,1)} %bitcast.96), calls=%async_computation.1 | async-start | bytes 4194304 | tf_op jit(solution)/shard_map/all_to_all | solution.py:468
  91.4 0.2 collective-permute-start.7
  91.6 1.4 collective-permute-done.7
  93.0 1.6 %collective-permute-start.8 = (bf16[2,4,2,4,8,128]{5,4,3,0,2,1:T(8,128)(2,1)S(1)}, bf16[2,4,2,4,8,128]{5,4,3,0,2,1:T(8,128)(2,1)S(1)}, u32[]{:S(2)}, u32[]{:S(2)}) collective-permute-start(bf16[2,4,2,4,8,128]{5,4,3,0,2,1:T(8,128)(2,1)S(1)} %get-tuple-element.27), channel_id=1, source_target_pairs={{0,16},{8,24},{16,32},{24,40},{32,48},{40,56},{48,0},{56,8},{64,80... | collective-permute-start | bytes 393224 | tf_op jit(solution)/shard_map/ppermute | solution.py:81
  94.6 1.8 %collective-permute-start.10 = (bf16[2,4,2,4,8,128]{5,4,3,0,2,1:T(8,128)(2,1)S(1)}, bf16[2,4,2,4,8,128]{5,4,3,0,2,1:T(8,128)(2,1)S(1)}, u32[]{:S(2)}, u32[]{:S(2)}) collective-permute-start(bf16[2,4,2,4,8,128]{5,4,3,0,2,1:T(8,128)(2,1)S(1)} %get-tuple-element.28), channel_id=1, source_target_pairs={{0,48},{8,56},{16,0},{24,8},{32,16},{40,24},{48,32},{56,40},{64,11... | collective-permute-start | bytes 393224 | tf_op jit(solution)/shard_map/ppermute | solution.py:81
  96.4 1.8 %collective-permute-start.9 = (bf16[2,4,2,4,8,128]{5,4,3,0,2,1:T(8,128)(2,1)S(1)}, bf16[2,4,2,4,8,128]{5,4,3,0,2,1:T(8,128)(2,1)S(1)}, u32[]{:S(2)}, u32[]{:S(2)}) collective-permute-start(bf16[2,4,2,4,8,128]{5,4,3,0,2,1:T(8,128)(2,1)S(1)} %get-tuple-element.29), channel_id=1, source_target_pairs={{0,32},{8,40},{16,48},{24,56},{32,0},{40,8},{48,16},{56,24},{64,96... | collective-permute-start | bytes 393224 | tf_op jit(solution)/shard_map/ppermute | solution.py:81
  98.2 4.3 %collective-permute-done.8 = bf16[2,4,2,4,8,128]{5,4,3,0,2,1:T(8,128)(2,1)S(1)} collective-permute-done((bf16[2,4,2,4,8,128]{5,4,3,0,2,1:T(8,128)(2,1)S(1)}, bf16[2,4,2,4,8,128]{5,4,3,0,2,1:T(8,128)(2,1)S(1)}, u32[]{:S(2)}, u32[]{:S(2)}) %collective-permute-start.8) | collective-permute-done | bytes 131104 | tf_op jit(solution)/shard_map/ppermute | solution.py:81
  102.5 0.3 collective-permute-done.10
  102.8 4.6 %collective-permute-done.9 = bf16[2,4,2,4,8,128]{5,4,3,0,2,1:T(8,128)(2,1)S(1)} collective-permute-done((bf16[2,4,2,4,8,128]{5,4,3,0,2,1:T(8,128)(2,1)S(1)}, bf16[2,4,2,4,8,128]{5,4,3,0,2,1:T(8,128)(2,1)S(1)}, u32[]{:S(2)}, u32[]{:S(2)}) %collective-permute-start.9) | collective-permute-done | bytes 131104 | tf_op jit(solution)/shard_map/ppermute | solution.py:81
  107.3 0.1 pad_maximum_fusion.2
  107.4 3.0 %collective-permute-start.13 = (bf16[4,2,2,4,8,128]{5,4,3,1,0,2:T(8,128)(2,1)S(1)}, bf16[4,2,2,4,8,128]{5,4,3,1,0,2:T(8,128)(2,1)S(1)}, u32[]{:S(2)}, u32[]{:S(2)}) collective-permute-start(bf16[4,2,2,4,8,128]{5,4,3,1,0,2:T(8,128)(2,1)S(1)} %get-tuple-element.23), channel_id=1, source_target_pairs={{0,192},{8,200},{16,208},{24,216},{32,224},{40,232},{48,240},{56,2... | collective-permute-start | bytes 393224 | tf_op jit(solution)/shard_map/ppermute | solution.py:81
  110.4 0.7 collective-permute-start.12
  111.1 0.9 collective-permute-start.11
  112.0 7.1 %collective-permute-done.13 = bf16[4,2,2,4,8,128]{5,4,3,1,0,2:T(8,128)(2,1)S(1)} collective-permute-done((bf16[4,2,2,4,8,128]{5,4,3,1,0,2:T(8,128)(2,1)S(1)}, bf16[4,2,2,4,8,128]{5,4,3,1,0,2:T(8,128)(2,1)S(1)}, u32[]{:S(2)}, u32[]{:S(2)}) %collective-permute-start.13) | collective-permute-done | bytes 131104 | tf_op jit(solution)/shard_map/ppermute | solution.py:81
  119.2 0.9 collective-permute-done.12
  120.1 3.4 %collective-permute-done.11 = bf16[4,2,2,4,8,128]{5,4,3,1,0,2:T(8,128)(2,1)S(1)} collective-permute-done((bf16[4,2,2,4,8,128]{5,4,3,1,0,2:T(8,128)(2,1)S(1)}, bf16[4,2,2,4,8,128]{5,4,3,1,0,2:T(8,128)(2,1)S(1)}, u32[]{:S(2)}, u32[]{:S(2)}) %collective-permute-start.11) | collective-permute-done | bytes 131104 | tf_op jit(solution)/shard_map/ppermute | solution.py:81
  123.5 0.1 pad_maximum_fusion.3
  123.6 0.7 slice_bitcast_fusion
  124.3 2.5 %collective-permute-start.15 = (bf16[32,4,8,128]{3,2,1,0:T(8,128)(2,1)}, bf16[32,4,8,128]{3,2,1,0:T(8,128)(2,1)S(1)}, u32[]{:S(2)}, u32[]{:S(2)}) collective-permute-start(bf16[32,4,8,128]{3,2,1,0:T(8,128)(2,1)} %get-tuple-element.20), channel_id=1, source_target_pairs={{0,6},{1,7},{2,0},{3,1},{4,2},{5,3},{6,4},{7,5},{8,14},{9,15},{10,... | collective-permute-start | bytes 786440 | tf_op jit(solution)/shard_map/ppermute | solution.py:471
  126.8 5.0 %collective-permute-start.14 = (bf16[32,4,8,128]{3,2,1,0:T(8,128)(2,1)S(1)}, bf16[32,4,8,128]{3,2,1,0:T(8,128)(2,1)S(1)}, u32[]{:S(2)}, u32[]{:S(2)}) collective-permute-start(bf16[32,4,8,128]{3,2,1,0:T(8,128)(2,1)S(1)} %get-tuple-element.21), channel_id=1, source_target_pairs={{0,2},{1,3},{2,4},{3,5},{4,6},{5,7},{6,0},{7,1},{8,10},{9,11},{10,... | collective-permute-start | bytes 786440 | tf_op jit(solution)/shard_map/ppermute | solution.py:470
  131.7 11.6 %all-to-all-done.1 = bf16[256,8,512]{2,1,0:T(8,128)(2,1)} async-done(((bf16[256,8,512]{2,1,0:T(8,128)(2,1)}), bf16[256,8,512]{2,1,0:T(8,128)(2,1)}, u32[]{:S(2)}, u32[]{:S(2)}) %all-to-all-start.1) | async-done | bytes 2097184 | tf_op jit(solution)/shard_map/all_to_all | solution.py:468
  143.4 6.3 %backward.1 = bf16[512,2048]{1,0:T(8,128)(2,1)} custom-call(bf16[16,2,8,8,512]{4,3,2,1,0:T(8,128)(2,1)} %bitcast.59.g_hbm, bf16[16,2,8,8,512]{4,3,2,1,0:T(8,128)(2,1)S(1)} %copy-done.1, f32[8,2,512]{2,1,0:T(2,128)S(1)} %get-tuple-element.16.r_ref, f32[64,1024]{1,0:T(8,128)S(1)} %copy-done.2, f32[24,1024]{1,0:T(8,128)S(1)} %copy-done.4, f32[24,1024]{1,0:T(8,128)S(1)} %copy-done.3), custom_call_target="tpu_custom_call" | custom-call | flops 2147483648 | bytes 10485760 | tf_op jit(solution)/shard_map/backward/pallas_call | solution.py:244
  149.6 0.0 collective-permute-done.15.down_ref
  149.6 2.2 %unpack_correl.1 = f32[3,16,16,256]{3,2,1,0:T(8,128)} custom-call(s32[7]{0:T(128)S(1)} %concatenate.3.sc_ref, bf16[32,4,8,128]{3,2,1,0:T(8,128)(2,1)S(1)} %collective-permute-done.14.up_ref, bf16[32,4,8,128]{3,2,1,0:T(8,128)(2,1)S(1)} %collective-permute-done.15.down_ref), custom_call_target="tpu_custom_call" | custom-call | tf_op jit(solution)/shard_map/unpack_correl/pallas_call | solution.py:443
  (17 shorter events, 0.3 us)
Async XLA Ops:
  6.2 14.3 %copy-start.5 = (s32[1,3]{1,0:T(1,128)S(1)}, s32[1,3]{1,0:T(1,128)}, u32[]{:S(2)}) copy-start(s32[1,3]{1,0:T(1,128)} %param.7) | copy-start | bytes 40
  6.3 66.8 %all-to-all-start = ((bf16[256,8,512]{2,1,0:T(8,128)(2,1)}), bf16[256,8,512]{2,1,0:T(8,128)(2,1)S(1)}, u32[]{:S(2)}, u32[]{:S(2)}) async-start(bf16[256,8,512]{2,1,0:T(8,128)(2,1)} %bitcast.94), calls=%async_computation | async-start | bytes 4194304 | tf_op jit(solution)/shard_map/all_to_all | solution.py:465
  20.6 2.8 %copy-start = (f32[1,3,16,16,2048]{4,3,2,1,0:T(8,128)S(1)}, f32[1,3,16,16,2048]{4,3,2,1,0:T(8,128)}, u32[]{:S(2)}) copy-start(f32[1,3,16,16,2048]{4,3,2,1,0:T(8,128)} %param.8) | copy-start | bytes 18874372
  24.6 1.6 %collective-permute-start = (bf16[4,4,2,4,8,128]{5,4,3,2,1,0:T(8,128)(2,1)S(1)}, bf16[4,4,2,4,8,128]{5,4,3,2,1,0:T(8,128)(2,1)S(1)}, u32[]{:S(2)}, u32[]{:S(2)}) collective-permute-start(bf16[4,4,2,4,8,128]{5,4,3,2,1,0:T(8,128)(2,1)S(1)} %bitcast.103), channel_id=1, source_target_pairs={{0,8},{8,0},{16,24},{24,16},{32,40},{40,32},{48,56},{56,48},{64,72... | collective-permute-start | bytes 786440 | tf_op jit(solution)/shard_map/ppermute | solution.py:81
  26.3 9.3 %collective-permute-start.1 = (bf16[2,4,2,4,8,128]{5,4,3,2,0,1:T(8,128)(2,1)S(1)}, bf16[2,4,2,4,8,128]{5,4,3,2,0,1:T(8,128)(2,1)S(1)}, u32[]{:S(2)}, u32[]{:S(2)}) collective-permute-start(bf16[2,4,2,4,8,128]{5,4,3,2,0,1:T(8,128)(2,1)S(1)} %get-tuple-element.37), channel_id=1, source_target_pairs={{0,16},{8,24},{16,32},{24,40},{32,48},{40,56},{48,0},{56,8},{64,80... | collective-permute-start | bytes 393224 | tf_op jit(solution)/shard_map/ppermute | solution.py:81
  27.9 11.4 %collective-permute-start.3 = (bf16[2,4,2,4,8,128]{5,4,3,2,0,1:T(8,128)(2,1)S(1)}, bf16[2,4,2,4,8,128]{5,4,3,2,0,1:T(8,128)(2,1)S(1)}, u32[]{:S(2)}, u32[]{:S(2)}) collective-permute-start(bf16[2,4,2,4,8,128]{5,4,3,2,0,1:T(8,128)(2,1)S(1)} %get-tuple-element.38), channel_id=1, source_target_pairs={{0,48},{8,56},{16,0},{24,8},{32,16},{40,24},{48,32},{56,40},{64,11... | collective-permute-start | bytes 393224 | tf_op jit(solution)/shard_map/ppermute | solution.py:81
  29.6 11.7 %collective-permute-start.2 = (bf16[2,4,2,4,8,128]{5,4,3,2,0,1:T(8,128)(2,1)S(1)}, bf16[2,4,2,4,8,128]{5,4,3,2,0,1:T(8,128)(2,1)S(1)}, u32[]{:S(2)}, u32[]{:S(2)}) collective-permute-start(bf16[2,4,2,4,8,128]{5,4,3,2,0,1:T(8,128)(2,1)S(1)} %get-tuple-element.39), channel_id=1, source_target_pairs={{0,32},{8,40},{16,48},{24,56},{32,0},{40,8},{48,16},{56,24},{64,96... | collective-permute-start | bytes 393224 | tf_op jit(solution)/shard_map/ppermute | solution.py:81
  41.4 11.4 %collective-permute-start.6 = (bf16[4,2,2,4,8,128]{5,4,3,2,1,0:T(8,128)(2,1)S(1)}, bf16[4,2,2,4,8,128]{5,4,3,2,1,0:T(8,128)(2,1)S(1)}, u32[]{:S(2)}, u32[]{:S(2)}) collective-permute-start(bf16[4,2,2,4,8,128]{5,4,3,2,1,0:T(8,128)(2,1)S(1)} %get-tuple-element.33), channel_id=1, source_target_pairs={{0,192},{8,200},{16,208},{24,216},{32,224},{40,232},{48,240},{56,2... | collective-permute-start | bytes 393224 | tf_op jit(solution)/shard_map/ppermute | solution.py:81
  44.3 10.1 %collective-permute-start.5 = (bf16[4,2,2,4,8,128]{5,4,3,2,1,0:T(8,128)(2,1)S(1)}, bf16[4,2,2,4,8,128]{5,4,3,2,1,0:T(8,128)(2,1)S(1)}, u32[]{:S(2)}, u32[]{:S(2)}) collective-permute-start(bf16[4,2,2,4,8,128]{5,4,3,2,1,0:T(8,128)(2,1)S(1)} %get-tuple-element.34), channel_id=1, source_target_pairs={{0,128},{8,136},{16,144},{24,152},{32,160},{40,168},{48,176},{56,1... | collective-permute-start | bytes 393224 | tf_op jit(solution)/shard_map/ppermute | solution.py:81
  45.1 11.5 %collective-permute-start.4 = (bf16[4,2,2,4,8,128]{5,4,3,2,1,0:T(8,128)(2,1)S(1)}, bf16[4,2,2,4,8,128]{5,4,3,2,1,0:T(8,128)(2,1)S(1)}, u32[]{:S(2)}, u32[]{:S(2)}) collective-permute-start(bf16[4,2,2,4,8,128]{5,4,3,2,1,0:T(8,128)(2,1)S(1)} %get-tuple-element.35), channel_id=1, source_target_pairs={{0,64},{8,72},{16,80},{24,88},{32,96},{40,104},{48,112},{56,120},{... | collective-permute-start | bytes 393224 | tf_op jit(solution)/shard_map/ppermute | solution.py:81
  82.2 61.2 %all-to-all-start.1 = ((bf16[256,8,512]{2,1,0:T(8,128)(2,1)}), bf16[256,8,512]{2,1,0:T(8,128)(2,1)}, u32[]{:S(2)}, u32[]{:S(2)}) async-start(bf16[256,8,512]{2,1,0:T(8,128)(2,1)} %bitcast.96), calls=%async_computation.1 | async-start | bytes 4194304 | tf_op jit(solution)/shard_map/all_to_all | solution.py:468
  91.4 1.6 %collective-permute-start.7 = (bf16[4,4,2,4,8,128]{5,4,3,2,1,0:T(8,128)(2,1)S(1)}, bf16[4,4,2,4,8,128]{5,4,3,2,1,0:T(8,128)(2,1)S(1)}, u32[]{:S(2)}, u32[]{:S(2)}) collective-permute-start(bf16[4,4,2,4,8,128]{5,4,3,2,1,0:T(8,128)(2,1)S(1)} %bitcast.104), channel_id=1, source_target_pairs={{0,8},{8,0},{16,24},{24,16},{32,40},{40,32},{48,56},{56,48},{64,72... | collective-permute-start | bytes 786440 | tf_op jit(solution)/shard_map/ppermute | solution.py:81
  93.0 9.5 %collective-permute-start.8 = (bf16[2,4,2,4,8,128]{5,4,3,0,2,1:T(8,128)(2,1)S(1)}, bf16[2,4,2,4,8,128]{5,4,3,0,2,1:T(8,128)(2,1)S(1)}, u32[]{:S(2)}, u32[]{:S(2)}) collective-permute-start(bf16[2,4,2,4,8,128]{5,4,3,0,2,1:T(8,128)(2,1)S(1)} %get-tuple-element.27), channel_id=1, source_target_pairs={{0,16},{8,24},{16,32},{24,40},{32,48},{40,56},{48,0},{56,8},{64,80... | collective-permute-start | bytes 393224 | tf_op jit(solution)/shard_map/ppermute | solution.py:81
  94.6 8.1 %collective-permute-start.10 = (bf16[2,4,2,4,8,128]{5,4,3,0,2,1:T(8,128)(2,1)S(1)}, bf16[2,4,2,4,8,128]{5,4,3,0,2,1:T(8,128)(2,1)S(1)}, u32[]{:S(2)}, u32[]{:S(2)}) collective-permute-start(bf16[2,4,2,4,8,128]{5,4,3,0,2,1:T(8,128)(2,1)S(1)} %get-tuple-element.28), channel_id=1, source_target_pairs={{0,48},{8,56},{16,0},{24,8},{32,16},{40,24},{48,32},{56,40},{64,11... | collective-permute-start | bytes 393224 | tf_op jit(solution)/shard_map/ppermute | solution.py:81
  96.4 10.9 %collective-permute-start.9 = (bf16[2,4,2,4,8,128]{5,4,3,0,2,1:T(8,128)(2,1)S(1)}, bf16[2,4,2,4,8,128]{5,4,3,0,2,1:T(8,128)(2,1)S(1)}, u32[]{:S(2)}, u32[]{:S(2)}) collective-permute-start(bf16[2,4,2,4,8,128]{5,4,3,0,2,1:T(8,128)(2,1)S(1)} %get-tuple-element.29), channel_id=1, source_target_pairs={{0,32},{8,40},{16,48},{24,56},{32,0},{40,8},{48,16},{56,24},{64,96... | collective-permute-start | bytes 393224 | tf_op jit(solution)/shard_map/ppermute | solution.py:81
  107.3 36.0 %copy-start.1 = (bf16[16,2,8,8,512]{4,3,2,1,0:T(8,128)(2,1)S(1)}, bf16[16,2,8,8,512]{4,3,2,1,0:T(8,128)(2,1)}, u32[]{:S(2)}) copy-start(bf16[16,2,8,8,512]{4,3,2,1,0:T(8,128)(2,1)} %get-tuple-element.13.y_ref) | copy-start | bytes 6291460
  107.3 36.0 %copy-start.2 = (f32[64,1024]{1,0:T(8,128)S(1)}, f32[64,1024]{1,0:T(8,128)}, u32[]{:S(2)}) copy-start(f32[64,1024]{1,0:T(8,128)} %constant.39.clone.a_hbm.a_ref) | copy-start | bytes 786436
  107.3 36.0 %copy-start.3 = (f32[24,1024]{1,0:T(8,128)S(1)}, f32[24,1024]{1,0:T(8,128)}, u32[]{:S(2)}) copy-start(f32[24,1024]{1,0:T(8,128)} %constant.41.clone.s_hbm.s_ref) | copy-start | bytes 294916
  107.3 36.0 %copy-start.4 = (f32[24,1024]{1,0:T(8,128)S(1)}, f32[24,1024]{1,0:T(8,128)}, u32[]{:S(2)}) copy-start(f32[24,1024]{1,0:T(8,128)} %constant.40.clone.c_hbm.c_ref) | copy-start | bytes 294916
  107.4 11.7 %collective-permute-start.13 = (bf16[4,2,2,4,8,128]{5,4,3,1,0,2:T(8,128)(2,1)S(1)}, bf16[4,2,2,4,8,128]{5,4,3,1,0,2:T(8,128)(2,1)S(1)}, u32[]{:S(2)}, u32[]{:S(2)}) collective-permute-start(bf16[4,2,2,4,8,128]{5,4,3,1,0,2:T(8,128)(2,1)S(1)} %get-tuple-element.23), channel_id=1, source_target_pairs={{0,192},{8,200},{16,208},{24,216},{32,224},{40,232},{48,240},{56,2... | collective-permute-start | bytes 393224 | tf_op jit(solution)/shard_map/ppermute | solution.py:81
  110.4 9.7 %collective-permute-start.12 = (bf16[4,2,2,4,8,128]{5,4,3,1,0,2:T(8,128)(2,1)S(1)}, bf16[4,2,2,4,8,128]{5,4,3,1,0,2:T(8,128)(2,1)S(1)}, u32[]{:S(2)}, u32[]{:S(2)}) collective-permute-start(bf16[4,2,2,4,8,128]{5,4,3,1,0,2:T(8,128)(2,1)S(1)} %get-tuple-element.24), channel_id=1, source_target_pairs={{0,128},{8,136},{16,144},{24,152},{32,160},{40,168},{48,176},{56,1... | collective-permute-start | bytes 393224 | tf_op jit(solution)/shard_map/ppermute | solution.py:81
  111.1 12.4 %collective-permute-start.11 = (bf16[4,2,2,4,8,128]{5,4,3,1,0,2:T(8,128)(2,1)S(1)}, bf16[4,2,2,4,8,128]{5,4,3,1,0,2:T(8,128)(2,1)S(1)}, u32[]{:S(2)}, u32[]{:S(2)}) collective-permute-start(bf16[4,2,2,4,8,128]{5,4,3,1,0,2:T(8,128)(2,1)S(1)} %get-tuple-element.25), channel_id=1, source_target_pairs={{0,64},{8,72},{16,80},{24,88},{32,96},{40,104},{48,112},{56,120},{... | collective-permute-start | bytes 393224 | tf_op jit(solution)/shard_map/ppermute | solution.py:81
  124.3 25.3 %collective-permute-start.15 = (bf16[32,4,8,128]{3,2,1,0:T(8,128)(2,1)}, bf16[32,4,8,128]{3,2,1,0:T(8,128)(2,1)S(1)}, u32[]{:S(2)}, u32[]{:S(2)}) collective-permute-start(bf16[32,4,8,128]{3,2,1,0:T(8,128)(2,1)} %get-tuple-element.20), channel_id=1, source_target_pairs={{0,6},{1,7},{2,0},{3,1},{4,2},{5,3},{6,4},{7,5},{8,14},{9,15},{10,... | collective-permute-start | bytes 786440 | tf_op jit(solution)/shard_map/ppermute | solution.py:471
  126.8 22.8 %collective-permute-start.14 = (bf16[32,4,8,128]{3,2,1,0:T(8,128)(2,1)S(1)}, bf16[32,4,8,128]{3,2,1,0:T(8,128)(2,1)S(1)}, u32[]{:S(2)}, u32[]{:S(2)}) collective-permute-start(bf16[32,4,8,128]{3,2,1,0:T(8,128)(2,1)S(1)} %get-tuple-element.21), channel_id=1, source_target_pairs={{0,2},{1,3},{2,4},{3,5},{4,6},{5,7},{6,0},{7,1},{8,10},{9,11},{10,... | collective-permute-start | bytes 786440 | tf_op jit(solution)/shard_map/ppermute | solution.py:470
